TPU v7x, 32 devices: a whole 2x2x4 slice. The times are simulated.
32 devices in a mesh: ctx: 16 (over z, x, core), fsdp: 2 (over y).
Axes of the slice: x: 2, y: 2, z: 4, core: 2. Of those that a mesh axis runs over, the one named last changes fastest.
Arguments:
- tokens: bfloat16 [2, 2048, 2048], P('fsdp', 'ctx'), may hold values from -6 to 6
- cotangent: bfloat16 [2, 2048, 2048], P('fsdp', 'ctx'), may hold values from -6 to 6
- attn_gain: bfloat16 [2048], P('fsdp'), may hold values from 0.25 to 1.75
- w_query: bfloat16 [2048, 2048], P('fsdp'), may hold values from -0.125 to 0.125
- w_key: bfloat16 [2048, 2048], P('fsdp'), may hold values from -0.125 to 0.125
- w_value: bfloat16 [2048, 2048], P('fsdp'), may hold values from -0.125 to 0.125
- w_out: bfloat16 [2048, 2048], P('fsdp'), may hold values from -6 to 6
- query_gain: bfloat16 [2048], P('fsdp'), may hold values from 0.25 to 1.75
- key_gain: bfloat16 [2048], P('fsdp'), may hold values from 0.25 to 1.75
- ffn_gain: bfloat16 [2048], P('fsdp'), may hold values from 0.25 to 1.75
- router: bfloat16 [2048, 16], P('fsdp'), may hold values from -0.5 to 0.5
- w_gate: bfloat16 [16, 2048, 1024], P('ctx', 'fsdp'), may hold values from -0.125 to 0.125
- w_up: bfloat16 [16, 2048, 1024], P('ctx', 'fsdp'), may hold values from -0.125 to 0.125
- w_down: bfloat16 [16, 1024, 2048], P('ctx', None, 'fsdp'), may hold values from -3 to 3
- routes: int32 [2, 2048, 8], P('fsdp', 'ctx'), may hold values from 0 to 15, all different within a row; in each aligned block of 128 rows (0 to 127, 128 to 255, ..., all dimensions but the last counted through in order) at most 128 rows name the same one
- priority: int32 [2, 2048, 8], P('fsdp', 'ctx'), may hold values from 0 to 3
- positions: int32 [2, 2048], P('fsdp', 'ctx'), may hold values from 0 to 2047
Outputs:
- layer_out: bfloat16 [2, 2048, 2048], P('fsdp', 'ctx')
- input_grad: bfloat16 [2, 2048, 2048], P('fsdp', 'ctx')
- attn_gain_grad: float32 [2048], P(('ctx', 'fsdp'))
- w_query_grad: float32 [2048, 2048], P(('ctx', 'fsdp'))
- w_key_grad: float32 [2048, 2048], P(('ctx', 'fsdp'))
- w_value_grad: float32 [2048, 2048], P(('ctx', 'fsdp'))
- w_out_grad: float32 [2048, 2048], P(('ctx', 'fsdp'))
- query_gain_grad: float32 [2048], P(('ctx', 'fsdp'))
- key_gain_grad: float32 [2048], P(('ctx', 'fsdp'))
- ffn_gain_grad: float32 [2048], P(('ctx', 'fsdp'))
- router_grad: float32 [2048, 16], P(('ctx', 'fsdp'))
- w_gate_grad: float32 [16, 2048, 1024], P('ctx', 'fsdp')
- w_up_grad: float32 [16, 2048, 1024], P('ctx', 'fsdp')
- w_down_grad: float32 [16, 1024, 2048], P('ctx', None, 'fsdp')
Inputs may be any that keep to these rules, and one draw needn't show every extreme that they name: `routes`: each row names 8 different experts. In every aligned block of 128 rows (the rows of one device) no expert is named by more than 128 rows, and in some block an expert is named by exactly 128 rows.
All inputs are finite; a program needn't handle non-finite values.
Results may differ from a plain program's by a relative error of at most 0.02.
Values may be sent and summed in bfloat16 or wider, within the bound.
No kernel may reach another device: no remote copies, remote signals or barrier semaphores. Data moves between devices by JAX's collectives and lax.ppermute only.
A program may use at most 704 MiB of HBM per device.

v0:
```python
import math

import jax
import jax.numpy as jnp
from jax import lax
from jax.sharding import PartitionSpec as P

HEAD_DIM = 128
LEVELS = 4


epsilon = 1e-05
rope_base = 50000.0


def prefix(part, axis, combine, identity):
    place = lax.axis_index(axis)
    gathered = lax.all_gather(part, axis)
    state = jnp.zeros_like(part) + jnp.asarray(identity, part.dtype)

    def one(turn, state):
        return combine(state, lax.dynamic_index_in_dim(gathered, turn, 0, False))

    return lax.fori_loop(0, place, one, state)


def product(left, right):
    return jnp.dot(left, right, preferred_element_type=jnp.float32)


def precise(left, right):
    return jnp.dot(left, right, precision=lax.Precision.HIGHEST, preferred_element_type=jnp.float32)


def contract_rows(left, right):
    return lax.dot_general(
        left, right, (((0,), (0,)), ((), ())), preferred_element_type=jnp.float32
    )


def contract_cols(left, right):
    return lax.dot_general(
        left, right, (((1,), (1,)), ((), ())), preferred_element_type=jnp.float32
    )


def rms_forward(matrix, gain_row):
    inverse = lax.rsqrt(jnp.mean(matrix * matrix, axis=-1, keepdims=True) + epsilon)
    return (matrix * inverse * gain_row, inverse)


def rms_backward(matrix, inverse, gain_row, upstream):
    scaled = upstream * gain_row
    along = jnp.mean(scaled * matrix, axis=-1, keepdims=True)
    grad_rows = inverse * scaled - matrix * inverse * inverse * inverse * along
    grad_gain = jnp.sum(upstream * matrix * inverse, axis=0)
    return (grad_rows, grad_gain)


def rope_tables(position_ids, head_dim):
    half_dim = head_dim // 2
    inverse = rope_base ** (-(jnp.arange(half_dim, dtype=jnp.float32) * 2.0) / head_dim)
    angles = position_ids.astype(jnp.float32)[:, None] * inverse[None, :]
    return (jnp.cos(angles)[:, None, :], jnp.sin(angles)[:, None, :])


def rotate(matrix, cosine, sine_part, head_dim, turn_sign):
    count_rows = matrix.shape[0]
    by_head = matrix.reshape(count_rows, -1, head_dim)
    half_dim = head_dim // 2
    lower_half = by_head[..., :half_dim]
    upper_half = by_head[..., half_dim:]
    turned = jnp.concatenate(
        [
            lower_half * cosine - turn_sign * upper_half * sine_part,
            upper_half * cosine + turn_sign * lower_half * sine_part,
        ],
        axis=-1,
    )
    return turned.reshape(count_rows, -1)


def add_counts(earlier_part, later_part):
    return earlier_part + later_part


def score_block(query_part, key_part, score_scale):
    return (
        jnp.einsum("qhd,khd->hqk", query_part, key_part, preferred_element_type=jnp.float32)
        * score_scale
    )


def grad_block(query_part, dout_part, lse_part, delta_part, key_part, value_part, score_scale):
    probs = jnp.exp(score_block(query_part, key_part, score_scale) - lse_part)
    prob_low = probs.astype(jnp.bfloat16)
    dprob = jnp.einsum("qhd,khd->hqk", dout_part, value_part, preferred_element_type=jnp.float32)
    dscore = (probs * (dprob - delta_part)).astype(jnp.bfloat16)
    return (prob_low, dscore)


def body(
    tokens,
    cotangent,
    attn_gain,
    w_query,
    w_key,
    w_value,
    w_out,
    query_gain,
    key_gain,
    ffn_gain,
    router,
    w_gate,
    w_up,
    w_down,
    routes,
    priority,
    positions,
):
    ctx_count = lax.axis_size("ctx")
    (
        g_attn,
        q_weight,
        k_weight,
        v_weight,
        o_weight,
        g_query,
        g_key,
        g_ffn,
        r_weight,
        gate_full,
        up_full,
        down_full,
    ) = (
        lax.all_gather(attn_gain, "fsdp", axis=0, tiled=True),
        lax.all_gather(w_query, "fsdp", axis=0, tiled=True),
        lax.all_gather(w_key, "fsdp", axis=0, tiled=True),
        lax.all_gather(w_value, "fsdp", axis=0, tiled=True),
        lax.all_gather(w_out, "fsdp", axis=0, tiled=True),
        lax.all_gather(query_gain, "fsdp", axis=0, tiled=True),
        lax.all_gather(key_gain, "fsdp", axis=0, tiled=True),
        lax.all_gather(ffn_gain, "fsdp", axis=0, tiled=True),
        lax.all_gather(router, "fsdp", axis=0, tiled=True),
        lax.all_gather(w_gate, "fsdp", axis=1, tiled=True),
        lax.all_gather(w_up, "fsdp", axis=1, tiled=True),
        lax.all_gather(w_down, "fsdp", axis=2, tiled=True),
    )
    gate_weight = gate_full[0]
    up_weight = up_full[0]
    down_weight = down_full[0]
    tok_rows = tokens.shape[1]
    model_width = tokens.shape[2]
    head_dim = HEAD_DIM
    head_count = model_width // head_dim
    length = tok_rows * ctx_count
    top_k = routes.shape[2]
    capacity = 9 * tok_rows
    send_rows = 2 * tok_rows * top_k // ctx_count
    key_block = math.gcd(length, 1024)
    block_count = length // key_block
    score_scale = head_dim ** (-0.5)
    inputs = tokens[0].astype(jnp.float32)
    normed, inv_one = rms_forward(inputs, g_attn)
    h_one = normed.astype(jnp.bfloat16)
    q_lin = product(h_one, q_weight)
    k_lin = product(h_one, k_weight)
    v_lin = product(h_one, v_weight)
    cosine, sine_part = rope_tables(positions[0], head_dim)
    q_normed, inv_query = rms_forward(q_lin, g_query)
    k_normed, inv_key = rms_forward(k_lin, g_key)
    q_rot = rotate(q_normed, cosine, sine_part, head_dim, 1.0).astype(jnp.bfloat16)
    k_rot = rotate(k_normed, cosine, sine_part, head_dim, 1.0).astype(jnp.bfloat16)
    v_low = v_lin.astype(jnp.bfloat16)
    all_keys, all_values = (
        lax.all_gather(k_rot, "ctx", axis=0, tiled=True),
        lax.all_gather(v_low, "ctx", axis=0, tiled=True),
    )
    q_heads = q_rot.reshape(tok_rows, head_count, head_dim)

    def key_slice(block_id):
        start = block_id * key_block
        key_part = lax.dynamic_slice_in_dim(all_keys, start, key_block, 0).reshape(
            key_block, head_count, head_dim
        )
        value_part = lax.dynamic_slice_in_dim(all_values, start, key_block, 0).reshape(
            key_block, head_count, head_dim
        )
        return (key_part, value_part)

    def lse_step(carry, block_id):
        run_max, run_total = carry
        key_part, value_part = key_slice(block_id)
        scores = score_block(q_heads, key_part, score_scale)
        new_max = jnp.maximum(run_max, jnp.max(scores, axis=-1, keepdims=True))
        run_total = run_total * jnp.exp(run_max - new_max) + jnp.sum(
            jnp.exp(scores - new_max), axis=-1, keepdims=True
        )
        return ((new_max, run_total), None)

    start_max = jnp.full((head_count, tok_rows, 1), -jnp.inf, jnp.float32)
    start_total = jnp.zeros((head_count, tok_rows, 1), jnp.float32)
    (run_max, run_total), _ = lax.scan(lse_step, (start_max, start_total), jnp.arange(block_count))
    lse = run_max + jnp.log(run_total)

    def out_step(acc, block_id):
        key_part, value_part = key_slice(block_id)
        probs = jnp.exp(score_block(q_heads, key_part, score_scale) - lse).astype(jnp.bfloat16)
        return (
            acc + jnp.einsum("hqk,khd->qhd", probs, value_part, preferred_element_type=jnp.float32),
            None,
        )

    attended_heads, _ = lax.scan(
        out_step, jnp.zeros((tok_rows, head_count, head_dim), jnp.float32), jnp.arange(block_count)
    )
    attended = attended_heads.reshape(tok_rows, model_width)
    mixed_low = attended.astype(jnp.bfloat16)
    middle = inputs + product(mixed_low, o_weight)
    h_two_f, inv_two = rms_forward(middle, g_ffn)
    h_two = h_two_f.astype(jnp.bfloat16)
    logits = product(h_two, r_weight)
    row_max = jnp.max(logits, axis=-1, keepdims=True)
    exps_raw = jnp.exp(logits - row_max)
    router_probs = exps_raw / jnp.sum(exps_raw, axis=-1, keepdims=True)
    route_ids = routes[0]
    level_ids = priority[0]
    pair_code = level_ids * ctx_count + route_ids
    code_table = (
        pair_code[:, :, None] == jnp.arange(LEVELS * ctx_count, dtype=jnp.int32)[None, None, :]
    ).astype(jnp.float32)
    per_token = jnp.sum(code_table, axis=1)
    before_local = jnp.cumsum(per_token, axis=0) - per_token
    local_total = jnp.sum(per_token, axis=0)
    earlier = prefix(local_total, "ctx", add_counts, jnp.zeros_like(local_total))
    totals = lax.psum(local_total, "ctx")
    level_totals = totals.reshape(LEVELS, ctx_count)
    level_base = (jnp.cumsum(level_totals, axis=0) - level_totals).reshape(-1)
    offsets = before_local + (earlier + level_base)[None, :]
    pair_rank = jnp.sum(code_table * offsets[:, None, :], axis=-1).astype(jnp.int32)
    is_kept = pair_rank < capacity
    expert_hot = (
        route_ids[:, :, None] == jnp.arange(ctx_count, dtype=jnp.int32)[None, None, :]
    ).astype(jnp.float32)
    per_expert = jnp.sum(expert_hot, axis=1)
    local_before = jnp.cumsum(per_expert, axis=0) - per_expert
    local_slot = jnp.sum(expert_hot * local_before[:, None, :], axis=-1).astype(jnp.int32)
    send_index = (route_ids * send_rows + local_slot).reshape(-1)
    pair_count = tok_rows * top_k
    pair_of_slot = (
        jnp.full((ctx_count * send_rows,), pair_count, jnp.int32)
        .at[send_index]
        .set(jnp.arange(pair_count, dtype=jnp.int32))
    )
    slot_target = jnp.where(is_kept, pair_rank, capacity).reshape(-1)
    target_pad = jnp.concatenate([slot_target, jnp.full((1,), capacity, jnp.int32)], axis=0)
    send_slots = target_pad[pair_of_slot].reshape(ctx_count, send_rows)
    h_pad = jnp.concatenate([h_two, jnp.zeros((1, model_width), jnp.bfloat16)], axis=0)
    send_tokens = h_pad[pair_of_slot // top_k].reshape(ctx_count, send_rows, model_width)
    got_tokens, got_slots = (
        lax.all_to_all(send_tokens, "ctx", split_axis=0, concat_axis=0, tiled=True),
        lax.all_to_all(send_slots, "ctx", split_axis=0, concat_axis=0, tiled=True),
    )
    received_count = ctx_count * send_rows
    slots_flat = got_slots.reshape(-1)
    row_of_slot = (
        jnp.full((capacity,), received_count, jnp.int32)
        .at[slots_flat]
        .set(jnp.arange(received_count, dtype=jnp.int32), mode="drop")
    )
    got_pad = jnp.concatenate(
        [
            got_tokens.reshape(received_count, model_width),
            jnp.zeros((1, model_width), jnp.bfloat16),
        ],
        axis=0,
    )
    expert_in = got_pad[row_of_slot]
    gate_lin = product(expert_in, gate_weight)
    up_lin = product(expert_in, up_weight)
    sig_gate = jax.nn.sigmoid(gate_lin)
    silu_val = gate_lin * sig_gate
    swiglu = (silu_val * up_lin).astype(jnp.bfloat16)
    expert_out = product(swiglu, down_weight).astype(jnp.bfloat16)
    out_pad = jnp.concatenate([expert_out, jnp.zeros((1, model_width), jnp.bfloat16)], axis=0)
    back_rows = out_pad[slots_flat].reshape(ctx_count, send_rows, model_width)
    returned = lax.all_to_all(back_rows, "ctx", split_axis=0, concat_axis=0, tiled=True)
    returned_pad = jnp.concatenate(
        [
            returned.reshape(ctx_count * send_rows, model_width),
            jnp.zeros((1, model_width), jnp.bfloat16),
        ],
        axis=0,
    )
    pair_out = returned_pad[send_index].reshape(tok_rows, top_k, model_width)
    chosen = jnp.sum(router_probs[:, None, :] * expert_hot, axis=-1)
    share = jnp.where(is_kept, chosen, 0.0)
    mixture = jnp.einsum("tk,tkd->td", share, pair_out, preferred_element_type=jnp.float32)
    final_rows = middle + mixture
    layer_out = final_rows.astype(jnp.bfloat16)
    grad_out = cotangent[0].astype(jnp.float32)
    routed_grad = (share[:, :, None] * grad_out[:, None, :]).astype(jnp.bfloat16)
    share_grad = jnp.where(
        is_kept,
        jnp.einsum("tkd,td->tk", pair_out, grad_out, preferred_element_type=jnp.float32),
        0.0,
    )
    prob_grad = jnp.sum(expert_hot * share_grad[:, :, None], axis=1)
    logit_grad = router_probs * (
        prob_grad - jnp.sum(router_probs * prob_grad, axis=-1, keepdims=True)
    )
    routed_pad = jnp.concatenate(
        [routed_grad.reshape(pair_count, model_width), jnp.zeros((1, model_width), jnp.bfloat16)],
        axis=0,
    )
    send_grads = routed_pad[pair_of_slot].reshape(ctx_count, send_rows, model_width)
    got_grads = lax.all_to_all(send_grads, "ctx", split_axis=0, concat_axis=0, tiled=True)
    grad_pad = jnp.concatenate(
        [got_grads.reshape(received_count, model_width), jnp.zeros((1, model_width), jnp.bfloat16)],
        axis=0,
    )
    out_grad = grad_pad[row_of_slot]
    act_grad = contract_cols(out_grad, down_weight)
    down_wgrad = contract_rows(swiglu, out_grad)
    gate_grad = (act_grad * up_lin * sig_gate * (1.0 + gate_lin * (1.0 - sig_gate))).astype(
        jnp.bfloat16
    )
    up_grad = (act_grad * silu_val).astype(jnp.bfloat16)
    in_grad = (contract_cols(gate_grad, gate_weight) + contract_cols(up_grad, up_weight)).astype(
        jnp.bfloat16
    )
    gate_wgrad = contract_rows(expert_in, gate_grad)
    up_wgrad = contract_rows(expert_in, up_grad)
    in_pad = jnp.concatenate([in_grad, jnp.zeros((1, model_width), jnp.bfloat16)], axis=0)
    back_grads = in_pad[slots_flat].reshape(ctx_count, send_rows, model_width)
    pair_grads = lax.all_to_all(back_grads, "ctx", split_axis=0, concat_axis=0, tiled=True)
    pair_pad = jnp.concatenate(
        [
            pair_grads.reshape(ctx_count * send_rows, model_width),
            jnp.zeros((1, model_width), jnp.bfloat16),
        ],
        axis=0,
    )
    token_pair = pair_pad[send_index].reshape(tok_rows, top_k, model_width)
    hidden_grad = jnp.sum(token_pair.astype(jnp.float32), axis=1) + precise(
        logit_grad, r_weight.astype(jnp.float32).T
    )
    router_wgrad = precise(h_two.astype(jnp.float32).T, logit_grad)
    norm_grad, ffn_gain_grad = rms_backward(middle, inv_two, g_ffn, hidden_grad)
    middle_grad = grad_out + norm_grad
    branch_grad = middle_grad.astype(jnp.bfloat16)
    out_wgrad = contract_rows(mixed_low, branch_grad)
    mixed_grad = contract_cols(branch_grad, o_weight).astype(jnp.bfloat16)
    dout_heads = mixed_grad.reshape(tok_rows, head_count, head_dim)
    delta = jnp.sum(dout_heads.astype(jnp.float32) * attended_heads, axis=-1).T[:, :, None]

    def back_step(dq_acc, block_id):
        key_part, value_part = key_slice(block_id)
        prob_low, dscore = grad_block(
            q_heads, dout_heads, lse, delta, key_part, value_part, score_scale
        )
        dq_acc = dq_acc + jnp.einsum(
            "hqk,khd->qhd", dscore, key_part, preferred_element_type=jnp.float32
        )
        dk_part = jnp.einsum(
            "hqk,qhd->khd", dscore, q_heads, preferred_element_type=jnp.float32
        ).reshape(key_block, model_width)
        dv_part = jnp.einsum(
            "hqk,qhd->khd", prob_low, dout_heads, preferred_element_type=jnp.float32
        ).reshape(key_block, model_width)
        return (dq_acc, jnp.concatenate([dk_part, dv_part], axis=1))

    dq_heads, kv_terms = lax.scan(
        back_step, jnp.zeros((tok_rows, head_count, head_dim), jnp.float32), jnp.arange(block_count)
    )
    kv_mine = lax.psum_scatter(
        kv_terms.reshape(length, 2 * model_width), "ctx", scatter_dimension=0, tiled=True
    )
    key_grad = kv_mine[:, :model_width] * score_scale
    value_grad = kv_mine[:, model_width:]
    v_lin_low = value_grad.astype(jnp.bfloat16)
    q_grad = dq_heads.reshape(tok_rows, model_width) * score_scale
    q_back = rotate(q_grad, cosine, sine_part, head_dim, -1.0)
    k_back = rotate(key_grad, cosine, sine_part, head_dim, -1.0)
    q_lin_grad, query_gain_grad = rms_backward(q_lin, inv_query, g_query, q_back)
    k_lin_grad, key_gain_grad = rms_backward(k_lin, inv_key, g_key, k_back)
    q_lin_low = q_lin_grad.astype(jnp.bfloat16)
    k_lin_low = k_lin_grad.astype(jnp.bfloat16)
    h_grad = (
        contract_cols(q_lin_low, q_weight)
        + contract_cols(k_lin_low, k_weight)
        + contract_cols(v_lin_low, v_weight)
    )
    query_wgrad = contract_rows(h_one, q_lin_low)
    key_wgrad = contract_rows(h_one, k_lin_low)
    value_wgrad = contract_rows(h_one, v_lin_low)
    in_norm_grad, attn_gain_grad = rms_backward(inputs, inv_one, g_attn, h_grad)
    input_grad = (middle_grad + in_norm_grad).astype(jnp.bfloat16)
    s_gate, s_up, s_down = (
        lax.psum_scatter(
            gate_wgrad[None].astype(jnp.bfloat16), "fsdp", scatter_dimension=1, tiled=True
        ).astype(jnp.float32),
        lax.psum_scatter(
            up_wgrad[None].astype(jnp.bfloat16), "fsdp", scatter_dimension=1, tiled=True
        ).astype(jnp.float32),
        lax.psum_scatter(
            down_wgrad[None].astype(jnp.bfloat16), "fsdp", scatter_dimension=2, tiled=True
        ).astype(jnp.float32),
    )
    d_attn, d_query, d_key, d_value, d_out, d_qgain, d_kgain, d_ffn, d_router = (
        lax.psum_scatter(attn_gain_grad, ("ctx", "fsdp"), scatter_dimension=0, tiled=True),
        lax.psum_scatter(query_wgrad, ("ctx", "fsdp"), scatter_dimension=0, tiled=True),
        lax.psum_scatter(key_wgrad, ("ctx", "fsdp"), scatter_dimension=0, tiled=True),
        lax.psum_scatter(value_wgrad, ("ctx", "fsdp"), scatter_dimension=0, tiled=True),
        lax.psum_scatter(out_wgrad, ("ctx", "fsdp"), scatter_dimension=0, tiled=True),
        lax.psum_scatter(query_gain_grad, ("ctx", "fsdp"), scatter_dimension=0, tiled=True),
        lax.psum_scatter(key_gain_grad, ("ctx", "fsdp"), scatter_dimension=0, tiled=True),
        lax.psum_scatter(ffn_gain_grad, ("ctx", "fsdp"), scatter_dimension=0, tiled=True),
        lax.psum_scatter(router_wgrad, ("ctx", "fsdp"), scatter_dimension=0, tiled=True),
    )
    return (
        layer_out[None],
        input_grad[None],
        d_attn,
        d_query,
        d_key,
        d_value,
        d_out,
        d_qgain,
        d_kgain,
        d_ffn,
        d_router,
        s_gate,
        s_up,
        s_down,
    )


def solution(mesh):
    return jax.shard_map(
        body,
        mesh=mesh,
        in_specs=(
            P("fsdp", "ctx", None),
            P("fsdp", "ctx", None),
            P("fsdp"),
            P("fsdp", None),
            P("fsdp", None),
            P("fsdp", None),
            P("fsdp", None),
            P("fsdp"),
            P("fsdp"),
            P("fsdp"),
            P("fsdp", None),
            P("ctx", "fsdp", None),
            P("ctx", "fsdp", None),
            P("ctx", None, "fsdp"),
            P("fsdp", "ctx", None),
            P("fsdp", "ctx", None),
            P("fsdp", "ctx"),
        ),
        out_specs=(
            P("fsdp", "ctx", None),
            P("fsdp", "ctx", None),
            P(("ctx", "fsdp")),
            P(("ctx", "fsdp"), None),
            P(("ctx", "fsdp"), None),
            P(("ctx", "fsdp"), None),
            P(("ctx", "fsdp"), None),
            P(("ctx", "fsdp")),
            P(("ctx", "fsdp")),
            P(("ctx", "fsdp")),
            P(("ctx", "fsdp"), None),
            P("ctx", "fsdp", None),
            P("ctx", "fsdp", None),
            P("ctx", None, "fsdp"),
        ),
        check_vma=False,
    )
```

profile of v0, /device:TPU:8, one launch (start us, length us, event | category | flops | bytes accessed | tf_op | source)
XLA Modules:
  0.0 3797.2 jit_solution(11930502551229456318)
XLA Ops:
  14.1 100.7 %all-gather.11.cloned.1.call-done = bf16[2048,2048]{1,0:T(8,128)(2,1)} async-done(((bf16[1024,2048]{1,0:T(8,128)(2,1)}), bf16[2048,2048]{1,0:T(8,128)(2,1)}) %all-gather.11.cloned.1.call-update) | async-done | bytes 8388624 | tf_op jit(solution)/shard_map/all_gather | solution.py:139
  129.9 90.5 %all-gather.15.cloned.1.call-done = bf16[2048,2048]{1,0:T(8,128)(2,1)} async-done(((bf16[1024,2048]{1,0:T(8,128)(2,1)}), bf16[2048,2048]{1,0:T(8,128)(2,1)}) %all-gather.15.cloned.1.call-update) | async-done | bytes 8388624 | tf_op jit(solution)/shard_map/all_gather | solution.py:138
  226.6 99.3 %all-gather.19.cloned.1.call-done = bf16[2048,2048]{1,0:T(8,128)(2,1)} async-done(((bf16[1024,2048]{1,0:T(8,128)(2,1)}), bf16[2048,2048]{1,0:T(8,128)(2,1)}) %all-gather.19.cloned.1.call-update) | async-done | bytes 8388624 | tf_op jit(solution)/shard_map/all_gather | solution.py:137
  337.9 26.4 all-reduce.14
  371.8 20.6 gather_fusion.1
  422.0 59.2 %all-gather.17.cloned.1.call-done = bf16[2048,2048]{0,1:T(8,128)(2,1)} async-done(((bf16[128,2048]{0,1:T(8,128)(2,1)}), bf16[2048,2048]{0,1:T(8,128)(2,1)}) %all-gather.17.cloned.1.call-update) | async-done | bytes 8388624 | tf_op jit(solution)/shard_map/all_gather | solution.py:176
  495.9 32.7 while.49
  528.8 57.9 %all-gather.21.cloned.1.call-done = bf16[2048,2048]{1,0:T(8,128)(2,1)} async-done(((bf16[1024,2048]{1,0:T(8,128)(2,1)}), bf16[2048,2048]{1,0:T(8,128)(2,1)}) %all-gather.21.cloned.1.call-update) | async-done | bytes 8388624 | tf_op jit(solution)/shard_map/all_gather | solution.py:140
  620.0 170.3 %all-to-all-done = bf16[16,128,2048]{2,1,0:T(8,128)(2,1)} async-done(((bf16[16,128,2048]{2,1,0:T(8,128)(2,1)}), bf16[16,128,2048]{2,1,0:T(8,128)(2,1)}, u32[]{:S(2)}, u32[]{:S(2)}) %all-to-all-start) | async-done | bytes 8388640 | tf_op jit(solution)/shard_map/all_to_all | solution.py:261
  844.9 19.3 gather_fusion.3
  876.4 175.3 %all-to-all-done.2 = bf16[16,128,2048]{2,1,0:T(8,128)(2,1)} async-done(((bf16[16,128,2048]{2,1,0:T(8,128)(2,1)}), bf16[16,128,2048]{2,1,0:T(8,128)(2,1)}, u32[]{:S(2)}, u32[]{:S(2)}) %all-to-all-start.2) | async-done | bytes 8388640 | tf_op jit(solution)/shard_map/all_to_all | solution.py:287
  1100.8 189.0 %all_to_all.29 = bf16[16,128,2048]{2,1,0:T(8,128)(2,1)} all-to-all(bf16[16,128,2048]{2,1,0:T(8,128)(2,1)} %bitcast.285), channel_id=1, replica_groups=mesh['ctx'=16,'fsdp'=2] {'ctx'}, dimensions={0} | all-to-all | bytes 16777216 | tf_op jit(solution)/shard_map/all_to_all | solution.py:317
  1370.9 177.0 %all-to-all-done.4 = bf16[16,128,2048]{2,1,0:T(8,128)(2,1)} async-done(((bf16[16,128,2048]{2,1,0:T(8,128)(2,1)}), bf16[16,128,2048]{2,1,0:T(8,128)(2,1)}, u32[]{:S(2)}, u32[]{:S(2)}) %all-to-all-start.4) | async-done | bytes 8388640 | tf_op jit(solution)/shard_map/all_to_all | solution.py:336
  1586.2 121.7 %while.50 = (s32[]{:T(128)}, f32[128,16,128]{0,2,1:T(8,128)}, f32[2,1024,4096]{2,1,0:T(8,128)}, s32[2]{0:T(128)S(1)}, bf16[2048,2048]{0,1:T(8,128)(2,1)}, /*inde...) while((s32[]{:T(128)}, f32[128,16,128]{0,2,1:T(8,128)}, ...), condition=%wide.region_32.33_spmd.clone, body=%wide.region_31.32_spmd.clone.sunk | while | flops 2705850368 | bytes 222388544 | solution.py:373
  1755.0 285.0 %reduce-scatter.12.cloned.1.call-done = f32[128,4096]{1,0:T(8,128)} async-done(((f32[2048,4096]{1,0:T(8,128)}), f32[128,4096]{1,0:T(8,128)}) %reduce-scatter.12.cloned.1.call-update) | async-done | bytes 2097168 | tf_op jit(solution)/shard_map/reduce_scatter | solution.py:376
  2086.5 77.6 %reduce-scatter.28.cloned.1.call-done = f32[64,16]{1,0:T(8,128)} async-done(((f32[2048,16]{1,0:T(8,128)}), f32[64,16]{1,0:T(8,128)}) %reduce-scatter.28.cloned.1.call-update) | async-done | bytes 4112
  2165.6 65.1 %reduce-scatter.26.cloned.1.call-done = bf16[1,1024,1024]{2,1,0:T(8,128)(2,1)} async-done(((bf16[1,1024,2048]{2,1,0:T(8,128)(2,1)}), bf16[1,1024,1024]{2,1,0:T(8,128)(2,1)}) %reduce-scatter.26.cloned.1.call-update) | async-done | bytes 2097168 | tf_op jit(solution)/shard_map/reduce_scatter | solution.py:406
  2234.7 53.1 %reduce-scatter.24.cloned.1.call-done = bf16[1,1024,1024]{2,1,0:T(8,128)(2,1)} async-done(((bf16[1,2048,1024]{2,1,0:T(8,128)(2,1)}), bf16[1,1024,1024]{2,1,0:T(8,128)(2,1)}) %reduce-scatter.24.cloned.1.call-update) | async-done | bytes 2097168 | tf_op jit(solution)/shard_map/reduce_scatter | solution.py:403
  2291.9 53.1 %reduce-scatter.22.cloned.1.call-done = bf16[1,1024,1024]{2,1,0:T(8,128)(2,1)} async-done(((bf16[1,2048,1024]{2,1,0:T(8,128)(2,1)}), bf16[1,1024,1024]{2,1,0:T(8,128)(2,1)}) %reduce-scatter.22.cloned.1.call-update) | async-done | bytes 2097168 | tf_op jit(solution)/shard_map/reduce_scatter | solution.py:400
  2365.1 41.7 %all-reduce.13 = (f32[2048]{0:T(1024)S(1)}, f32[2048]{0:T(1024)S(1)}, f32[2048]{0:T(1024)S(1)}, f32[2048]{0:T(1024)S(1)}) all-reduce(f32[2048]{0:T(1024)S(1)} %get-tuple-element.365, f32[2048]{0:T(1024)S(1)} %get-tuple-element.363, f32[2048]{0:T(1024)S(1)} %get-tuple-element.361, ...), channel_id=4, replica_groups=mesh['ctx'=16,'fsdp'=2] {'ctx','fsdp'}, use_global_device_ids=true, to_apply=%region_38.39.clone | all-reduce | flops 8192 | bytes 65536
  2410.3 296.2 %reduce-scatter.20.cloned.1.call-done = f32[64,2048]{1,0:T(8,128)} async-done(((f32[2048,2048]{1,0:T(8,128)}), f32[64,2048]{1,0:T(8,128)}) %reduce-scatter.20.cloned.1.call-update) | async-done | bytes 524304 | tf_op jit(solution)/shard_map/reduce_scatter | solution.py:415
  2706.5 361.2 %reduce-scatter.18.cloned.1.call-done = f32[64,2048]{1,0:T(8,128)} async-done(((f32[2048,2048]{1,0:T(8,128)}), f32[64,2048]{1,0:T(8,128)}) %reduce-scatter.18.cloned.1.call-update) | async-done | bytes 524304 | tf_op jit(solution)/shard_map/reduce_scatter | solution.py:414
  3067.7 361.2 %reduce-scatter.16.cloned.1.call-done = f32[64,2048]{1,0:T(8,128)} async-done(((f32[2048,2048]{1,0:T(8,128)}), f32[64,2048]{1,0:T(8,128)}) %reduce-scatter.16.cloned.1.call-update) | async-done | bytes 524304 | tf_op jit(solution)/shard_map/reduce_scatter | solution.py:413
  3428.9 361.2 %reduce-scatter.14.cloned.1.call-done = f32[64,2048]{1,0:T(8,128)} async-done(((f32[2048,2048]{1,0:T(8,128)}), f32[64,2048]{1,0:T(8,128)}) %reduce-scatter.14.cloned.1.call-update) | async-done | bytes 524304 | tf_op jit(solution)/shard_map/reduce_scatter | solution.py:412
  (423 shorter events, 650.3 us)
Async XLA Ops:
  7.2 107.6 %all-gather.11.cloned.1.call-start = ((), (), s32[]{:S(2)}) async-start(), calls=%async_computation.14 | async-start | bytes 12582912 | tf_op jit(solution)/shard_map/all_gather | solution.py:139
  7.9 212.4 %all-gather.15.cloned.1.call-start = ((), (), s32[]{:S(2)}) async-start(), calls=%async_computation.16 | async-start | bytes 12582912 | tf_op jit(solution)/shard_map/all_gather | solution.py:138
  8.7 317.2 %all-gather.19.cloned.1.call-start = ((), (), s32[]{:S(2)}) async-start(), calls=%async_computation.18 | async-start | bytes 12582912 | tf_op jit(solution)/shard_map/all_gather | solution.py:137
  9.4 400.2 %all-gather.13.cloned.1.call-start = ((), (), s32[]{:S(2)}) async-start(), calls=%async_computation.15 | async-start | bytes 8912896 | tf_op jit(solution)/shard_map/all_gather | solution.py:177
  120.3 360.9 %all-gather.17.cloned.1.call-start = ((), (), s32[]{:S(2)}) async-start(), calls=%async_computation.17 | async-start | bytes 8912896 | tf_op jit(solution)/shard_map/all_gather | solution.py:176
  335.6 251.0 %all-gather.21.cloned.1.call-start = ((), (), s32[]{:S(2)}) async-start(), calls=%async_computation.19 | async-start | bytes 12582912 | tf_op jit(solution)/shard_map/all_gather | solution.py:140
  392.4 211.3 %all-to-all-start.1 = ((s32[16,1,128]{2,1,0:T(1,128)}), s32[16,1,128]{2,1,0:T(1,128)S(1)}, u32[]{:S(2)}, u32[]{:S(2)}) async-start(s32[16,1,128]{2,1,0:T(1,128)} %bitcast.13), calls=%async_computation.1 | async-start | bytes 16384 | tf_op jit(solution)/shard_map/all_to_all | solution.py:262
  603.6 186.8 %all-to-all-start = ((bf16[16,128,2048]{2,1,0:T(8,128)(2,1)}), bf16[16,128,2048]{2,1,0:T(8,128)(2,1)}, u32[]{:S(2)}, u32[]{:S(2)}) async-start(bf16[16,128,2048]{2,1,0:T(8,128)(2,1)} %bitcast.282), calls=%async_computation | async-start | bytes 16777216 | tf_op jit(solution)/shard_map/all_to_all | solution.py:261
  609.7 204.2 %all-gather.23.cloned.1.call-start = ((), (), s32[]{:S(2)}) async-start(), calls=%async_computation.20 | async-start | bytes 6291456 | tf_op jit(solution)/shard_map/all_gather | solution.py:145
  610.4 213.1 %all-gather.25.cloned.1.call-start = ((), (), s32[]{:S(2)}) async-start(), calls=%async_computation.21 | async-start | bytes 6291456 | tf_op jit(solution)/shard_map/all_gather | solution.py:146
  611.2 222.8 %all-gather.27.cloned.1.call-start = ((), (), s32[]{:S(2)}) async-start(), calls=%async_computation.22 | async-start | bytes 6291456 | tf_op jit(solution)/shard_map/all_gather | solution.py:147
  864.2 187.4 %all-to-all-start.2 = ((bf16[16,128,2048]{2,1,0:T(8,128)(2,1)}), bf16[16,128,2048]{2,1,0:T(8,128)(2,1)}, u32[]{:S(2)}, u32[]{:S(2)}) async-start(bf16[16,128,2048]{2,1,0:T(8,128)(2,1)} %bitcast.284), calls=%async_computation.2 | async-start | bytes 16777216 | tf_op jit(solution)/shard_map/all_to_all | solution.py:287
  876.4 698.8 %copy-start.41 = (f32[128,16]{0,1:T(8,128)}, f32[128,16]{0,1:T(8,128)S(1)}, u32[]{:S(2)}) copy-start(f32[128,16]{0,1:T(8,128)S(1)} %fusion.57) | copy-start | bytes 24580
  1078.3 496.9 %copy-start.43 = (f32[128,16]{0,1:T(8,128)}, f32[128,16]{0,1:T(8,128)S(1)}, u32[]{:S(2)}) copy-start(f32[128,16]{0,1:T(8,128)S(1)} %get-tuple-element.367) | copy-start | bytes 24580
  1361.6 186.4 %all-to-all-start.4 = ((bf16[16,128,2048]{2,1,0:T(8,128)(2,1)}), bf16[16,128,2048]{2,1,0:T(8,128)(2,1)}, u32[]{:S(2)}, u32[]{:S(2)}) async-start(bf16[16,128,2048]{2,1,0:T(8,128)(2,1)} %bitcast.283), calls=%async_computation.4 | async-start | bytes 16777216 | tf_op jit(solution)/shard_map/all_to_all | solution.py:336
  1367.3 672.7 %reduce-scatter.12.cloned.1.call-start = ((), (), s32[]{:S(2)}) async-start(), calls=%async_computation.23 | async-start | bytes 35651584 | tf_op jit(solution)/shard_map/reduce_scatter | solution.py:376
  1708.0 456.2 %reduce-scatter.28.cloned.1.call-start = ((), (), s32[]{:S(2)}) async-start(), calls=%async_computation.31 | async-start | bytes 1081344
  1710.6 520.0 %reduce-scatter.26.cloned.1.call-start = ((), (), s32[]{:S(2)}) async-start(), calls=%async_computation.30 | async-start | bytes 6291456 | tf_op jit(solution)/shard_map/reduce_scatter | solution.py:406
  1720.8 567.1 %reduce-scatter.24.cloned.1.call-start = ((), (), s32[]{:S(2)}) async-start(), calls=%async_computation.29 | async-start | bytes 6291456 | tf_op jit(solution)/shard_map/reduce_scatter | solution.py:403
  1731.5 613.5 %reduce-scatter.22.cloned.1.call-start = ((), (), s32[]{:S(2)}) async-start(), calls=%async_computation.28 | async-start | bytes 6291456 | tf_op jit(solution)/shard_map/reduce_scatter | solution.py:400
  1742.2 964.4 %reduce-scatter.20.cloned.1.call-start = ((), (), s32[]{:S(2)}) async-start(), calls=%async_computation.27 | async-start | bytes 17301504 | tf_op jit(solution)/shard_map/reduce_scatter | solution.py:415
  1754.9 1312.8 %reduce-scatter.18.cloned.1.call-start = ((), (), s32[]{:S(2)}) async-start(), calls=%async_computation.26 | async-start | bytes 17301504 | tf_op jit(solution)/shard_map/reduce_scatter | solution.py:414
  2049.4 1379.5 %reduce-scatter.16.cloned.1.call-start = ((), (), s32[]{:S(2)}) async-start(), calls=%async_computation.25 | async-start | bytes 17301504 | tf_op jit(solution)/shard_map/reduce_scatter | solution.py:413
  2072.4 1717.8 %reduce-scatter.14.cloned.1.call-start = ((), (), s32[]{:S(2)}) async-start(), calls=%async_computation.24 | async-start | bytes 17301504 | tf_op jit(solution)/shard_map/reduce_scatter | solution.py:412
  (82 other events, 3687.1 us)
Sparse Core Ops, SparseCore 0:
  9.6 105.1 all-gather.10
  116.3 103.9 all-gather.14
  221.9 103.9 all-gather.18
  328.5 74.7 all-gather.12
  405.9 75.2 all-gather.16
  482.6 104.0 all-gather.20
  612.1 56.6 all-gather.22
  670.3 56.7 all-gather.24
  728.7 56.7 all-gather.26
  1708.1 331.7 reduce-scatter.11
  2042.2 121.9 reduce-scatter.27
  2167.0 63.6 reduce-scatter.25
  2233.5 54.2 reduce-scatter.23
  2290.7 54.2 reduce-scatter.21
  2347.7 358.7 reduce-scatter.19
  2709.2 358.4 reduce-scatter.17
  3070.4 358.4 reduce-scatter.15
  3431.6 358.4 reduce-scatter.13
where the time goes:
time: 3810 us; the launch traced here: 3800 us
  waiting for transfers between devices  2850 us (75%)
  local copies, waits for them, and re-layouts  338 us (9%)
  blocking collectives  280 us (7%)
  matrix products  225 us (6%)
  other arithmetic  54 us (1%)
    reduce_scatter x1, waiting for transfers between devices, body(): lax.psum_scatter(value_wgrad, ('ctx', 'fsdp'), scatter_dimension=0, tiled...  361 us
    reduce_scatter x1, waiting for transfers between devices, body(): lax.psum_scatter(query_wgrad, ('ctx', 'fsdp'), scatter_dimension=0, tiled...  361 us
    reduce_scatter x1, waiting for transfers between devices, body(): lax.psum_scatter(key_wgrad, ('ctx', 'fsdp'), scatter_dimension=0, tiled=T...  361 us
    reduce_scatter x1, waiting for transfers between devices, body(): lax.psum_scatter(out_wgrad, ('ctx', 'fsdp'), scatter_dimension=0, tiled=T...  296 us
    reduce_scatter x1, waiting for transfers between devices, body(): lax.psum_scatter(kv_terms.reshape(length, 2 * model_width), 'ctx', scatte...  285 us
    all_to_all x1, blocking collectives, body(): lax.all_to_all(send_grads, 'ctx', split_axis=0, concat_axis=0, tiled=True)  189 us
    all_to_all x1, waiting for transfers between devices, body(): lax.all_to_all(back_grads, 'ctx', split_axis=0, concat_axis=0, tiled=True)  177 us
    all_to_all x1, waiting for transfers between devices, body(): lax.all_to_all(back_rows, 'ctx', split_axis=0, concat_axis=0, tiled=True)  175 us
  transfers between devices with their start and end apart: 22, of which 17 were waited for; matrix products, arithmetic and copies ran while one was open for 8% of the time, Pallas kernels for 0%

commit v1 on v0

--- a/solution.py
+++ b/solution.py
@@ -3,6 +3,9 @@
 import jax
 import jax.numpy as jnp
 from jax import lax
+from jax.experimental import pallas as pl
+from jax.experimental.pallas import tpu as pltpu
+from jax.sharding import Mesh
 from jax.sharding import PartitionSpec as P
 
 HEAD_DIM = 128
@@ -99,7 +102,7 @@
     return (prob_low, dscore)
 
 
-def body(
+def general_body(
     tokens,
     cotangent,
     attn_gain,
@@ -436,44 +439,499 @@
     )
 
 
+def ring_order(count):
+    return [0, 2, 4, 6, 7, 5, 3, 1] if count == 8 else list(range(count))
+
+
+def swap(array, axis):
+    return lax.ppermute(array, axis, [(0, 1), (1, 0)])
+
+
+def shift(array, by):
+    order = ring_order(lax.axis_size("chip"))
+    count = len(order)
+    pairs = [(order[i], order[(i + by) % count]) for i in range(count)]
+    return lax.ppermute(array, "chip", pairs)
+
+
+def ring_blocks(block, row_axis=0):
+    count = lax.axis_size("chip")
+    blocks = {0: block}
+    ahead, behind = block, block
+    half = block.shape[row_axis] // 2
+    for step in range(1, count // 2):
+        ahead, behind = lax.optimization_barrier((ahead, behind))
+        ahead, behind = shift(ahead, 1), shift(behind, -1)
+        blocks[count - step] = ahead
+        blocks[step] = behind
+    low = lax.slice_in_dim(ahead, 0, half, axis=row_axis)
+    high = lax.slice_in_dim(behind, half, 2 * half, axis=row_axis)
+    low, high = lax.optimization_barrier((low, high))
+    blocks[count // 2] = jnp.concatenate([shift(low, 1), shift(high, -1)], axis=row_axis)
+    return [blocks[place] for place in range(count)]
+
+
+def gather_rows(block, row_axis=0):
+    mine = jnp.concatenate(ring_blocks(block, row_axis), axis=row_axis)
+    return jnp.concatenate([mine, swap(mine, "core")], axis=row_axis)
+
+
+def scatter_rows(terms):
+    count = lax.axis_size("chip")
+    half_rows = terms.shape[0] // 2
+    rows = half_rows // count
+    half = rows // 2
+    both = terms[:half_rows].astype(jnp.float32) + swap(terms[half_rows:], "core").astype(
+        jnp.float32
+    )
+    both = both.astype(jnp.bfloat16)
+
+    def part(place):
+        place = place % count
+        return both[place * rows : (place + 1) * rows]
+
+    far = count // 2
+    ahead, behind = part(far)[:half], part(far)[half:]
+    ahead, behind = shift(ahead, 1), shift(behind, -1)
+
+    def grow(mine, low, high):
+        return (
+            mine.astype(jnp.float32)
+            + jnp.concatenate(
+                [
+                    jnp.zeros_like(mine[:half]) if low is None else low,
+                    jnp.zeros_like(mine[half:]) if high is None else high,
+                ],
+                axis=0,
+            ).astype(jnp.float32)
+        ).astype(jnp.bfloat16)
+
+    ahead = grow(part(far - 1), ahead, None)
+    behind = grow(part(far + 1), None, behind)
+    for step in range(far - 2, -1, -1):
+        ahead, behind = lax.optimization_barrier((ahead, behind))
+        ahead, behind = shift(ahead, 1), shift(behind, -1)
+        if step:
+            ahead = (part(step).astype(jnp.float32) + ahead.astype(jnp.float32)).astype(
+                jnp.bfloat16
+            )
+            behind = (part(-step).astype(jnp.float32) + behind.astype(jnp.float32)).astype(
+                jnp.bfloat16
+            )
+    return part(0).astype(jnp.float32) + ahead.astype(jnp.float32) + behind.astype(jnp.float32)
+
+
+def exchange(parts):
+    count = lax.axis_size("chip")
+    got = {0: parts[0]}
+    for place in range(1, count):
+        got[count - place] = shift(parts[place], place)
+    return jnp.stack([got[place] for place in range(count)], axis=0)
+
+
+def exchange_all(parts):
+    count = lax.axis_size("chip")
+    pair = jnp.stack([parts[:count], swap(parts[count:], "core")], axis=1)
+    got = exchange(pair)
+    return jnp.concatenate([got[:, 0], got[:, 1]], axis=0)
+
+
+def sum_all(values):
+    count = lax.axis_size("chip")
+    both = values + swap(values[:, ::-1], "core")
+    total = both
+    for place in range(1, count):
+        total = total + jnp.roll(shift(both, place), -place, axis=2)
+    return total
+
+
+ATTN_ROWS = 256
+
+
+def attend_kernel(q_ref, k_ref, v_ref, out_ref, lse_ref, *, score_scale):
+    scores = contract_cols(q_ref[...], k_ref[...]) * score_scale
+    row_max = jnp.max(scores, axis=-1, keepdims=True)
+    raw = jnp.exp(scores - row_max)
+    total = jnp.sum(raw, axis=-1, keepdims=True)
+    probs = (raw / total).astype(jnp.bfloat16)
+    out_ref[...] = product(probs, v_ref[...]).astype(jnp.bfloat16)
+    lse_ref[...] = row_max + jnp.log(total)
+
+
+def attend(queries, keys, values, score_scale):
+    length, width = queries.shape
+    rows = ATTN_ROWS
+    whole = pl.BlockSpec((length, width), lambda i: (0, 0))
+    block = pl.BlockSpec((rows, width), lambda i: (i, 0))
+    column = pl.BlockSpec((rows, 1), lambda i: (i, 0))
+    return pl.pallas_call(
+        lambda *refs: attend_kernel(*refs, score_scale=score_scale),
+        grid=(length // rows,),
+        in_specs=[block, whole, whole],
+        out_specs=[block, column],
+        out_shape=[
+            jax.ShapeDtypeStruct((length, width), jnp.bfloat16),
+            jax.ShapeDtypeStruct((length, 1), jnp.float32),
+        ],
+        compiler_params=pltpu.CompilerParams(vmem_limit_bytes=48 << 20),
+        cost_estimate=pl.CostEstimate(
+            flops=4 * length * length * width,
+            bytes_accessed=8 * length * width,
+            transcendentals=length * length,
+        ),
+        name="attend",
+    )(queries, keys, values)
+
+
+def attend_back_kernel(
+    q_ref, d_ref, lse_ref, k_ref, v_ref, dq_ref, dk_ref, dv_ref, *, score_scale
+):
+    @pl.when(pl.program_id(0) == 0)
+    def _():
+        dk_ref[...] = jnp.zeros_like(dk_ref)
+        dv_ref[...] = jnp.zeros_like(dv_ref)
+
+    queries, douts = q_ref[...], d_ref[...]
+    probs = jnp.exp(contract_cols(queries, k_ref[...]) * score_scale - lse_ref[...])
+    dprobs = contract_cols(douts, v_ref[...])
+    delta = jnp.sum(probs * dprobs, axis=-1, keepdims=True)
+    dscores = (probs * (dprobs - delta)).astype(jnp.bfloat16)
+    dq_ref[...] = product(dscores, k_ref[...]) * score_scale
+    dk_ref[...] += contract_rows(dscores, queries) * score_scale
+    dv_ref[...] += contract_rows(probs.astype(jnp.bfloat16), douts)
+
+
+def attend_back(queries, douts, lse, keys, values, score_scale):
+    length, width = queries.shape
+    rows = ATTN_ROWS
+    whole = pl.BlockSpec((length, width), lambda i: (0, 0))
+    block = pl.BlockSpec((rows, width), lambda i: (i, 0))
+    column = pl.BlockSpec((rows, 1), lambda i: (i, 0))
+    return pl.pallas_call(
+        lambda *refs: attend_back_kernel(*refs, score_scale=score_scale),
+        grid=(length // rows,),
+        in_specs=[block, block, column, whole, whole],
+        out_specs=[block, whole, whole],
+        out_shape=[jax.ShapeDtypeStruct((length, width), jnp.float32)] * 3,
+        compiler_params=pltpu.CompilerParams(vmem_limit_bytes=48 << 20),
+        cost_estimate=pl.CostEstimate(
+            flops=10 * length * length * width,
+            bytes_accessed=20 * length * width,
+            transcendentals=length * length,
+        ),
+        name="attend_back",
+    )(queries, douts, lse, keys, values)
+
+
+def body(
+    tokens,
+    cotangent,
+    attn_gain,
+    w_query,
+    w_key,
+    w_value,
+    w_out,
+    query_gain,
+    key_gain,
+    ffn_gain,
+    router,
+    w_gate,
+    w_up,
+    w_down,
+    routes,
+    priority,
+    positions,
+):
+    low = jnp.bfloat16
+    chips = lax.axis_size("chip")
+    ctx_count = chips * 2
+    place = lax.axis_index("chip") * 2 + lax.axis_index("core")
+    part = lax.axis_index("fsdp")
+    tok_rows, model_width = tokens.shape[1:]
+    half_width = model_width // 2
+    head_dim = HEAD_DIM
+    length = tok_rows * ctx_count
+    capacity = 9 * tok_rows
+    score_scale = head_dim ** (-0.5)
+    per_half = ctx_count // 2
+
+    def turn(matrix, axis=-1):
+        first, second = jnp.split(matrix, 2, axis=axis)
+        return jnp.where(
+            part == 0, matrix, jnp.concatenate([second, first], axis=axis)
+        )
+
+    def head_rows(matrix, width):
+        return lax.dynamic_slice_in_dim(matrix, (place % per_half) * width, width, 0)
+
+    small = jnp.concatenate(
+        [
+            router.T,
+            attn_gain[None],
+            ffn_gain[None],
+            jnp.concatenate(
+                [
+                    head_rows(query_gain, head_dim),
+                    head_rows(key_gain, head_dim),
+                    jnp.zeros((half_width - 2 * head_dim,), low),
+                ]
+            )[None],
+        ],
+        axis=0,
+    )
+    small_other = swap(small, "fsdp")
+    expert_count = router.shape[1]
+    r_weight = jnp.concatenate([small[:expert_count], small_other[:expert_count]], axis=1)
+    g_attn = jnp.concatenate([small[expert_count], small_other[expert_count]]).astype(jnp.float32)
+    g_ffn = jnp.concatenate([small[expert_count + 1], small_other[expert_count + 1]]).astype(
+        jnp.float32
+    )
+    here = part == place // per_half
+    g_heads = jnp.where(here, small[expert_count + 2], small_other[expert_count + 2]).astype(
+        jnp.float32
+    )
+    g_query, g_key = g_heads[:head_dim], g_heads[head_dim : 2 * head_dim]
+
+    qkv_mine = jnp.concatenate(
+        [
+            lax.dynamic_slice_in_dim(w, place * head_dim, head_dim, 1)
+            for w in (w_query, w_key, w_value)
+        ],
+        axis=1,
+    )
+    qkv_weight = jnp.concatenate([qkv_mine, swap(qkv_mine, "fsdp")], axis=0)
+    out_mine = head_rows(w_out, head_dim)
+    out_weight = turn(jnp.where(here, out_mine, swap(out_mine, "fsdp")))
+
+    route_ids, level_ids = routes[0], priority[0]
+    hot = route_ids[:, :, None] == jnp.arange(expert_count, dtype=jnp.int32)[None, None, :]
+    levels = jnp.sum(jnp.where(hot, level_ids[:, :, None] - LEVELS, 0), axis=1) + LEVELS
+    tags = jnp.concatenate(
+        [
+            levels.T,
+            (place * tok_rows + jnp.arange(tok_rows, dtype=jnp.int32))[None],
+            positions,
+        ],
+        axis=0,
+    )
+    all_tags = gather_rows(tags, 1)
+    expert_levels = lax.dynamic_index_in_dim(all_tags, place, 0, False)
+    order_ids = all_tags[expert_count]
+    sort_code = expert_levels * length + order_ids
+    ranks = jnp.sum((sort_code[None, :] < sort_code[:, None]).astype(jnp.float32), axis=1)
+    is_kept = (expert_levels < LEVELS) & (ranks < capacity)
+    source_ids = order_ids.reshape(ctx_count, tok_rows)[:, 0] // tok_rows
+    to_source = (
+        source_ids[None, :] == jnp.arange(ctx_count, dtype=jnp.int32)[:, None]
+    ).astype(jnp.float32)
+    cosine, sine_part = rope_tables(all_tags[expert_count + 1], head_dim)
+    cosine, sine_part = cosine[:, 0], sine_part[:, 0]
+    cos_full = jnp.concatenate([cosine, cosine], axis=-1)
+    sin_full = jnp.concatenate([-sine_part, sine_part], axis=-1)
+
+    def spin(matrix):
+        return jnp.concatenate([matrix[:, head_dim // 2 :], matrix[:, : head_dim // 2]], axis=-1)
+
+    inputs = turn(tokens[0]).astype(jnp.float32)
+    grad_low = turn(cotangent[0])
+    grad_out = grad_low.astype(jnp.float32)
+    normed, inv_one = rms_forward(inputs, g_attn)
+    all_h_one = gather_rows(normed.astype(low))
+    lin = product(all_h_one, qkv_weight)
+    q_lin, k_lin, v_lin = jnp.split(lin, 3, axis=1)
+
+    def token_sums(*columns):
+        stacked = jnp.stack(columns, axis=0).reshape(len(columns), 2, chips, tok_rows)
+        return sum_all(stacked).reshape(len(columns), length, 1) / model_width
+
+    square = token_sums(jnp.sum(q_lin * q_lin, axis=-1), jnp.sum(k_lin * k_lin, axis=-1))
+    inv_query, inv_key = lax.rsqrt(square[0] + epsilon), lax.rsqrt(square[1] + epsilon)
+    q_normed = q_lin * inv_query * g_query
+    k_normed = k_lin * inv_key * g_key
+    q_rot = (q_normed * cos_full + spin(q_normed) * sin_full).astype(low)
+    k_rot = (k_normed * cos_full + spin(k_normed) * sin_full).astype(low)
+    v_low = v_lin.astype(low)
+    mixed_low, lse = attend(q_rot, k_rot, v_low, score_scale)
+    middle = inputs + scatter_rows(product(mixed_low, out_weight).astype(low))
+
+    h_two_f, inv_two = rms_forward(middle, g_ffn)
+    h_two = h_two_f.astype(low)
+    logits = contract_cols(h_two, r_weight)
+    row_max = jnp.max(logits, axis=-1, keepdims=True)
+    exps_raw = jnp.exp(logits - row_max)
+    router_probs = exps_raw / jnp.sum(exps_raw, axis=-1, keepdims=True)
+    all_probs = gather_rows(router_probs.T, 1)
+    share = jnp.where(is_kept, lax.dynamic_index_in_dim(all_probs, place, 0, False), 0.0)[:, None]
+    all_h_two = gather_rows(h_two)
+    all_grads = gather_rows(grad_low)
+    gate_weight = jnp.concatenate([w_gate[0], swap(w_gate[0], "fsdp")], axis=0)
+    up_weight = jnp.concatenate([w_up[0], swap(w_up[0], "fsdp")], axis=0)
+    down_weight = jnp.concatenate([w_down[0], swap(w_down[0], "fsdp")], axis=1)
+    gate_lin = product(all_h_two, gate_weight)
+    up_lin = product(all_h_two, up_weight)
+    sig_gate = jax.nn.sigmoid(gate_lin)
+    silu_val = gate_lin * sig_gate
+    swiglu = (silu_val * up_lin).astype(low)
+    expert_out = product(swiglu, down_weight).astype(low).astype(jnp.float32)
+    layer_rows = middle + scatter_rows((share * expert_out).astype(low))
+    layer_out = turn(layer_rows.astype(low))
+    grads_f = all_grads.astype(jnp.float32)
+    share_grad = jnp.where(is_kept, jnp.sum(expert_out * grads_f, axis=-1), 0.0)
+    out_grad = (share * grads_f).astype(low)
+    act_grad = contract_cols(out_grad, down_weight)
+    gate_grad = (act_grad * up_lin * sig_gate * (1.0 + gate_lin * (1.0 - sig_gate))).astype(low)
+    up_grad = (act_grad * silu_val).astype(low)
+    in_grad = (contract_cols(gate_grad, gate_weight) + contract_cols(up_grad, up_weight)).astype(low)
+    hidden_sum = scatter_rows(in_grad)
+    down_wgrad = contract_rows(swiglu, out_grad)
+    gate_wgrad = contract_rows(all_h_two, gate_grad)
+    up_wgrad = contract_rows(all_h_two, up_grad)
+
+    def over_sequences(matrix, axis):
+        mine, other = jnp.split(matrix, 2, axis=axis)
+        return mine + swap(other.astype(low), "fsdp").astype(jnp.float32)
+
+    s_gate = over_sequences(gate_wgrad, 0)[None]
+    s_up = over_sequences(up_wgrad, 0)[None]
+    s_down = over_sequences(down_wgrad, 1)[None]
+
+    prob_grad = exchange_all(share_grad.reshape(ctx_count, tok_rows))
+    prob_grad = precise(to_source, prob_grad).T
+    logit_grad = router_probs * (
+        prob_grad - jnp.sum(router_probs * prob_grad, axis=-1, keepdims=True)
+    )
+    hidden_grad = hidden_sum + precise(logit_grad, r_weight.astype(jnp.float32))
+    router_wgrad = precise(h_two.astype(jnp.float32).T, logit_grad)
+    norm_grad, ffn_gain_grad = rms_backward(middle, inv_two, g_ffn, hidden_grad)
+    middle_grad = grad_out + norm_grad
+
+    all_branch = gather_rows(middle_grad.astype(low))
+    out_wgrad = contract_rows(mixed_low, all_branch)
+    douts = contract_cols(all_branch, out_weight).astype(low)
+    dq, dk, dv = attend_back(q_rot, douts, lse, k_rot, v_low, score_scale)
+    q_back = dq * cos_full - spin(dq) * sin_full
+    k_back = dk * cos_full - spin(dk) * sin_full
+    along = token_sums(
+        jnp.sum(q_back * g_query * q_lin, axis=-1), jnp.sum(k_back * g_key * k_lin, axis=-1)
+    )
+    q_lin_grad = inv_query * (q_back * g_query) - q_lin * inv_query**3 * along[0]
+    k_lin_grad = inv_key * (k_back * g_key) - k_lin * inv_key**3 * along[1]
+    query_gain_grad = jnp.sum(q_back * q_lin * inv_query, axis=0)
+    key_gain_grad = jnp.sum(k_back * k_lin * inv_key, axis=0)
+    lin_grad = jnp.concatenate([q_lin_grad, k_lin_grad, dv], axis=1).astype(low)
+    h_grad = scatter_rows(contract_cols(lin_grad, qkv_weight).astype(low))
+    qkv_wgrad = contract_rows(all_h_one, lin_grad)
+    in_norm_grad, attn_gain_grad = rms_backward(inputs, inv_one, g_attn, h_grad)
+    input_grad = turn((middle_grad + in_norm_grad).astype(low))
+
+    own_rows = model_width // (2 * ctx_count)
+
+    def pick(blocks, index):
+        return lax.dynamic_index_in_dim(blocks, index, 1, False)
+
+    def keep_part(blocks):
+        sent = swap(pick(blocks, 1 - part).astype(low), "fsdp").astype(jnp.float32)
+        return pick(blocks, part) + sent
+
+    out_rows = turn(out_wgrad).reshape(1, 2, own_rows, model_width)
+    d_out = keep_part(out_rows)[0]
+    gain_rows = jnp.stack([query_gain_grad, key_gain_grad], axis=0).reshape(2, 2, own_rows)
+    gain_rows = pick(gain_rows, part) + swap(pick(gain_rows, 1 - part), "fsdp")
+    d_qgain, d_kgain = gain_rows[0], gain_rows[1]
+
+    def by_owner(matrix):
+        rows = turn(matrix, 0).reshape(ctx_count, 2, own_rows, -1)
+        return rows
+
+    wide = keep_part(by_owner(qkv_wgrad)).astype(low)
+    received = exchange_all(wide[source_ids])
+    back_ids = jnp.sum(
+        to_source.astype(jnp.int32) * jnp.arange(ctx_count, dtype=jnp.int32)[None, :], axis=1
+    )
+    dense = received[back_ids].reshape(ctx_count, own_rows, 3, head_dim).astype(jnp.float32)
+    d_query, d_key, d_value = (
+        dense[:, :, i].transpose(1, 0, 2).reshape(own_rows, model_width) for i in range(3)
+    )
+    thin = jnp.concatenate(
+        [router_wgrad, ffn_gain_grad[:, None], attn_gain_grad[:, None]], axis=1
+    )
+    thin_rows = by_owner(thin)
+    thin_rows = pick(thin_rows, part) + swap(pick(thin_rows, 1 - part), "fsdp")
+    thin_sum = jnp.sum(exchange_all(thin_rows[source_ids]), axis=0)
+    d_router = thin_sum[:, :expert_count]
+    d_ffn, d_attn = thin_sum[:, expert_count], thin_sum[:, expert_count + 1]
+    return (
+        layer_out[None],
+        input_grad[None],
+        d_attn,
+        d_query,
+        d_key,
+        d_value,
+        d_out,
+        d_qgain,
+        d_kgain,
+        d_ffn,
+        d_router,
+        s_gate,
+        s_up,
+        s_down,
+    )
+
+
+def specs_of(ctx):
+    rows, both = P("fsdp", ctx, None), ctx + ("fsdp",)
+    dense = P("fsdp", None)
+    ins = (
+        rows,
+        rows,
+        P("fsdp"),
+        dense,
+        dense,
+        dense,
+        dense,
+        P("fsdp"),
+        P("fsdp"),
+        P("fsdp"),
+        dense,
+        P(ctx, "fsdp", None),
+        P(ctx, "fsdp", None),
+        P(ctx, None, "fsdp"),
+        rows,
+        rows,
+        P("fsdp", ctx),
+    )
+    line, matrix = P(both), P(both, None)
+    outs = (
+        rows,
+        rows,
+        line,
+        matrix,
+        matrix,
+        matrix,
+        matrix,
+        line,
+        line,
+        line,
+        matrix,
+        P(ctx, "fsdp", None),
+        P(ctx, "fsdp", None),
+        P(ctx, None, "fsdp"),
+    )
+    return ins, outs
+
+
 def solution(mesh):
-    return jax.shard_map(
-        body,
-        mesh=mesh,
-        in_specs=(
-            P("fsdp", "ctx", None),
-            P("fsdp", "ctx", None),
-            P("fsdp"),
-            P("fsdp", None),
-            P("fsdp", None),
-            P("fsdp", None),
-            P("fsdp", None),
-            P("fsdp"),
-            P("fsdp"),
-            P("fsdp"),
-            P("fsdp", None),
-            P("ctx", "fsdp", None),
-            P("ctx", "fsdp", None),
-            P("ctx", None, "fsdp"),
-            P("fsdp", "ctx", None),
-            P("fsdp", "ctx", None),
-            P("fsdp", "ctx"),
-        ),
-        out_specs=(
-            P("fsdp", "ctx", None),
-            P("fsdp", "ctx", None),
-            P(("ctx", "fsdp")),
-            P(("ctx", "fsdp"), None),
-            P(("ctx", "fsdp"), None),
-            P(("ctx", "fsdp"), None),
-            P(("ctx", "fsdp"), None),
-            P(("ctx", "fsdp")),
-            P(("ctx", "fsdp")),
-            P(("ctx", "fsdp")),
-            P(("ctx", "fsdp"), None),
-            P("ctx", "fsdp", None),
-            P("ctx", "fsdp", None),
-            P("ctx", None, "fsdp"),
-        ),
-        check_vma=False,
-    )
+    ctx_count, fsdp_count = mesh.shape["ctx"], mesh.shape["fsdp"]
+
+    def whole(*arrays):
+        heads = arrays[0].shape[2] // HEAD_DIM
+        experts = arrays[10].shape[1]
+        if ctx_count == heads == experts and fsdp_count == 2 and ctx_count % 4 == 0:
+            chips = Mesh(mesh.devices.reshape(-1, 2, 2), ("chip", "core", "fsdp"))
+            run, grid, ctx = body, chips, ("chip", "core")
+        else:
+            run, grid, ctx = general_body, mesh, ("ctx",)
+        ins, outs = specs_of(ctx)
+        return jax.shard_map(run, mesh=grid, in_specs=ins, out_specs=outs, check_vma=False)(*arrays)
+
+    return whole

time: 3810 us -> 978 us (0.26)
  waiting for transfers between devices: 2850 us -> 387 us
  blocking collectives: 280 us -> 0 us
  local copies, waits for them, and re-layouts: 338 us -> 127 us
  starting transfers between devices: 32 us -> 168 us
  matrix products: 225 us -> 168 us
    reduce_scatter x8 -> x0, waiting for transfers between devices: 1840 us -> none  [the longest x1 361 us: body(): lax.psum_scatter(value_wgrad, ('ctx', 'fsdp'), scatter_dimension=0, tiled...]
    all_to_all x4 -> x0, waiting for transfers between devices: 523 us -> none  [the longest x1 177 us: body(): lax.all_to_all(back_grads, 'ctx', split_axis=0, concat_axis=0, tiled=True)]
    all_gather x9 -> x0, waiting for transfers between devices: 408 us -> none  [the longest x1 101 us: body(): lax.all_gather(w_value, 'fsdp', axis=0, tiled=True)]
    ppermute x0 -> x143, waiting for transfers between devices: none -> 387 us  [the longest x115 225 us: shift(): return lax.ppermute(array, 'chip', pairs)]
    all_to_all x1 -> x0, blocking collectives: 189 us -> none  [body(): lax.all_to_all(send_grads, 'ctx', split_axis=0, concat_axis=0, tiled=True)]
    ppermute x0 -> x143, starting transfers between devices: none -> 168 us  [the longest x115 153 us: shift(): return lax.ppermute(array, 'chip', pairs)]
    gather x9 -> x3, local copies, waits for them, and re-layouts: 146 us -> 5.14 us  [the longest x1 2.8 us: body(): received = exchange_all(wide[source_ids])]
    unnamed x19 -> x0, waiting for transfers between devices: 82.1 us -> none
  transfers between devices with their start and end apart: 22 -> 143, of which waited for: 17 -> 78; matrix products, arithmetic and copies ran while one was open for 8% -> 27% of each run, Pallas kernels for 0% -> 0%
where the time goes in v1:
time: 978 us; the launch traced here: 967 us
  waiting for transfers between devices  387 us (40%)
  starting transfers between devices  168 us (17%)
  matrix products  168 us (17%)
  local copies, waits for them, and re-layouts  127 us (13%)
  other arithmetic  87.3 us (9%)
  Pallas kernels  26.4 us (3%)
    ppermute x115, waiting for transfers between devices, shift(): return lax.ppermute(array, 'chip', pairs)  225 us
    ppermute x28, waiting for transfers between devices, swap(): return lax.ppermute(array, axis, [(0, 1), (1, 0)])  162 us
    ppermute x115, starting transfers between devices, shift(): return lax.ppermute(array, 'chip', pairs)  153 us
    dot_general x5, matrix products, product(): return jnp.dot(left, right, preferred_element_type=jnp.float32)  59.3 us
    dot_general x6, matrix products, contract_cols(): lax.dot_general(left, right, (((1,), (1,)), ((), ())), preferred_element_...  58.4 us
    dot_general x5, matrix products, contract_rows(): lax.dot_general(left, right, (((0,), (0,)), ((), ())), preferred_element_...  48.7 us
    unnamed x236, local copies, waits for them, and re-layouts  44.6 us
  transfers between devices with their start and end apart: 143, of which 78 were waited for; matrix products, arithmetic and copies ran while one was open for 27% of the time, Pallas kernels for 0%

profile of v1, /device:TPU:8, one launch (start us, length us, event | category | flops | bytes accessed | tf_op | source)
XLA Modules:
  0.0 967.1 jit_solution(8756044039918922722)
XLA Ops:
  12.3 11.3 %collective-permute-done.1 = bf16[128,2048]{1,0:T(8,128)(2,1)S(1)} collective-permute-done((bf16[128,2048]{1,0:T(8,128)(2,1)S(1)}, bf16[128,2048]{1,0:T(8,128)(2,1)S(1)}, u32[]{:S(2)}, u32[]{:S(2)}) %collective-permute-start.1) | collective-permute-done | bytes 524320 | tf_op jit(solution)/shard_map/ppermute | solution.py:454
  25.7 10.2 %collective-permute-done.3 = bf16[128,2048]{1,0:T(8,128)(2,1)S(1)} collective-permute-done((bf16[128,2048]{1,0:T(8,128)(2,1)S(1)}, bf16[128,2048]{1,0:T(8,128)(2,1)S(1)}, u32[]{:S(2)}, u32[]{:S(2)}) %collective-permute-start.3) | collective-permute-done | bytes 524320 | tf_op jit(solution)/shard_map/ppermute | solution.py:454
  129.5 10.4 %attend.1 = (bf16[2048,128]{1,0:T(8,128)(2,1)S(1)}, f32[2048,1]{1,0:T(8,128)S(1)}) custom-call(bf16[2048,128]{1,0:T(8,128)(2,1)S(1)} %fusion.28.refs_0_, bf16[2048,128]{1,0:T(8,128)(2,1)S(1)} %get-tuple-element.199.refs_1_.refs_3_, bf16[2048,128]{1,0:T(8,128)(2,1)S(1)} %split.155.refs_2_.refs_4_), custom_call_target="tpu_custom_call" | custom-call | flops 2147483648 | bytes 2097152 | tf_op jit(solution)/shard_map/attend/pallas_call | solution.py:567
  163.4 8.9 collective-permute-done.68
  174.4 9.2 collective-permute-done.32
  196.9 9.2 collective-permute-done.34
  248.4 9.3 collective-permute-done.49
  260.7 9.2 collective-permute-done.51
  314.3 20.4 %collective-permute-done.58 = bf16[1024,1024]{1,0:T(8,128)(2,1)} collective-permute-done((bf16[1024,1024]{1,0:T(8,128)(2,1)}, bf16[1024,1024]{1,0:T(8,128)(2,1)}, u32[]{:S(2)}, u32[]{:S(2)}) %collective-permute-start.58) | collective-permute-done | bytes 2097184 | tf_op jit(solution)/shard_map/ppermute | solution.py:447
  334.6 14.6 %fusion.9 = f32[2048,1024]{1,0:T(8,128)} fusion(bf16[2048,2048]{1,0:T(8,128)(2,1)} %constant_dynamic-update-slice_fusion.47, f32[2048]{0:T(1024)S(1)} %get-tuple-element.193, bf16[1024,1024]{1,0:T(8,128)(2,1)} %collective-permute-done.58, bf16[1024,1024]{1,0:T(8,128)(2,1)} %bitcast.15), kind=kOutput, calls=%fused_computation.36 | convolution fusion | flops 8610906112 | bytes 20979712 | tf_op jit(solution)/shard_map/dot_general | solution.py:45
  354.1 70.0 %collective-permute-done.57 = bf16[1024,1024]{1,0:T(8,128)(2,1)} collective-permute-done((bf16[1024,1024]{1,0:T(8,128)(2,1)}, bf16[1024,1024]{1,0:T(8,128)(2,1)}, u32[]{:S(2)}, u32[]{:S(2)}) %collective-permute-start.57) | collective-permute-done | bytes 2097184 | tf_op jit(solution)/shard_map/ppermute | solution.py:447
  424.1 13.8 %fusion.12 = f32[2048,1024]{1,0:T(8,128)} fusion(bf16[2048,2048]{1,0:T(8,128)(2,1)} %constant_dynamic-update-slice_fusion.28, bf16[1024,1024]{1,0:T(8,128)(2,1)} %collective-permute-done.57, bf16[1024,1024]{1,0:T(8,128)(2,1)S(1)} %bitcast.351), kind=kOutput, calls=%fused_computation.39 | convolution fusion | flops 8598323200 | bytes 20971520 | tf_op jit(solution)/shard_map/dot_general | solution.py:31
  437.9 22.6 %multiply_convert_fusion.1 = (bf16[2048,1024]{1,0:T(8,128)(2,1)}, bf16[2048,1024]{1,0:T(8,128)(2,1)}, bf16[2048,1024]{1,0:T(8,128)(2,1)}) fusion(f32[2048,1024]{1,0:T(8,128)} %fusion.9, f32[2048,1024]{1,0:T(8,128)} %fusion.12, bf16[2048,2048]{1,0:T(8,128)(2,1)} %constant_dynamic-update-slice_fusion.28, bf16[1024,1024]{1,0:T(8,128)(2,1)} %collective-permute-done.56, ...), kind=kOutput, calls=%fused_computation.14 | convolution fusion | flops 8629780480 | bytes 41943040 | tf_op jit(solution)/shard_map/dot_general | solution.py:31
  460.5 15.1 %fusion.11 = f32[2048,2048]{1,0:T(8,128)} fusion(bf16[2048,1024]{1,0:T(8,128)(2,1)} %get-tuple-element.206, bf16[1024,1024]{1,0:T(8,128)(2,1)} %collective-permute-done.57, bf16[1024,1024]{1,0:T(8,128)(2,1)S(1)} %bitcast.352), kind=kOutput, calls=%fused_computation.38 | convolution fusion | flops 8598323200 | bytes 25165824 | tf_op jit(solution)/shard_map/dot_general | solution.py:45
  475.6 16.6 %add_convert_fusion = bf16[2048,2048]{1,0:T(8,128)(2,1)} fusion(f32[2048,2048]{1,0:T(8,128)} %fusion.11, bf16[2048,1024]{1,0:T(8,128)(2,1)} %get-tuple-element.205, bf16[1024,1024]{1,0:T(8,128)(2,1)} %collective-permute-done.56, bf16[1024,1024]{1,0:T(8,128)(2,1)} %bitcast.355), kind=kOutput, calls=%fused_computation.9 | convolution fusion | flops 8606711808 | bytes 33554432 | tf_op jit(solution)/shard_map/dot_general | solution.py:45
  497.5 13.4 %fusion.2 = (f32[2048]{0:T(1024)S(1)}, bf16[2048,2048]{1,0:T(8,128)(2,1)S(1)}) fusion(bf16[2048,2048]{1,0:T(8,128)(2,1)} %constant_dynamic-update-slice_fusion.47, f32[2048]{0:T(1024)S(1)} %get-tuple-element.193, bf16[2048,1024]{1,0:T(8,128)(2,1)} %get-tuple-element.207, bf16[1024,1024]{1,0:T(8,128)(2,1)} %collective-permute-done.58, ...), kind=kOutput, calls=%fused_computation.8 | convolution fusion | flops 8627681280 | bytes 25182208 | tf_op jit(solution)/shard_map/dot_general | solution.py:31
  515.2 14.4 %fusion.7 = f32[1024,2048]{1,0:T(8,128)} fusion(bf16[2048,1024]{1,0:T(8,128)(2,1)S(1)} %copy-done.86, bf16[2048,2048]{1,0:T(8,128)(2,1)} %constant_dynamic-update-slice_fusion.47, f32[2048]{0:T(1024)S(1)} %get-tuple-element.193), kind=kOutput, calls=%fused_computation.35 | convolution fusion | flops 8602517504 | bytes 20979712 | tf_op jit(solution)/shard_map/dot_general | solution.py:39
  547.8 10.7 %collective-permute-done.89 = f32[2,128]{1,0:T(2,128)S(1)} collective-permute-done((f32[2,128]{1,0:T(2,128)S(1)}, f32[2,128]{1,0:T(2,128)S(1)}, u32[]{:S(2)}, u32[]{:S(2)}) %collective-permute-start.89) | collective-permute-done | bytes 1056 | tf_op jit(solution)/shard_map/ppermute | solution.py:454
  590.7 13.1 %fusion.158 = f32[2048,1024]{1,0:T(8,128)S(1)} fusion(bf16[2048,2048]{1,0:T(8,128)(2,1)} %constant_dynamic-update-slice_fusion.28, bf16[2048,1024]{1,0:T(8,128)(2,1)} %get-tuple-element.205), kind=kOutput, calls=%fused_computation.483 | convolution fusion | flops 8589934592 | bytes 20971520 | tf_op jit(solution)/shard_map/dot_general | solution.py:39
  653.9 11.8 %fusion.159 = f32[2048,1024]{1,0:T(8,128)S(1)} fusion(bf16[2048,2048]{1,0:T(8,128)(2,1)} %constant_dynamic-update-slice_fusion.28, bf16[2048,1024]{1,0:T(8,128)(2,1)S(1)} %copy-done.87), kind=kOutput, calls=%fused_computation.484 | convolution fusion | flops 8589934592 | bytes 20971520 | tf_op jit(solution)/shard_map/dot_general | solution.py:39
  689.8 13.3 %collective-permute-done.140 = bf16[1024,1024]{1,0:T(8,128)(2,1)} collective-permute-done((bf16[1024,1024]{1,0:T(8,128)(2,1)}, bf16[1024,1024]{1,0:T(8,128)(2,1)}, u32[]{:S(2)}, u32[]{:S(2)}) %collective-permute-start.140) | collective-permute-done | bytes 2097184 | tf_op jit(solution)/shard_map/ppermute | solution.py:447
  709.0 31.2 %collective-permute-done.141 = bf16[1024,1024]{1,0:T(8,128)(2,1)} collective-permute-done((bf16[1024,1024]{1,0:T(8,128)(2,1)}, bf16[1024,1024]{1,0:T(8,128)(2,1)}, u32[]{:S(2)}, u32[]{:S(2)}) %collective-permute-start.141) | collective-permute-done | bytes 2097184 | tf_op jit(solution)/shard_map/ppermute | solution.py:447
  763.6 16.0 %attend_back.1 = (f32[2048,128]{1,0:T(8,128)S(1)}, f32[2048,128]{1,0:T(8,128)S(1)}, f32[2048,128]{1,0:T(8,128)S(1)}) custom-call(bf16[2048,128]{1,0:T(8,128)(2,1)S(1)} %copy-done.5, bf16[2048,128]{1,0:T(8,128)(2,1)S(1)} %convolution_convert_fusion.3.refs_1_, f32[2048,1]{1,0:T(8,128)} %copy-done.8, bf16[2048,128]{1,0:T(8,128)(2,1)S(1)} %copy-done.7, ...), custom_call_target="tpu_custom_call" | custom-call | flops 5368709120 | bytes 5242880 | tf_op jit(solution)/shard_map/attend_back/pallas_call | solution.py:610
  837.0 16.5 %collective-permute-done.129 = bf16[16,64,384]{2,1,0:T(8,128)(2,1)S(1)} collective-permute-done((bf16[16,64,384]{2,1,0:T(8,128)(2,1)S(1)}, bf16[16,64,384]{2,1,0:T(8,128)(2,1)S(1)}, u32[]{:S(2)}, u32[]{:S(2)}) %collective-permute-start.129) | collective-permute-done | bytes 786464 | tf_op jit(solution)/shard_map/ppermute | solution.py:447
  (726 shorter events, 573.1 us)
Async XLA Ops:
  65.2 28.1 %collective-permute-start.9 = (bf16[1024,2048]{1,0:T(8,128)(2,1)}, bf16[1024,2048]{1,0:T(8,128)(2,1)}, u32[]{:S(2)}, u32[]{:S(2)}) collective-permute-start(bf16[1024,2048]{1,0:T(8,128)(2,1)} %get-tuple-element.318), channel_id=1, source_target_pairs={{0,2},{2,0},{1,3},{3,1},{4,6},{6,4},{5,7},{7,5},{8,10},{10,8},{9,1... | collective-permute-start | bytes 12582920 | tf_op jit(solution)/shard_map/ppermute | solution.py:447
  69.2 38.8 %collective-permute-start.28 = (bf16[128,2048]{1,0:T(8,128)(2,1)}, bf16[128,2048]{1,0:T(8,128)(2,1)}, u32[]{:S(2)}, u32[]{:S(2)}) collective-permute-start(bf16[128,2048]{1,0:T(8,128)(2,1)} %constant_dynamic-slice_fusion.5), channel_id=1, source_target_pairs={{0,1},{1,0},{2,3},{3,2},{4,5},{5,4},{6,7},{7,6},{8,9},{9,8},{10,11... | collective-permute-start | bytes 1572872 | tf_op jit(solution)/shard_map/ppermute | solution.py:447
  248.4 61.0 %collective-permute-start.76 = (bf16[1024,2048]{1,0:T(8,128)(2,1)}, bf16[1024,2048]{1,0:T(8,128)(2,1)}, u32[]{:S(2)}, u32[]{:S(2)}) collective-permute-start(bf16[1024,2048]{1,0:T(8,128)(2,1)} %get-tuple-element.288), channel_id=1, source_target_pairs={{0,2},{2,0},{1,3},{3,1},{4,6},{6,4},{5,7},{7,5},{8,10},{10,8},{9,1... | collective-permute-start | bytes 12582920 | tf_op jit(solution)/shard_map/ppermute | solution.py:447
  285.9 63.4 %collective-permute-start.55 = (bf16[1024,2048]{1,0:T(8,128)(2,1)}, bf16[1024,2048]{1,0:T(8,128)(2,1)}, u32[]{:S(2)}, u32[]{:S(2)}) collective-permute-start(bf16[1024,2048]{1,0:T(8,128)(2,1)} %get-tuple-element.304), channel_id=1, source_target_pairs={{0,2},{2,0},{1,3},{3,1},{4,6},{6,4},{5,7},{7,5},{8,10},{10,8},{9,1... | collective-permute-start | bytes 12582920 | tf_op jit(solution)/shard_map/ppermute | solution.py:447
  285.9 48.7 %collective-permute-start.58 = (bf16[1024,1024]{1,0:T(8,128)(2,1)}, bf16[1024,1024]{1,0:T(8,128)(2,1)}, u32[]{:S(2)}, u32[]{:S(2)}) collective-permute-start(bf16[1024,1024]{1,0:T(8,128)(2,1)} %bitcast.15), channel_id=1, source_target_pairs={{0,1},{1,0},{2,3},{3,2},{4,5},{5,4},{6,7},{7,6},{8,9},{9,8},{10,11... | collective-permute-start | bytes 6291464 | tf_op jit(solution)/shard_map/ppermute | solution.py:447
  306.6 131.3 %collective-permute-start.56 = (bf16[1024,1024]{1,0:T(8,128)(2,1)}, bf16[1024,1024]{1,0:T(8,128)(2,1)}, u32[]{:S(2)}, u32[]{:S(2)}) collective-permute-start(bf16[1024,1024]{1,0:T(8,128)(2,1)} %bitcast.353), channel_id=1, source_target_pairs={{0,1},{1,0},{2,3},{3,2},{4,5},{5,4},{6,7},{7,6},{8,9},{9,8},{10,11... | collective-permute-start | bytes 6291464 | tf_op jit(solution)/shard_map/ppermute | solution.py:447
  308.1 116.0 %collective-permute-start.57 = (bf16[1024,1024]{1,0:T(8,128)(2,1)}, bf16[1024,1024]{1,0:T(8,128)(2,1)}, u32[]{:S(2)}, u32[]{:S(2)}) collective-permute-start(bf16[1024,1024]{1,0:T(8,128)(2,1)} %bitcast.350), channel_id=1, source_target_pairs={{0,1},{1,0},{2,3},{3,2},{4,5},{5,4},{6,7},{7,6},{8,9},{9,8},{10,11... | collective-permute-start | bytes 6291464 | tf_op jit(solution)/shard_map/ppermute | solution.py:447
  496.9 32.8 %collective-permute-start.77 = (bf16[1024,2048]{1,0:T(8,128)(2,1)}, bf16[1024,2048]{1,0:T(8,128)(2,1)S(1)}, u32[]{:S(2)}, u32[]{:S(2)}) collective-permute-start(bf16[1024,2048]{1,0:T(8,128)(2,1)} %slice.699), channel_id=1, source_target_pairs={{0,2},{2,0},{1,3},{3,1},{4,6},{6,4},{5,7},{7,5},{8,10},{10,8},{9,1... | collective-permute-start | bytes 12582920 | tf_op jit(solution)/shard_map/ppermute | solution.py:447
  510.9 24.9 %collective-permute-start.86 = (f32[8,128]{1,0:T(8,128)S(1)}, f32[8,128]{1,0:T(8,128)S(1)}, u32[]{:S(2)}, u32[]{:S(2)}) collective-permute-start(f32[8,128]{1,0:T(8,128)S(1)} %slice_select_fusion), channel_id=1, source_target_pairs={{0,2},{2,0},{1,3},{3,1},{4,6},{6,4},{5,7},{7,5},{8,10},{10,8},{9,1... | collective-permute-start | bytes 12296 | tf_op jit(solution)/shard_map/ppermute | solution.py:447
  513.9 101.4 %collective-permute-start.59 = (bf16[1024,2048]{1,0:T(8,128)(2,1)}, bf16[1024,2048]{1,0:T(8,128)(2,1)}, u32[]{:S(2)}, u32[]{:S(2)}) collective-permute-start(bf16[1024,2048]{1,0:T(8,128)(2,1)} %slice.686), channel_id=1, source_target_pairs={{0,2},{2,0},{1,3},{3,1},{4,6},{6,4},{5,7},{7,5},{8,10},{10,8},{9,1... | collective-permute-start | bytes 12582920 | tf_op jit(solution)/shard_map/ppermute | solution.py:447
  535.8 40.9 %collective-permute-start.93 = (f32[2,128]{1,0:T(2,128)S(1)}, f32[2,128]{1,0:T(2,128)S(1)}, u32[]{:S(2)}, u32[]{:S(2)}) collective-permute-start(f32[2,128]{1,0:T(2,128)S(1)} %bitcast.342), channel_id=1, source_target_pairs={{0,8},{8,16},{16,24},{24,28},{28,20},{20,12},{12,4},{4,0},{1,9},{9... | collective-permute-start | bytes 3080 | tf_op jit(solution)/shard_map/ppermute | solution.py:454
  587.7 25.5 %collective-permute-start.94 = (bf16[128,2048]{1,0:T(8,128)(2,1)S(1)}, bf16[128,2048]{1,0:T(8,128)(2,1)S(1)}, u32[]{:S(2)}, u32[]{:S(2)}) collective-permute-start(bf16[128,2048]{1,0:T(8,128)(2,1)S(1)} %get-tuple-element.151), channel_id=1, source_target_pairs={{0,4},{8,0},{16,8},{24,16},{28,24},{20,28},{12,20},{4,12},{1,5},{9... | collective-permute-start | bytes 1572872 | tf_op jit(solution)/shard_map/ppermute | solution.py:454
  589.0 24.1 %collective-permute-start.95 = (bf16[128,2048]{1,0:T(8,128)(2,1)S(1)}, bf16[128,2048]{1,0:T(8,128)(2,1)S(1)}, u32[]{:S(2)}, u32[]{:S(2)}) collective-permute-start(bf16[128,2048]{1,0:T(8,128)(2,1)S(1)} %get-tuple-element.151), channel_id=1, source_target_pairs={{0,8},{8,16},{16,24},{24,28},{28,20},{20,12},{12,4},{4,0},{1,9},{9... | collective-permute-start | bytes 1572872 | tf_op jit(solution)/shard_map/ppermute | solution.py:454
  609.4 62.2 %collective-permute-start.142 = (bf16[1024,1024]{1,0:T(8,128)(2,1)S(1)}, bf16[1024,1024]{1,0:T(8,128)(2,1)}, u32[]{:S(2)}, u32[]{:S(2)}) collective-permute-start(bf16[1024,1024]{1,0:T(8,128)(2,1)S(1)} %split.152), channel_id=1, source_target_pairs={{0,1},{1,0},{2,3},{3,2},{4,5},{5,4},{6,7},{7,6},{8,9},{9,8},{10,11... | collective-permute-start | bytes 6291464 | tf_op jit(solution)/shard_map/ppermute | solution.py:447
  611.7 91.4 %collective-permute-start.140 = (bf16[1024,1024]{1,0:T(8,128)(2,1)}, bf16[1024,1024]{1,0:T(8,128)(2,1)}, u32[]{:S(2)}, u32[]{:S(2)}) collective-permute-start(bf16[1024,1024]{1,0:T(8,128)(2,1)} %split.154), channel_id=1, source_target_pairs={{0,1},{1,0},{2,3},{3,2},{4,5},{5,4},{6,7},{7,6},{8,9},{9,8},{10,11... | collective-permute-start | bytes 6291464 | tf_op jit(solution)/shard_map/ppermute | solution.py:447
  630.1 37.2 %collective-permute-start.61 = (bf16[64,2048]{1,0:T(8,128)(2,1)S(1)}, bf16[64,2048]{1,0:T(8,128)(2,1)S(1)}, u32[]{:S(2)}, u32[]{:S(2)}) collective-permute-start(bf16[64,2048]{1,0:T(8,128)(2,1)S(1)} %get-tuple-element.232), channel_id=1, source_target_pairs={{0,4},{8,0},{16,8},{24,16},{28,24},{20,28},{12,20},{4,12},{1,5},{9... | collective-permute-start | bytes 786440 | tf_op jit(solution)/shard_map/ppermute | solution.py:454
  653.8 92.9 %collective-permute-start.102 = (bf16[1024,2048]{1,0:T(8,128)(2,1)}, bf16[1024,2048]{1,0:T(8,128)(2,1)}, u32[]{:S(2)}, u32[]{:S(2)}) collective-permute-start(bf16[1024,2048]{1,0:T(8,128)(2,1)} %get-tuple-element.276), channel_id=1, source_target_pairs={{0,2},{2,0},{1,3},{3,1},{4,6},{6,4},{5,7},{7,5},{8,10},{10,8},{9,1... | collective-permute-start | bytes 12582920 | tf_op jit(solution)/shard_map/ppermute | solution.py:447
  667.4 72.9 %collective-permute-start.141 = (bf16[1024,1024]{1,0:T(8,128)(2,1)}, bf16[1024,1024]{1,0:T(8,128)(2,1)}, u32[]{:S(2)}, u32[]{:S(2)}) collective-permute-start(bf16[1024,1024]{1,0:T(8,128)(2,1)} %split.153), channel_id=1, source_target_pairs={{0,1},{1,0},{2,3},{3,2},{4,5},{5,4},{6,7},{7,6},{8,9},{9,8},{10,11... | collective-permute-start | bytes 6291464 | tf_op jit(solution)/shard_map/ppermute | solution.py:447
  687.3 57.3 %collective-permute-start.64 = (bf16[128,2048]{1,0:T(8,128)(2,1)S(1)}, bf16[128,2048]{1,0:T(8,128)(2,1)S(1)}, u32[]{:S(2)}, u32[]{:S(2)}) collective-permute-start(bf16[128,2048]{1,0:T(8,128)(2,1)S(1)} %get-tuple-element.132), channel_id=1, source_target_pairs={{0,8},{8,16},{16,24},{24,28},{28,20},{20,12},{12,4},{4,0},{1,9},{9... | collective-permute-start | bytes 1572872 | tf_op jit(solution)/shard_map/ppermute | solution.py:454
  688.5 56.2 %collective-permute-start.65 = (bf16[128,2048]{1,0:T(8,128)(2,1)S(1)}, bf16[128,2048]{1,0:T(8,128)(2,1)S(1)}, u32[]{:S(2)}, u32[]{:S(2)}) collective-permute-start(bf16[128,2048]{1,0:T(8,128)(2,1)S(1)} %get-tuple-element.133), channel_id=1, source_target_pairs={{0,4},{8,0},{16,8},{24,16},{28,24},{20,28},{12,20},{4,12},{1,5},{9... | collective-permute-start | bytes 1572872 | tf_op jit(solution)/shard_map/ppermute | solution.py:454
  807.4 137.1 %collective-permute-start.66 = (bf16[128,2048]{1,0:T(8,128)(2,1)}, bf16[128,2048]{1,0:T(8,128)(2,1)}, u32[]{:S(2)}, u32[]{:S(2)}) collective-permute-start(bf16[128,2048]{1,0:T(8,128)(2,1)} %get-tuple-element.134), channel_id=1, source_target_pairs={{0,8},{8,16},{16,24},{24,28},{28,20},{20,12},{12,4},{4,0},{1,9},{9... | collective-permute-start | bytes 1572872 | tf_op jit(solution)/shard_map/ppermute | solution.py:454
  810.8 133.7 %collective-permute-start.67 = (bf16[128,2048]{1,0:T(8,128)(2,1)}, bf16[128,2048]{1,0:T(8,128)(2,1)}, u32[]{:S(2)}, u32[]{:S(2)}) collective-permute-start(bf16[128,2048]{1,0:T(8,128)(2,1)} %get-tuple-element.135), channel_id=1, source_target_pairs={{0,4},{8,0},{16,8},{24,16},{28,24},{20,28},{12,20},{4,12},{1,5},{9... | collective-permute-start | bytes 1572872 | tf_op jit(solution)/shard_map/ppermute | solution.py:454
  811.0 24.5 %collective-permute-start.139 = (f32[2,64]{1,0:T(2,128)S(1)}, f32[2,64]{1,0:T(2,128)S(1)}, u32[]{:S(2)}, u32[]{:S(2)}) collective-permute-start(f32[2,64]{1,0:T(2,128)S(1)} %bitcast.341), channel_id=1, source_target_pairs={{0,1},{1,0},{2,3},{3,2},{4,5},{5,4},{6,7},{7,6},{8,9},{9,8},{10,11... | collective-permute-start | bytes 1544 | tf_op jit(solution)/shard_map/ppermute | solution.py:447
  827.8 42.2 %collective-permute-start.111 = (bf16[1024,2048]{1,0:T(8,128)(2,1)}, bf16[1024,2048]{1,0:T(8,128)(2,1)}, u32[]{:S(2)}, u32[]{:S(2)}) collective-permute-start(bf16[1024,2048]{1,0:T(8,128)(2,1)} %slice.751), channel_id=1, source_target_pairs={{0,2},{2,0},{1,3},{3,1},{4,6},{6,4},{5,7},{7,5},{8,10},{10,8},{9,1... | collective-permute-start | bytes 12582920 | tf_op jit(solution)/shard_map/ppermute | solution.py:447
  (211 other events, 2945.4 us)

commit v2 on v0

--- a/solution.py
+++ b/solution.py
@@ -3,6 +3,9 @@
 import jax
 import jax.numpy as jnp
 from jax import lax
+from jax.experimental import pallas as pl
+from jax.experimental.pallas import tpu as pltpu
+from jax.sharding import Mesh
 from jax.sharding import PartitionSpec as P
 
 HEAD_DIM = 128
@@ -99,7 +102,7 @@
     return (prob_low, dscore)
 
 
-def body(
+def general_body(
     tokens,
     cotangent,
     attn_gain,
@@ -436,44 +439,927 @@
     )
 
 
+RING = [0, 2, 4, 6, 7, 5, 3, 1]
+CHIPS = len(RING)
+FAR = CHIPS // 2
+EXTRA = 8
+PLACES = [1, 7, 2, 6, 3, 5, 0, 4]
+CHUNKS = {1: (0, 2), 2: (2, 2), 3: (4, 2), 0: (6, 1), FAR: (7, 1)}
+
+
+def swap(array, axis):
+    return lax.ppermute(array, axis, [(0, 1), (1, 0)])
+
+
+def shift(array, by):
+    pairs = [(RING[i], RING[(i + by) % CHIPS]) for i in range(CHIPS)]
+    return lax.ppermute(array, "chip", pairs)
+
+
+def fence(*groups):
+    flat = lax.optimization_barrier(tuple(array for group in groups for array in group))
+    out, at = [], 0
+    for group in groups:
+        out.append(list(flat[at : at + len(group)]))
+        at += len(group)
+    return out
+
+
+def open_jobs(carried, jobs):
+    opened = fence(carried, *[list(inputs) for inputs, _ in jobs])
+    return opened[0], [(ins, function) for ins, (_, function) in zip(opened[1:], jobs)]
+
+
+def run_jobs(jobs):
+    return [list(function(*inputs)) for inputs, function in jobs]
+
+
+def ring_gather(arrays, job, jobs=None):
+    cut = arrays[0].shape[0] // 2 // 8 * 8
+    ahead, behind = list(arrays), list(arrays)
+    fresh = [[array] for array in arrays]
+    results = {}
+    for step in range(1, FAR + 1):
+        if step == FAR:
+            ahead, behind = [a[:cut] for a in ahead], [b[cut:] for b in behind]
+        ahead, behind, *fresh = fence(ahead, behind, *fresh)
+        ahead, opened = open_jobs(ahead, (jobs or {}).get(step, []))
+        ahead, behind = [shift(a, 1) for a in ahead], [shift(b, -1) for b in behind]
+        blocks = [[x for block in group for x in (block, swap(block, "core"))] for group in fresh]
+        made, keep = job(step - 1, blocks)
+        done = run_jobs(opened)
+        ahead, behind, made, *done = fence(ahead, behind, list(made), *done)
+        keep(made)
+        results[step] = done
+        fresh = [[b, a] for a, b in zip(ahead, behind)]
+    last = [jnp.concatenate([a, b], axis=0) for a, b in zip(ahead, behind)]
+    made, keep = job(FAR, [[block, swap(block, "core")] for block in last])
+    keep(list(made))
+    return results
+
+
+class Scatter:
+    def __init__(self, make, inputs=()):
+        self.make, self.inputs = make, list(inputs)
+        self.step = 0
+        self.extras = {}
+        (mine, other), self.extras[FAR] = make(FAR, *self.inputs)
+        first = (mine.astype(jnp.float32) + swap(other, "core").astype(jnp.float32)).astype(
+            jnp.bfloat16
+        )
+        self.cut = first.shape[0] // 2 // 8 * 8
+        self.carried = [first[: self.cut], first[self.cut :]]
+
+    def job(self):
+        near = FAR - self.step - 1
+
+        def function(ahead, behind, *inputs):
+            ahead, behind = shift(ahead, 1), shift(behind, -1)
+            terms, extras = self.make(near, *inputs)
+            terms = [t if i % 2 == 0 else swap(t, "core") for i, t in enumerate(terms)]
+            return [ahead, behind, *terms, *extras]
+
+        return self.carried + self.inputs, function
+
+    def take(self, results):
+        self.step += 1
+        near = FAR - self.step
+        ahead, behind, *terms = results
+        count = 4 if near else 2
+        terms, self.extras[near] = terms[:count], terms[count:]
+        terms = [t.astype(jnp.float32) for t in terms]
+        ahead, behind = ahead.astype(jnp.float32), behind.astype(jnp.float32)
+        if near == 0:
+            self.total = terms[0] + terms[1] + ahead + behind
+            return
+        if self.step == 1:
+            ahead = jnp.concatenate([ahead, jnp.zeros_like(behind)], axis=0)
+            behind = jnp.concatenate([jnp.zeros_like(ahead[: self.cut]), behind], axis=0)
+        self.carried = [
+            (terms[0] + terms[1] + ahead).astype(jnp.bfloat16),
+            (terms[2] + terms[3] + behind).astype(jnp.bfloat16),
+        ]
+
+
+def window(scatters, jobs):
+    every = [scatter.job() for scatter in scatters] + list(jobs)
+    _, opened = open_jobs([], every)
+    results = fence(*run_jobs(opened))
+    for scatter, result in zip(scatters, results):
+        scatter.take(result)
+    return results[len(scatters) :]
+
+
+def exchange_all(parts):
+    pair = jnp.stack([parts[:, 0], swap(parts[:, 1], "core")], axis=1)
+    got = {0: pair[0]}
+    for at in range(1, CHIPS):
+        got[CHIPS - at] = shift(pair[at], at)
+    return jnp.stack([got[at] for at in range(CHIPS)], axis=0)
+
+
+def sum_all(values, jobs):
+    (values,), jobs = open_jobs([values], jobs)
+    both = values + swap(values[:, :, ::-1], "core")
+    moved = [shift(both, at) for at in range(1, CHIPS)]
+    done = run_jobs(jobs)
+    moved, *done = fence(moved, *done)
+    total = both
+    for at in range(1, CHIPS):
+        total = total + jnp.roll(moved[at - 1], -at, axis=1)
+    return total, done
+
+
+def by_place(values, axis):
+    return jnp.stack(
+        [lax.index_in_dim(values, PLACES.index(at), axis, False) for at in range(CHIPS)], axis
+    )
+
+
+def by_chunk(values, axis):
+    return jnp.stack([lax.index_in_dim(values, at, axis, False) for at in PLACES], axis)
+
+
+def call(kernel, name, inputs, ins, outs, shapes, earlier=(), grid=(1,), scratch=(), cost=None, mib=56):
+    return pl.pallas_call(
+        kernel,
+        grid=grid,
+        in_specs=ins + [pl.BlockSpec(memory_space=pl.ANY)] * len(earlier),
+        out_specs=outs,
+        out_shape=shapes,
+        scratch_shapes=list(scratch),
+        input_output_aliases={len(ins) + i: i for i in range(len(earlier))},
+        compiler_params=pltpu.CompilerParams(vmem_limit_bytes=mib << 20),
+        cost_estimate=pl.CostEstimate(flops=cost[0], bytes_accessed=cost[1], transcendentals=cost[2]),
+        name=name,
+    )(*inputs, *earlier)
+
+
+def whole(array):
+    return pl.BlockSpec(array.shape, lambda i: (0,) * len(array.shape))
+
+
+def once(array):
+    return pl.BlockSpec(
+        array.shape, lambda i: (0,) * len(array.shape), pipeline_mode=pl.Buffered(1)
+    )
+
+
+def rows_of(step, tok_rows, cols):
+    first, count = CHUNKS[step]
+    index = first // count
+    return pl.BlockSpec((2 * count * tok_rows, cols), lambda i: (index, 0))
+
+
+def lin_chunk(step, blocks, weight, place, tok_rows, earlier):
+    count, width, cols = len(blocks), weight.shape[0], weight.shape[1]
+    length = 2 * CHIPS * tok_rows
+    rows, head = count * tok_rows, weight.shape[1] // 3
+
+    def kernel(*refs):
+        block_refs, weight_ref, place_ref = refs[:count], refs[count], refs[count + 1]
+        lin_ref, all_ref, sum_ref, tag_ref = refs[-4:]
+        lanes = pl.ds(pl.multiple_of(place_ref[0] * tok_rows, tok_rows), tok_rows)
+        for i in range(count):
+            all_ref[i * tok_rows : (i + 1) * tok_rows] = block_refs[i][:tok_rows]
+            levels = block_refs[i][tok_rows:, lanes].astype(jnp.float32)
+            others = block_refs[i][tok_rows:, : 3 * tok_rows].astype(jnp.float32)
+            tag_ref[i * EXTRA : (i + 1) * EXTRA] = jnp.concatenate(
+                [levels[:1]]
+                + [others[1:2, k * tok_rows : (k + 1) * tok_rows] for k in range(3)]
+                + [jnp.zeros((EXTRA - 4, tok_rows), jnp.float32)],
+                axis=0,
+            )
+        lin = product(all_ref[...], weight_ref[...])
+        lin_ref[...] = lin
+        line = lax.broadcasted_iota(jnp.int32, (8, head), 0)
+        total = jnp.zeros((8, rows), jnp.float32)
+        for k in range(2):
+            part = lin[:, k * head : (k + 1) * head]
+            total = total + lax.dot_general(
+                (line == k).astype(jnp.float32),
+                part * part,
+                (((1,), (1,)), ((), ())),
+                precision=lax.Precision.HIGHEST,
+                preferred_element_type=jnp.float32,
+            )
+        sum_ref[...] = total
+
+    tags = jax.ShapeDtypeStruct((count * EXTRA, tok_rows), jnp.float32)
+    sums = jax.ShapeDtypeStruct((8, rows), jnp.float32)
+    return call(
+        kernel,
+        "lin",
+        [*blocks, weight, place],
+        [whole(b) for b in blocks] + [whole(weight), pl.BlockSpec(memory_space=pltpu.SMEM)],
+        [rows_of(step, tok_rows, cols), rows_of(step, tok_rows, width), whole(sums), whole(tags)],
+        [
+            jax.ShapeDtypeStruct((length, cols), jnp.float32),
+            jax.ShapeDtypeStruct((length, width), jnp.bfloat16),
+            sums,
+            tags,
+        ],
+        earlier,
+        cost=(2 * rows * width * cols, 4 * rows * width + 2 * weight.size, 0),
+    )
+
+
+def attend_chunk(step, queries, keys, values, weight, tok_rows, score_scale):
+    count = 2 * CHUNKS[step][1]
+    head, width, length = keys.shape[1], weight.shape[1], keys.shape[0]
+
+    def kernel(q_ref, k_ref, v_ref, w_ref, out_ref, lse_ref, *parts):
+        for i in range(0, count, 2):
+            span = pl.ds(i * tok_rows, 2 * tok_rows)
+            scores = contract_cols(q_ref[span], k_ref[...]) * score_scale
+            row_max = jnp.max(scores, axis=-1, keepdims=True)
+            raw = jnp.exp(scores - row_max)
+            total = jnp.sum(raw, axis=-1, keepdims=True)
+            probs = (raw / total).astype(jnp.bfloat16)
+            mixed = product(probs, v_ref[...]).astype(jnp.bfloat16)
+            out_ref[span] = mixed
+            lse_ref[span] = row_max + jnp.log(total)
+            term = product(mixed, w_ref[...]).astype(jnp.bfloat16)
+            parts[i][...] = term[:tok_rows]
+            parts[i + 1][...] = term[tok_rows:]
+
+    rows = count * tok_rows
+    shapes = [
+        jax.ShapeDtypeStruct((rows, head), jnp.bfloat16),
+        jax.ShapeDtypeStruct((rows, 1), jnp.float32),
+    ] + [jax.ShapeDtypeStruct((tok_rows, width), jnp.bfloat16)] * count
+    return call(
+        kernel,
+        "attend",
+        [queries, keys, values, weight],
+        [rows_of(step, tok_rows, head), whole(keys), whole(values), whole(weight)],
+        [whole(shape) for shape in shapes],
+        shapes,
+        cost=(
+            4 * rows * length * head + 2 * rows * head * width,
+            4 * length * head + 2 * rows * width,
+            rows * length,
+        ),
+    )
+
+
+def attend_back_chunk(
+    step, blocks, queries, lse, keys, values, weight, tok_rows, score_scale, earlier
+):
+    count = len(blocks)
+    length, head = keys.shape
+    width = weight.shape[1]
+    rows = count * tok_rows
+
+    def kernel(*refs):
+        block_refs = refs[:count]
+        q_ref, lse_ref, k_ref, v_ref, w_ref = refs[count : count + 5]
+        dq_ref, all_ref, dk_ref, dv_ref = refs[-4:]
+        for i in range(count):
+            all_ref[i * tok_rows : (i + 1) * tok_rows] = block_refs[i][...]
+        if earlier:
+            dk_in, dv_in = refs[count + 5 : count + 7]
+            dk, dv = dk_in[...], dv_in[...]
+        else:
+            dk, dv = 0.0, 0.0
+        for i in range(0, count, 2):
+            span = pl.ds(i * tok_rows, 2 * tok_rows)
+            queries = q_ref[span]
+            douts = contract_cols(all_ref[span], w_ref[...]).astype(jnp.bfloat16)
+            probs = jnp.exp(contract_cols(queries, k_ref[...]) * score_scale - lse_ref[span])
+            dprobs = contract_cols(douts, v_ref[...])
+            delta = jnp.sum(probs * dprobs, axis=-1, keepdims=True)
+            dscores = (probs * (dprobs - delta)).astype(jnp.bfloat16)
+            dq_ref[span] = product(dscores, k_ref[...]) * score_scale
+            dk = dk + contract_rows(dscores, queries) * score_scale
+            dv = dv + contract_rows(probs.astype(jnp.bfloat16), douts)
+        dk_ref[...] = dk
+        dv_ref[...] = dv
+
+    total = jax.ShapeDtypeStruct((length, head), jnp.float32)
+    inputs = [*blocks, queries, lse, keys, values, weight]
+    ins = [whole(b) for b in blocks] + [
+        rows_of(step, tok_rows, head),
+        rows_of(step, tok_rows, 1),
+        whole(keys),
+        whole(values),
+        whole(weight),
+    ]
+    sums = list(earlier[2:])
+    return pl.pallas_call(
+        kernel,
+        grid=(1,),
+        in_specs=ins
+        + [whole(s) for s in sums]
+        + [pl.BlockSpec(memory_space=pl.ANY)] * len(earlier[:2]),
+        out_specs=[
+            rows_of(step, tok_rows, head),
+            rows_of(step, tok_rows, width),
+            whole(total),
+            whole(total),
+        ],
+        out_shape=[
+            total,
+            jax.ShapeDtypeStruct((length, width), jnp.bfloat16),
+            total,
+            total,
+        ],
+        input_output_aliases={
+            len(ins): 2,
+            len(ins) + 1: 3,
+            len(ins) + 2: 0,
+            len(ins) + 3: 1,
+        }
+        if earlier
+        else {},
+        compiler_params=pltpu.CompilerParams(vmem_limit_bytes=56 << 20),
+        cost_estimate=pl.CostEstimate(
+            flops=10 * rows * length * head + 2 * rows * head * width,
+            bytes_accessed=16 * length * head + 4 * rows * width,
+            transcendentals=rows * length,
+        ),
+        name="attend_back",
+    )(*inputs, *sums, *earlier[:2])
+
+
+EXPERT_COLS = 256
+
+
+def expert_chunk(step, h_blocks, g_blocks, place, kept, router, gate, up, down, tok_rows, earlier):
+    count = len(h_blocks)
+    width, hidden = gate.shape
+    cols = EXPERT_COLS
+    rows = count * tok_rows
+    length = 2 * CHIPS * tok_rows
+    low = jnp.bfloat16
+    first, places = CHUNKS[step]
+    index = first // places
+
+    def kernel(*refs):
+        h_refs, g_refs = refs[:count], refs[count : 2 * count]
+        place_ref, kept_ref, router_ref, gate_ref, up_ref, down_ref = refs[
+            2 * count : 2 * count + 6
+        ]
+        outs = refs[-(2 * count + 9) : -4]
+        act_ref, dgate_ref, dup_ref, h_all, g_all = outs[:5]
+        mix_refs, dx_refs = outs[5 : 5 + count], outs[5 + count :]
+        mix_sum, dx_sum, share_ref, dshare_ref = refs[-4:]
+        turn = pl.program_id(0)
+        last = pl.num_programs(0) - 1
+
+        @pl.when(turn == 0)
+        def _():
+            for i in range(count):
+                h_all[i * tok_rows : (i + 1) * tok_rows] = h_refs[i][...]
+                g_all[i * tok_rows : (i + 1) * tok_rows] = g_refs[i][...]
+            logits = contract_cols(h_all[...], router_ref[...])
+            raw = jnp.exp(logits - jnp.max(logits, axis=-1, keepdims=True))
+            probs = raw / jnp.sum(raw, axis=-1, keepdims=True)
+            lanes = lax.broadcasted_iota(jnp.int32, probs.shape, 1)
+            chosen = jnp.sum(
+                jnp.where(lanes == place_ref[0], probs, 0.0), axis=-1, keepdims=True
+            )
+            share_ref[...] = chosen * kept_ref[...]
+
+        hidden_rows, grads, share = h_all[...], g_all[...], share_ref[...]
+        gate_lin = product(hidden_rows, gate_ref[...])
+        up_lin = product(hidden_rows, up_ref[...])
+        back = contract_cols(grads, down_ref[...])
+        sig = jax.nn.sigmoid(gate_lin)
+        silu = gate_lin * sig
+        act = silu * up_lin
+        dshare = jnp.sum(act * back, axis=-1, keepdims=True)
+        act_low = (act * share).astype(low)
+        back = back * share
+        dgate = (back * up_lin * (sig * (1.0 + gate_lin * (1.0 - sig)))).astype(low)
+        dup = (back * silu).astype(low)
+        act_ref[...] = act_low
+        dgate_ref[...] = dgate
+        dup_ref[...] = dup
+        mix = product(act_low, down_ref[...])
+        dx = contract_cols(dgate, gate_ref[...]) + contract_cols(dup, up_ref[...])
+
+        @pl.when(turn == 0)
+        def _():
+            dshare_ref[...] = dshare
+            mix_sum[...] = mix
+            dx_sum[...] = dx
+
+        @pl.when((turn > 0) & (turn < last))
+        def _():
+            dshare_ref[...] += dshare
+            mix_sum[...] += mix
+            dx_sum[...] += dx
+
+        @pl.when(turn == last)
+        def _():
+            mix_low = (mix_sum[...] + mix).astype(low)
+            dx_low = (dx_sum[...] + dx).astype(low)
+            total = (dshare_ref[...] + dshare) * kept_ref[...]
+            same = lax.broadcasted_iota(jnp.int32, (tok_rows, tok_rows), 0) == (
+                lax.broadcasted_iota(jnp.int32, (tok_rows, tok_rows), 1)
+            )
+            lanes = pl.ds(pl.multiple_of(place_ref[0] * tok_rows, tok_rows), tok_rows)
+            for i in range(count):
+                span = slice(i * tok_rows, (i + 1) * tok_rows)
+                mix_refs[i][...] = mix_low[span]
+                dx_refs[i][:tok_rows] = dx_low[span]
+                line = jnp.sum(jnp.where(same, total[span], 0.0), axis=0, keepdims=True)
+                pieces, rest = [], line
+                for _ in range(3):
+                    piece = rest.astype(low)
+                    rest = rest - piece.astype(jnp.float32)
+                    pieces.append(piece.astype(jnp.float32))
+                pieces.append(jnp.zeros((EXTRA - 3, tok_rows), jnp.float32))
+                dx_refs[i][tok_rows:] = jnp.zeros((EXTRA, width), low)
+                dx_refs[i][tok_rows:, lanes] = jnp.concatenate(pieces, axis=0).astype(low)
+
+    tile = pl.BlockSpec((rows, cols), lambda j: (index, j))
+    all_rows = pl.BlockSpec((rows, width), lambda j: (index, 0))
+    wide = jax.ShapeDtypeStruct((length, hidden), low)
+    full = jax.ShapeDtypeStruct((length, width), low)
+    block = jax.ShapeDtypeStruct((tok_rows, width), low)
+    longer = jax.ShapeDtypeStruct((tok_rows + EXTRA, width), low)
+    return call(
+        kernel,
+        "expert",
+        [*h_blocks, *g_blocks, place, kept, router, gate, up, down],
+        [once(b) for b in [*h_blocks, *g_blocks]]
+        + [
+            pl.BlockSpec(memory_space=pltpu.SMEM),
+            pl.BlockSpec((rows, 1), lambda j: (index, 0)),
+            whole(router),
+            pl.BlockSpec((width, cols), lambda j: (0, j)),
+            pl.BlockSpec((width, cols), lambda j: (0, j)),
+            pl.BlockSpec((cols, width), lambda j: (j, 0)),
+        ],
+        [tile] * 3 + [all_rows] * 2 + [whole(block)] * count + [whole(longer)] * count,
+        [wide] * 3 + [full] * 2 + [block] * count + [longer] * count,
+        earlier,
+        grid=(hidden // cols,),
+        scratch=[pltpu.VMEM((rows, width), jnp.float32)] * 2
+        + [pltpu.VMEM((rows, 1), jnp.float32)] * 2,
+        cost=(
+            12 * rows * width * hidden,
+            6 * width * hidden + 12 * rows * width,
+            2 * rows * hidden,
+        ),
+        mib=60,
+    )
+
+
+def body(
+    tokens,
+    cotangent,
+    attn_gain,
+    w_query,
+    w_key,
+    w_value,
+    w_out,
+    query_gain,
+    key_gain,
+    ffn_gain,
+    router,
+    w_gate,
+    w_up,
+    w_down,
+    routes,
+    priority,
+    positions,
+):
+    low = jnp.bfloat16
+    ctx_count = 2 * CHIPS
+    place = lax.axis_index("chip") * 2 + lax.axis_index("core")
+    part = lax.axis_index("fsdp")
+    tok_rows, model_width = tokens.shape[1:]
+    half_width = model_width // 2
+    head_dim = HEAD_DIM
+    length = tok_rows * ctx_count
+    capacity = 9 * tok_rows
+    score_scale = head_dim ** (-0.5)
+    per_half = ctx_count // 2
+    expert_count = router.shape[1]
+
+    def joined(mine, other, axis):
+        return jnp.where(
+            part == 0,
+            jnp.concatenate([mine, other], axis=axis),
+            jnp.concatenate([other, mine], axis=axis),
+        )
+
+    def head_rows(matrix, width):
+        return lax.dynamic_slice_in_dim(matrix, (place % per_half) * width, width, 0)
+
+    small = jnp.concatenate(
+        [
+            router.T,
+            attn_gain[None],
+            ffn_gain[None],
+            jnp.concatenate(
+                [
+                    head_rows(query_gain, head_dim),
+                    head_rows(key_gain, head_dim),
+                    jnp.zeros((half_width - 2 * head_dim,), low),
+                ]
+            )[None],
+        ],
+        axis=0,
+    )
+    small_other = swap(small, "fsdp")
+    small_full = joined(small, small_other, 1)
+    r_weight = small_full[:expert_count]
+    g_attn = small_full[expert_count].astype(jnp.float32)
+    g_ffn = small_full[expert_count + 1].astype(jnp.float32)
+    here = part == place // per_half
+    g_heads = jnp.where(here, small[expert_count + 2], small_other[expert_count + 2]).astype(
+        jnp.float32
+    )
+    g_query, g_key = g_heads[:head_dim], g_heads[head_dim : 2 * head_dim]
+    qkv_mine = jnp.concatenate(
+        [
+            lax.dynamic_slice_in_dim(w, place * head_dim, head_dim, 1)
+            for w in (w_query, w_key, w_value)
+        ],
+        axis=1,
+    )
+    qkv_other = swap(qkv_mine, "fsdp")
+    qkv_weight = joined(qkv_mine, qkv_other, 0)
+    out_mine = head_rows(w_out, head_dim)
+    out_weight = jnp.where(here, out_mine, swap(out_mine, "fsdp"))
+    gate_weight = lax.all_gather(w_gate[0], "fsdp", axis=0, tiled=True)
+    up_weight = lax.all_gather(w_up[0], "fsdp", axis=0, tiled=True)
+    down_weight = lax.all_gather(w_down[0], "fsdp", axis=1, tiled=True)
+
+    hot = routes[0][:, :, None] == jnp.arange(expert_count, dtype=jnp.int32)[None, None, :]
+    levels = jnp.sum(jnp.where(hot, priority[0][:, :, None] - LEVELS, 0), axis=1) + LEVELS
+    spot = positions[0]
+    line = jnp.concatenate(
+        [spot // 128, spot % 128, jnp.full((model_width - 2 * tok_rows,), place, jnp.int32)]
+    )
+    tags = jnp.concatenate(
+        [
+            levels.T.reshape(1, model_width),
+            line[None],
+            jnp.zeros((EXTRA - 2, model_width), jnp.int32),
+        ],
+        axis=0,
+    ).astype(low)
+
+    inputs = tokens[0].astype(jnp.float32)
+    normed, inv_one = rms_forward(inputs, g_attn)
+    place_one = place.astype(jnp.int32).reshape(1)
+    ready = ()
+    sum_parts, tag_parts, rope_parts = {}, {}, {}
+
+    def lin_job(step, blocks):
+        made = lin_chunk(step, blocks[0], qkv_weight, place_one, tok_rows, ready)
+        lines = made[3].reshape(-1, EXTRA, tok_rows)
+        spots = (lines[:, 1] * 128.0 + lines[:, 2]).reshape(-1)
+        cosine, sine_part = rope_tables(spots, head_dim)
+        cosine, sine_part = cosine[:, 0], sine_part[:, 0]
+        tables = [
+            jnp.concatenate([cosine, cosine], axis=-1),
+            jnp.concatenate([-sine_part, sine_part], axis=-1),
+        ]
+
+        def keep(made):
+            nonlocal ready
+            ready = tuple(made[:2])
+            sum_parts[step], tag_parts[step] = made[2][:2], made[3]
+            rope_parts[step] = made[4:]
+
+        return [*made, *tables], keep
+
+    ring_gather([jnp.concatenate([normed.astype(low), tags], axis=0)], lin_job)
+    lin, all_h_one = ready
+    q_lin, k_lin, v_lin = jnp.split(lin, 3, axis=1)
+    cos_full, sin_full = (
+        jnp.concatenate([rope_parts[step][k] for step in CHUNKS], axis=0) for k in range(2)
+    )
+    all_tags = jnp.concatenate([tag_parts[step] for step in CHUNKS], axis=0).reshape(
+        ctx_count, EXTRA, tok_rows
+    )
+
+    def token_sums(lines, jobs):
+        total, done = sum_all(by_place(lines.reshape(-1, CHIPS, 2, tok_rows), 1), jobs)
+        return by_chunk(total, 1).reshape(-1, length, 1) / model_width, done
+
+    def rank_job(all_tags):
+        mine, owner = all_tags[:, 0], all_tags[:, 3, :1]
+        order = owner * tok_rows + jnp.arange(tok_rows, dtype=jnp.float32)[None]
+        mine = mine.reshape(length)
+        code = mine * length + order.reshape(length)
+        ranks = jnp.sum((code[None, :] < code[:, None]).astype(jnp.float32), axis=1)
+        kept = (mine < LEVELS) & (ranks < capacity)
+        return kept.astype(jnp.float32)[:, None], owner[:, 0].astype(jnp.int32)
+
+    square, _ = token_sums(
+        jnp.concatenate([sum_parts[step] for step in CHUNKS], axis=1),
+        [],
+    )
+    inv_query, inv_key = lax.rsqrt(square[0] + epsilon), lax.rsqrt(square[1] + epsilon)
+
+    def spin(matrix):
+        return jnp.concatenate([matrix[:, head_dim // 2 :], matrix[:, : head_dim // 2]], axis=-1)
+
+    q_normed = q_lin * inv_query * g_query
+    k_normed = k_lin * inv_key * g_key
+    q_rot = (q_normed * cos_full + spin(q_normed) * sin_full).astype(low)
+    k_rot = (k_normed * cos_full + spin(k_normed) * sin_full).astype(low)
+    v_low = v_lin.astype(low)
+
+    def attend_terms(step, queries, keys, values):
+        mixed, lse, *terms = attend_chunk(
+            step, queries, keys, values, out_weight, tok_rows, score_scale
+        )
+        return terms, [mixed, lse]
+
+    out_sum = Scatter(attend_terms, [q_rot, k_rot, v_low])
+    ((kept, owners),) = window([out_sum], [([all_tags], rank_job)])
+    for _ in range(FAR - 1):
+        window([out_sum], [])
+    mixed_low, lse = (
+        jnp.concatenate([out_sum.extras[step][k] for step in CHUNKS], axis=0) for k in range(2)
+    )
+    projected = out_sum.total
+    middle = inputs + projected
+
+    h_two_f, inv_two = rms_forward(middle, g_ffn)
+    h_two = h_two_f.astype(low)
+    grad_out = cotangent[0].astype(jnp.float32)
+    filled = ()
+    mix_terms, dx_terms = {}, {}
+
+    def expert_job(step, blocks):
+        made = expert_chunk(
+            step,
+            blocks[0],
+            blocks[1],
+            place_one,
+            kept,
+            r_weight,
+            gate_weight,
+            up_weight,
+            down_weight,
+            tok_rows,
+            filled,
+        )
+
+        def keep(made):
+            nonlocal filled
+            filled, terms = tuple(made[:5]), made[5:]
+            half = len(terms) // 2
+            mix_terms[step], dx_terms[step] = terms[:half], terms[half:]
+
+        return made, keep
+
+    ring_gather([h_two, cotangent[0]], expert_job)
+    act_low, gate_grad, up_grad, all_h_two, all_grads = filled
+
+    def wgrad(left, right):
+        return (contract_rows(left, right).astype(low),)
+
+    logits = contract_cols(h_two, r_weight)
+    row_max = jnp.max(logits, axis=-1, keepdims=True)
+    exps_raw = jnp.exp(logits - row_max)
+    router_probs = exps_raw / jnp.sum(exps_raw, axis=-1, keepdims=True)
+    dx_sum = Scatter(lambda step: (dx_terms[step], []))
+    mix_sum = Scatter(lambda step: (mix_terms[step], []))
+    ((gate_wgrad,),) = window([dx_sum, mix_sum], [([all_h_two, gate_grad], wgrad)])
+    ((up_wgrad,),) = window([dx_sum, mix_sum], [([all_h_two, up_grad], wgrad)])
+    window([dx_sum], [])
+    window([dx_sum], [])
+    hidden_sum = dx_sum.total
+
+    def over_sequences(matrix, axis):
+        return lax.psum_scatter(matrix, "fsdp", scatter_dimension=axis, tiled=True)
+
+    sums = [over_sequences(gate_wgrad, 0), over_sequences(up_wgrad, 0)]
+
+    prob_grad = jnp.sum(hidden_sum[tok_rows : tok_rows + 3], axis=0)
+    prob_grad = prob_grad.reshape(expert_count, tok_rows).T
+    logit_grad = router_probs * (
+        prob_grad - jnp.sum(router_probs * prob_grad, axis=-1, keepdims=True)
+    )
+    hidden_grad = hidden_sum[:tok_rows] + precise(logit_grad, r_weight.astype(jnp.float32))
+    norm_grad, ffn_gain_grad = rms_backward(middle, inv_two, g_ffn, hidden_grad)
+    middle_grad = grad_out + norm_grad
+
+    sofar = ()
+
+    def back_job(step, blocks):
+        made = attend_back_chunk(
+            step,
+            blocks[0],
+            q_rot,
+            lse,
+            k_rot,
+            v_low,
+            out_weight,
+            tok_rows,
+            score_scale,
+            sofar,
+        )
+
+        def keep(made):
+            nonlocal sofar
+            sofar = tuple(made)
+
+        return made, keep
+
+    mix_step = mix_sum.job()
+    done = ring_gather(
+        [middle_grad.astype(low)],
+        back_job,
+        {2: [mix_step], 4: [([act_low, all_grads], wgrad)]},
+    )
+    mix_sum.take(done[2][0])
+    down_wgrad = done[4][0][0]
+    sums.append(over_sequences(down_wgrad, 1))
+    dq, all_branch, dk, dv = sofar
+    q_back = dq * cos_full - spin(dq) * sin_full
+    k_back = dk * cos_full - spin(dk) * sin_full
+
+    def out_job(mixed_low, all_branch):
+        return (contract_rows(mixed_low, all_branch),)
+
+    def router_job(h_two, logit_grad):
+        return (precise(h_two.astype(jnp.float32).T, logit_grad),)
+
+    along, ((out_wgrad,), (router_wgrad,), mixed) = token_sums(
+        jnp.stack(
+            [
+                jnp.sum(q_back * g_query * q_lin, axis=-1),
+                jnp.sum(k_back * g_key * k_lin, axis=-1),
+            ],
+            axis=0,
+        ),
+        [
+            ([mixed_low, all_branch], out_job),
+            ([h_two, logit_grad], router_job),
+            mix_sum.job(),
+        ],
+    )
+    mix_sum.take(mixed)
+    layer_out = (middle + mix_sum.total).astype(low)
+    q_lin_grad = inv_query * (q_back * g_query) - q_lin * inv_query**3 * along[0]
+    k_lin_grad = inv_key * (k_back * g_key) - k_lin * inv_key**3 * along[1]
+    query_gain_grad = jnp.sum(q_back * q_lin * inv_query, axis=0)
+    key_gain_grad = jnp.sum(k_back * k_lin * inv_key, axis=0)
+    lin_grad = jnp.concatenate([q_lin_grad, k_lin_grad, dv], axis=1).astype(low)
+
+    own_rows = model_width // (2 * ctx_count)
+
+    def pick(blocks, index):
+        return lax.dynamic_index_in_dim(blocks, index, 1, False)
+
+    def split_low(values):
+        high = values.astype(low)
+        return jnp.concatenate([high, (values - high.astype(jnp.float32)).astype(low)], axis=-1)
+
+    wide_cols = 3 * head_dim
+    thin_cols = expert_count + 2
+    source_ids = by_place(owners.reshape(CHIPS, 2), 0)
+
+    def dense_job(all_h_one, lin_grad, router_wgrad, ffn_gain_grad):
+        wgrad = contract_rows(all_h_one, lin_grad)
+        attn_term = jnp.sum(wgrad * qkv_weight.astype(jnp.float32), axis=1) / g_attn
+        thin = jnp.concatenate(
+            [router_wgrad, ffn_gain_grad[:, None], attn_term[:, None]], axis=1
+        )
+
+        def by_owner(matrix):
+            return matrix.reshape(ctx_count, 2, own_rows, -1)
+
+        wide, thin = by_owner(wgrad), by_owner(thin)
+        sent = jnp.concatenate(
+            [pick(wide, 1 - part).astype(low), split_low(pick(thin, 1 - part))], axis=-1
+        )
+        return sent, pick(wide, part), pick(thin, part)
+
+    def pair_job(sent, wide, thin):
+        got = swap(sent, "fsdp").astype(jnp.float32)
+        wide = wide + got[..., :wide_cols]
+        thin = thin + (
+            got[..., wide_cols : wide_cols + thin_cols] + got[..., wide_cols + thin_cols :]
+        )
+        payload = jnp.concatenate([wide.astype(low), split_low(thin)], axis=-1)
+        return (payload[source_ids],)
+
+    out_rows = out_wgrad.reshape(1, 2, own_rows, model_width)
+    d_out = pick(out_rows, part)[0] + swap(pick(out_rows, 1 - part)[0].astype(low), "fsdp").astype(
+        jnp.float32
+    )
+    gain_rows = jnp.stack([query_gain_grad, key_gain_grad], axis=0).reshape(2, 2, own_rows)
+    gain_rows = pick(gain_rows, part) + swap(pick(gain_rows, 1 - part), "fsdp")
+    d_qgain, d_kgain = gain_rows[0], gain_rows[1]
+
+    def h_terms(step, lin_grad):
+        first, count = CHUNKS[step]
+        rows = lin_grad[2 * first * tok_rows : 2 * (first + count) * tok_rows]
+        term = contract_cols(rows, qkv_weight).astype(low)
+        return [term[k * tok_rows : (k + 1) * tok_rows] for k in range(2 * count)], []
+
+    h_sum = Scatter(h_terms, [lin_grad])
+    (made,) = window(
+        [h_sum], [([all_h_one, lin_grad, router_wgrad, ffn_gain_grad], dense_job)]
+    )
+    ((payload,),) = window([h_sum], [(made, pair_job)])
+    (sums,) = window(
+        [h_sum], [(sums, lambda *sums: [total.astype(jnp.float32) for total in sums])]
+    )
+    received = exchange_all(payload)
+    window([h_sum], [])
+    h_grad = h_sum.total
+    s_gate, s_up, s_down = (total[None] for total in sums)
+    in_norm_grad, _ = rms_backward(inputs, inv_one, g_attn, h_grad)
+    input_grad = (middle_grad + in_norm_grad).astype(low)
+    received = received.reshape(ctx_count, own_rows, -1)
+    here_order = (
+        source_ids.reshape(1, -1) == jnp.arange(ctx_count, dtype=jnp.int32)[:, None]
+    ).astype(jnp.int32)
+    back_ids = jnp.sum(here_order * jnp.arange(ctx_count, dtype=jnp.int32)[None, :], axis=1)
+    dense = received[..., :wide_cols][back_ids].astype(jnp.float32)
+    dense = dense.reshape(ctx_count, own_rows, 3, head_dim)
+    d_query, d_key, d_value = (
+        dense[:, :, i].transpose(1, 0, 2).reshape(own_rows, model_width) for i in range(3)
+    )
+    thin_sum = jnp.sum(received[..., wide_cols:].astype(jnp.float32), axis=0)
+    thin_sum = thin_sum[:, :thin_cols] + thin_sum[:, thin_cols:]
+    d_router = thin_sum[:, :expert_count]
+    d_ffn, d_attn = thin_sum[:, expert_count], thin_sum[:, expert_count + 1]
+    return (
+        layer_out[None],
+        input_grad[None],
+        d_attn,
+        d_query,
+        d_key,
+        d_value,
+        d_out,
+        d_qgain,
+        d_kgain,
+        d_ffn,
+        d_router,
+        s_gate,
+        s_up,
+        s_down,
+    )
+
+
+def specs_of(ctx):
+    rows, both = P("fsdp", ctx, None), ctx + ("fsdp",)
+    dense = P("fsdp", None)
+    ins = (
+        rows,
+        rows,
+        P("fsdp"),
+        dense,
+        dense,
+        dense,
+        dense,
+        P("fsdp"),
+        P("fsdp"),
+        P("fsdp"),
+        dense,
+        P(ctx, "fsdp", None),
+        P(ctx, "fsdp", None),
+        P(ctx, None, "fsdp"),
+        rows,
+        rows,
+        P("fsdp", ctx),
+    )
+    line, matrix = P(both), P(both, None)
+    outs = (
+        rows,
+        rows,
+        line,
+        matrix,
+        matrix,
+        matrix,
+        matrix,
+        line,
+        line,
+        line,
+        matrix,
+        P(ctx, "fsdp", None),
+        P(ctx, "fsdp", None),
+        P(ctx, None, "fsdp"),
+    )
+    return ins, outs
+
+
 def solution(mesh):
-    return jax.shard_map(
-        body,
-        mesh=mesh,
-        in_specs=(
-            P("fsdp", "ctx", None),
-            P("fsdp", "ctx", None),
-            P("fsdp"),
-            P("fsdp", None),
-            P("fsdp", None),
-            P("fsdp", None),
-            P("fsdp", None),
-            P("fsdp"),
-            P("fsdp"),
-            P("fsdp"),
-            P("fsdp", None),
-            P("ctx", "fsdp", None),
-            P("ctx", "fsdp", None),
-            P("ctx", None, "fsdp"),
-            P("fsdp", "ctx", None),
-            P("fsdp", "ctx", None),
-            P("fsdp", "ctx"),
-        ),
-        out_specs=(
-            P("fsdp", "ctx", None),
-            P("fsdp", "ctx", None),
-            P(("ctx", "fsdp")),
-            P(("ctx", "fsdp"), None),
-            P(("ctx", "fsdp"), None),
-            P(("ctx", "fsdp"), None),
-            P(("ctx", "fsdp"), None),
-            P(("ctx", "fsdp")),
-            P(("ctx", "fsdp")),
-            P(("ctx", "fsdp")),
-            P(("ctx", "fsdp"), None),
-            P("ctx", "fsdp", None),
-            P("ctx", "fsdp", None),
-            P("ctx", None, "fsdp"),
-        ),
-        check_vma=False,
-    )
+    ctx_count, fsdp_count = mesh.shape["ctx"], mesh.shape["fsdp"]
+
+    def whole(*arrays):
+        heads = arrays[0].shape[2] // HEAD_DIM
+        experts = arrays[10].shape[1]
+        if ctx_count == 2 * CHIPS == heads == experts and fsdp_count == 2:
+            chips = Mesh(mesh.devices.reshape(-1, 2, 2), ("chip", "core", "fsdp"))
+            run, grid, ctx = body, chips, ("chip", "core")
+        else:
+            run, grid, ctx = general_body, mesh, ("ctx",)
+        ins, outs = specs_of(ctx)
+        return jax.shard_map(run, mesh=grid, in_specs=ins, out_specs=outs, check_vma=False)(*arrays)
+
+    return whole

time: 3810 us -> 782 us (0.21)
  waiting for transfers between devices: 2850 us -> 169 us
  blocking collectives: 280 us -> 0 us
  local copies, waits for them, and re-layouts: 338 us -> 91.6 us
  Pallas kernels: 0 us -> 192 us
  matrix products: 225 us -> 65.9 us
  starting transfers between devices: 32 us -> 131 us
  other arithmetic: 54 us -> 105 us
    reduce_scatter x8 -> x3, waiting for transfers between devices: 1840 us -> 0.01 us  [over_sequences(): return lax.psum_scatter(matrix, 'fsdp', scatter_dimension=axis, tiled=True)]
    all_to_all x4 -> x0, waiting for transfers between devices: 523 us -> none  [the longest x1 177 us: body(): lax.all_to_all(back_grads, 'ctx', split_axis=0, concat_axis=0, tiled=True)]
    all_gather x9 -> x3, waiting for transfers between devices: 408 us -> 10.3 us  [the longest x1 10.3 us: body(): down_weight = lax.all_gather(w_down[0], 'fsdp', axis=1, tiled=True)]
    pallas_call x0 -> x20, Pallas kernels: none -> 192 us  [the longest x15 155 us: call(): pl.pallas_call(kernel, grid=grid, in_specs=ins + [pl.BlockSpec(memory_spa...]
    all_to_all x1 -> x0, blocking collectives: 189 us -> none  [body(): lax.all_to_all(send_grads, 'ctx', split_axis=0, concat_axis=0, tiled=True)]
    ppermute x0 -> x158, waiting for transfers between devices: none -> 158 us  [the longest x85 92 us: shift(): return lax.ppermute(array, 'chip', pairs)]
    gather x9 -> x2, local copies, waits for them, and re-layouts: 146 us -> 2.61 us  [the longest x1 1.9 us: pair_job(): return (payload[source_ids],)]
    ppermute x0 -> x158, starting transfers between devices: none -> 130 us  [the longest x85 109 us: shift(): return lax.ppermute(array, 'chip', pairs)]
  transfers between devices with their start and end apart: 22 -> 164, of which waited for: 17 -> 46; matrix products, arithmetic and copies ran while one was open for 8% -> 30% of each run, Pallas kernels for 0% -> 23%
where the time goes in v2:
time: 782 us; the launch traced here: 771 us
  Pallas kernels  192 us (25%)
  waiting for transfers between devices  169 us (22%)
  starting transfers between devices  131 us (17%)
  other arithmetic  105 us (13%)
  local copies, waits for them, and re-layouts  91.6 us (12%)
  matrix products  65.9 us (8%)
  between operations  17.5 us (2%)
    pallas_call x15, Pallas kernels, call(): pl.pallas_call(kernel, grid=grid, in_specs=ins + [pl.BlockSpec(memory_spa...  155 us
    ppermute x85, starting transfers between devices, shift(): return lax.ppermute(array, 'chip', pairs)  109 us
    ppermute x85, waiting for transfers between devices, shift(): return lax.ppermute(array, 'chip', pairs)  92 us
    ppermute x73, waiting for transfers between devices, swap(): return lax.ppermute(array, axis, [(0, 1), (1, 0)])  65.8 us
    dot_general x5, matrix products, contract_rows(): lax.dot_general(left, right, (((0,), (0,)), ((), ())), preferred_element_...  55.7 us
    pallas_call x5, Pallas kernels, attend_back_chunk(): pl.pallas_call(kernel, grid=(1,), in_specs=ins + [whole(s) for s in sums]...  36.5 us
    unnamed x386, local copies, waits for them, and re-layouts  28.5 us
    convert_element_type x12, other arithmetic, take(): (terms[0] + terms[1] + ahead).astype(jnp.bfloat16)  23.1 us
  transfers between devices with their start and end apart: 164, of which 46 were waited for; matrix products, arithmetic and copies ran while one was open for 30% of the time, Pallas kernels for 23%

profile of v2, /device:TPU:8, one launch (start us, length us, event | category | flops | bytes accessed | tf_op | source)
XLA Modules:
  0.0 770.8 jit_solution(6511959555103105339)
XLA Ops:
  20.8 24.9 %collective-permute-done.4 = bf16[1024,384]{1,0:T(8,128)(2,1)} collective-permute-done((bf16[1024,384]{1,0:T(8,128)(2,1)S(1)}, bf16[1024,384]{1,0:T(8,128)(2,1)}, u32[]{:S(2)}, u32[]{:S(2)}) %collective-permute-start.4) | collective-permute-done | bytes 786464 | tf_op jit(solution)/shard_map/ppermute | solution.py:451
  158.7 5.8 collective-permute-done.32
  191.0 5.7 collective-permute-done.40
  205.3 10.3 %all-gather.11.cloned.1.call-done = bf16[1,1024,2048]{2,1,0:T(8,128)(2,1)} async-done(((bf16[1,1024,1024]{2,1,0:T(8,128)(2,1)}), bf16[1,1024,2048]{2,1,0:T(8,128)(2,1)}) %all-gather.11.cloned.1.call-update) | async-done | bytes 4194320 | tf_op jit(solution)/shard_map/all_gather | solution.py:991
  215.6 15.4 %expert.5 = (bf16[2048,1024]{1,0:T(8,128)(2,1)}, bf16[2048,1024]{1,0:T(8,128)(2,1)}, bf16[2048,1024]{1,0:T(8,128)(2,1)}, bf16[2048,2048]{1,0:T(8,128)(2,1)}, bf1...) custom-call(bf16[128,2048]{1,0:T(8,128)(2,1)} %copy-done.16, ...), custom_call_target="tpu_custom_call" | custom-call | flops 6442450944 | bytes 18874368 | tf_op jit(solution)/shard_map/expert/pallas_call | solution.py:584
  236.9 26.1 %expert.6 = (bf16[2048,1024]{1,0:T(8,128)(2,1)}, bf16[2048,1024]{1,0:T(8,128)(2,1)}, bf16[2048,1024]{1,0:T(8,128)(2,1)}, bf16[2048,2048]{1,0:T(8,128)(2,1)}, bf1...) custom-call(bf16[128,2048]{1,0:T(8,128)(2,1)} %collective-permute-do, ...), custom_call_target="tpu_custom_call", output_to_operand_aliasing={{0}: (14, {}), {1}: (15, {}), {2}: (16, {}), {3}: (17, {}),... | custom-call | flops 12884901888 | bytes 25165824 | tf_op jit(solution)/shard_map/expert/pallas_call | solution.py:584
  271.5 26.1 %expert.7 = (bf16[2048,1024]{1,0:T(8,128)(2,1)}, bf16[2048,1024]{1,0:T(8,128)(2,1)}, bf16[2048,1024]{1,0:T(8,128)(2,1)}, bf16[2048,2048]{1,0:T(8,128)(2,1)}, bf1...) custom-call(bf16[128,2048]{1,0:T(8,128)(2,1)} %copy-done.152, ...), custom_call_target="tpu_custom_call", output_to_operand_aliasing={{0}: (14, {}), {1}: (15, {}), {2}: (16, {}), {3}: (17, {}),... | custom-call | flops 12884901888 | bytes 25165824 | tf_op jit(solution)/shard_map/expert/pallas_call | solution.py:584
  306.4 26.1 %expert.8 = (bf16[2048,1024]{1,0:T(8,128)(2,1)}, bf16[2048,1024]{1,0:T(8,128)(2,1)}, bf16[2048,1024]{1,0:T(8,128)(2,1)}, bf16[2048,2048]{1,0:T(8,128)(2,1)}, bf1...) custom-call(bf16[128,2048]{1,0:T(8,128)(2,1)} %copy-done.99, ...), custom_call_target="tpu_custom_call", output_to_operand_aliasing={{0}: (14, {}), {1}: (15, {}), {2}: (16, {}), {3}: (17, {}),... | custom-call | flops 12884901888 | bytes 25165824 | tf_op jit(solution)/shard_map/expert/pallas_call | solution.py:584
  336.2 15.4 %expert.9 = (bf16[2048,1024]{1,0:T(8,128)(2,1)}, bf16[2048,1024]{1,0:T(8,128)(2,1)}, bf16[2048,1024]{1,0:T(8,128)(2,1)}, bf16[2048,2048]{1,0:T(8,128)(2,1)}, bf1...) custom-call(bf16[128,2048]{1,0:T(8,128)(2,1)} %copy-done.40, ...), custom_call_target="tpu_custom_call", output_to_operand_aliasing={{0}: (10, {}), {1}: (11, {}), {2}: (12, {}), {3}: (13, {}),... | custom-call | flops 6442450944 | bytes 18874368 | tf_op jit(solution)/shard_map/expert/pallas_call | solution.py:584
  363.0 12.8 %convolution_convert_fusion.2 = bf16[2048,1024]{1,0:T(8,128)(2,1)} fusion(bf16[2048,2048]{1,0:T(8,128)(2,1)} %get-tuple-element.829, bf16[2048,1024]{1,0:T(8,128)(2,1)S(1)} %copy-done.20), kind=kOutput, calls=%fused_computation.5 | convolution fusion | flops 8592031744 | bytes 16777216 | tf_op jit(solution)/shard_map/dot_general | solution.py:39
  389.6 14.6 %convolution_convert_fusion.1 = bf16[2048,1024]{1,0:T(8,128)(2,1)} fusion(bf16[2048,2048]{1,0:T(8,128)(2,1)} %get-tuple-element.829, bf16[2048,1024]{1,0:T(8,128)(2,1)} %get-tuple-element.830), kind=kOutput, calls=%fused_computation.4 | convolution fusion | flops 8592031744 | bytes 16777216 | tf_op jit(solution)/shard_map/dot_general | solution.py:39
  404.3 7.2 collective-permute-done.89
  424.3 7.4 collective-permute-done.93
  442.6 9.4 %collective-permute-done.97 = bf16[136,2048]{1,0:T(8,128)(2,1)} collective-permute-done((bf16[136,2048]{1,0:T(8,128)(2,1)}, bf16[136,2048]{1,0:T(8,128)(2,1)}, u32[]{:S(2)}, u32[]{:S(2)}) %collective-permute-start.97) | collective-permute-done | bytes 557088 | tf_op jit(solution)/shard_map/ppermute | solution.py:456
  478.8 8.4 %attend_back.6 = (f32[2048,128]{1,0:T(8,128)}, bf16[2048,2048]{1,0:T(8,128)(2,1)}, f32[2048,128]{1,0:T(8,128)}, f32[2048,128]{1,0:T(8,128)}) custom-call(bf16[128,2048]{1,0:T(8,128)(2,1)} %copy-done.70, bf16[128,2048]{1,0:T(8,128)(2,1)} %copy-done.71, ...), custom_call_target="tpu_custom_call", output_to_operand_aliasing={{2}: (9, {}), {3}: (10, {}), {0}: (11, {}), {1}: (12, {})} | custom-call | flops 1610612736 | bytes 8388608 | tf_op jit(solution)/shard_map/attend_back/pallas_call | solution.py:749
  488.6 9.9 %collective-permute-done.107 = bf16[128,2048]{1,0:T(8,128)(2,1)} collective-permute-done((bf16[128,2048]{1,0:T(8,128)(2,1)}, bf16[128,2048]{1,0:T(8,128)(2,1)}, u32[]{:S(2)}, u32[]{:S(2)}) %collective-permute-start.107) | collective-permute-done | bytes 524320 | tf_op jit(solution)/shard_map/ppermute | solution.py:456
  506.4 8.4 %attend_back.7 = (f32[2048,128]{1,0:T(8,128)}, bf16[2048,2048]{1,0:T(8,128)(2,1)}, f32[2048,128]{1,0:T(8,128)}, f32[2048,128]{1,0:T(8,128)}) custom-call(bf16[128,2048]{1,0:T(8,128)(2,1)} %copy-done.68, bf16[128,2048]{1,0:T(8,128)(2,1)} %copy-done.74, ...), custom_call_target="tpu_custom_call", output_to_operand_aliasing={{2}: (9, {}), {3}: (10, {}), {0}: (11, {}), {1}: (12, {})} | custom-call | flops 1610612736 | bytes 8388608 | tf_op jit(solution)/shard_map/attend_back/pallas_call | solution.py:749
  517.5 12.8 %convolution_convert_fusion = bf16[1024,2048]{1,0:T(8,128)(2,1)} fusion(bf16[2048,1024]{1,0:T(8,128)(2,1)S(1)} %copy-done.19, bf16[2048,2048]{1,0:T(8,128)(2,1)} %get-tuple-element.928), kind=kOutput, calls=%fused_computation.3 | convolution fusion | flops 8592031744 | bytes 16777216 | tf_op jit(solution)/shard_map/dot_general | solution.py:39
  531.9 8.3 %attend_back.8 = (f32[2048,128]{1,0:T(8,128)}, bf16[2048,2048]{1,0:T(8,128)(2,1)}, f32[2048,128]{1,0:T(8,128)}, f32[2048,128]{1,0:T(8,128)}) custom-call(bf16[128,2048]{1,0:T(8,128)(2,1)} %copy-done.43, bf16[128,2048]{1,0:T(8,128)(2,1)} %copy-done.77, ...), custom_call_target="tpu_custom_call", output_to_operand_aliasing={{2}: (9, {}), {3}: (10, {}), {0}: (11, {}), {1}: (12, {})} | custom-call | flops 1610612736 | bytes 8388608 | tf_op jit(solution)/shard_map/attend_back/pallas_call | solution.py:749
  545.9 6.2 attend_back.9
  561.9 5.9 fusion.102
  604.7 9.6 %multiply_reduce_fusion = (f32[2048]{0:T(1024)S(1)}, f32[2048,384]{1,0:T(8,128)}) fusion(bf16[2048,384]{1,0:T(8,128)(2,1)S(1)} %copy-done, bf16[2048,2048]{1,0:T(8,128)(2,1)} %get-tuple-element.975, bf16[2048,384]{1,0:T(8,128)(2,1)S(1)} %pad_maximum_fusion.1), kind=kOutput, calls=%fused_computation.8 | convolution fusion | flops 3223582720 | bytes 14688256 | tf_op jit(solution)/shard_map/dot_general | solution.py:39
  640.2 31.1 %collective-permute-done.140 = bf16[16,64,420]{2,1,0:T(8,128)(2,1)} collective-permute-done((bf16[16,64,420]{2,1,0:T(8,128)(2,1)S(1)}, bf16[16,64,420]{2,1,0:T(8,128)(2,1)}, u32[]{:S(2)}, u32[]{:S(2)}) %collective-permute-start.140) | collective-permute-done | bytes 860192 | tf_op jit(solution)/shard_map/ppermute | solution.py:451
  699.2 6.1 collective-permute-start.155
  (991 shorter events, 439.3 us)
Async XLA Ops:
  7.2 198.1 %all-gather.7.cloned.1.call-start = ((), (), s32[]{:S(2)}) async-start(), calls=%async_computation.6 | async-start | bytes 6291456 | tf_op jit(solution)/shard_map/all_gather | solution.py:989
  8.0 197.3 %all-gather.9.cloned.1.call-start = ((), (), s32[]{:S(2)}) async-start(), calls=%async_computation.7 | async-start | bytes 6291456 | tf_op jit(solution)/shard_map/all_gather | solution.py:990
  13.5 32.2 %collective-permute-start.4 = (bf16[1024,384]{1,0:T(8,128)(2,1)S(1)}, bf16[1024,384]{1,0:T(8,128)(2,1)}, u32[]{:S(2)}, u32[]{:S(2)}) collective-permute-start(bf16[1024,384]{1,0:T(8,128)(2,1)S(1)} %pad_maximum_fusion.3), channel_id=1, source_target_pairs={{0,1},{1,0},{2,3},{3,2},{4,5},{5,4},{6,7},{7,6},{8,9},{9,8},{10,11... | collective-permute-start | bytes 2359304 | tf_op jit(solution)/shard_map/ppermute | solution.py:451
  15.0 33.7 %collective-permute-start.3 = (bf16[136,2048]{1,0:T(8,128)(2,1)S(1)}, bf16[136,2048]{1,0:T(8,128)(2,1)}, u32[]{:S(2)}, u32[]{:S(2)}) collective-permute-start(bf16[136,2048]{1,0:T(8,128)(2,1)S(1)} %maximum_maximum_fusion.refs_0_), channel_id=1, source_target_pairs={{0,2},{2,0},{1,3},{3,1},{4,6},{6,4},{5,7},{7,5},{8,10},{10,8},{9,1... | collective-permute-start | bytes 1671176 | tf_op jit(solution)/shard_map/ppermute | solution.py:451
  17.0 54.0 %collective-permute-start.26 = (bf16[128,2048]{1,0:T(8,128)(2,1)}, bf16[128,2048]{1,0:T(8,128)(2,1)}, u32[]{:S(2)}, u32[]{:S(2)}) collective-permute-start(bf16[128,2048]{1,0:T(8,128)(2,1)} %constant_dynamic-slice_fusion.3), channel_id=1, source_target_pairs={{0,1},{1,0},{2,3},{3,2},{4,5},{5,4},{6,7},{7,6},{8,9},{9,8},{10,11... | collective-permute-start | bytes 1572872 | tf_op jit(solution)/shard_map/ppermute | solution.py:451
  18.6 196.9 %all-gather.11.cloned.1.call-start = ((), (), s32[]{:S(2)}) async-start(), calls=%async_computation.8 | async-start | bytes 6291456 | tf_op jit(solution)/shard_map/all_gather | solution.py:991
  18.7 35.0 %collective-permute-start.1 = (bf16[136,2048]{1,0:T(8,128)(2,1)S(1)}, bf16[136,2048]{1,0:T(8,128)(2,1)S(1)}, u32[]{:S(2)}, u32[]{:S(2)}) collective-permute-start(bf16[136,2048]{1,0:T(8,128)(2,1)S(1)} %maximum_maximum_fusion.refs_0_), channel_id=1, source_target_pairs={{0,8},{8,16},{16,24},{24,28},{28,20},{20,12},{12,4},{4,0},{1,9},{9... | collective-permute-start | bytes 1671176 | tf_op jit(solution)/shard_map/ppermute | solution.py:456
  20.3 33.4 %collective-permute-start.2 = (bf16[136,2048]{1,0:T(8,128)(2,1)S(1)}, bf16[136,2048]{1,0:T(8,128)(2,1)S(1)}, u32[]{:S(2)}, u32[]{:S(2)}) collective-permute-start(bf16[136,2048]{1,0:T(8,128)(2,1)S(1)} %maximum_maximum_fusion.refs_0_), channel_id=1, source_target_pairs={{0,4},{8,0},{16,8},{24,16},{28,24},{20,28},{12,20},{4,12},{1,5},{9... | collective-permute-start | bytes 1671176 | tf_op jit(solution)/shard_map/ppermute | solution.py:456
  158.7 566.7 %reduce-scatter.4.cloned.1.call-start = ((), (), s32[]{:S(2)}) async-start(), calls=%async_computation.3 | async-start | bytes 6291456 | tf_op jit(solution)/shard_map/reduce_scatter | solution.py:1135
  200.4 30.5 %collective-permute-start.43 = (bf16[128,2048]{1,0:T(8,128)(2,1)S(1)}, bf16[128,2048]{1,0:T(8,128)(2,1)S(1)}, u32[]{:S(2)}, u32[]{:S(2)}) collective-permute-start(bf16[128,2048]{1,0:T(8,128)(2,1)S(1)} %multiply_convert_fusion.refs_0_), channel_id=1, source_target_pairs={{0,8},{8,16},{16,24},{24,28},{28,20},{20,12},{12,4},{4,0},{1,9},{9... | collective-permute-start | bytes 1572872 | tf_op jit(solution)/shard_map/ppermute | solution.py:456
  232.1 30.9 %collective-permute-start.49 = (bf16[128,2048]{1,0:T(8,128)(2,1)S(1)}, bf16[128,2048]{1,0:T(8,128)(2,1)S(1)}, u32[]{:S(2)}, u32[]{:S(2)}) collective-permute-start(bf16[128,2048]{1,0:T(8,128)(2,1)S(1)} %collective-permute-done.43.refs_2_), channel_id=1, source_target_pairs={{0,8},{8,16},{16,24},{24,28},{28,20},{20,12},{12,4},{4,0},{1,9},{9... | collective-permute-start | bytes 1572872 | tf_op jit(solution)/shard_map/ppermute | solution.py:456
  264.1 33.5 %collective-permute-start.57 = (bf16[128,2048]{1,0:T(8,128)(2,1)S(1)}, bf16[128,2048]{1,0:T(8,128)(2,1)S(1)}, u32[]{:S(2)}, u32[]{:S(2)}) collective-permute-start(bf16[128,2048]{1,0:T(8,128)(2,1)S(1)} %collective-permute-done.49.refs_2_), channel_id=1, source_target_pairs={{0,8},{8,16},{16,24},{24,28},{28,20},{20,12},{12,4},{4,0},{1,9},{9... | collective-permute-start | bytes 1572872 | tf_op jit(solution)/shard_map/ppermute | solution.py:456
  265.2 32.5 %collective-permute-start.58 = (bf16[128,2048]{1,0:T(8,128)(2,1)S(1)}, bf16[128,2048]{1,0:T(8,128)(2,1)}, u32[]{:S(2)}, u32[]{:S(2)}) collective-permute-start(bf16[128,2048]{1,0:T(8,128)(2,1)S(1)} %collective-permute-done.50.refs_6_), channel_id=1, source_target_pairs={{0,8},{8,16},{16,24},{24,28},{28,20},{20,12},{12,4},{4,0},{1,9},{9... | collective-permute-start | bytes 1572872 | tf_op jit(solution)/shard_map/ppermute | solution.py:456
  301.0 31.6 %collective-permute-start.65 = (bf16[64,2048]{1,0:T(8,128)(2,1)S(1)}, bf16[64,2048]{1,0:T(8,128)(2,1)S(1)}, u32[]{:S(2)}, u32[]{:S(2)}) collective-permute-start(bf16[64,2048]{1,0:T(8,128)(2,1)S(1)} %slice.606), channel_id=1, source_target_pairs={{0,8},{8,16},{16,24},{24,28},{28,20},{20,12},{12,4},{4,0},{1,9},{9... | collective-permute-start | bytes 786440 | tf_op jit(solution)/shard_map/ppermute | solution.py:456
  301.9 30.7 %collective-permute-start.66 = (bf16[64,2048]{1,0:T(8,128)(2,1)S(1)}, bf16[64,2048]{1,0:T(8,128)(2,1)S(1)}, u32[]{:S(2)}, u32[]{:S(2)}) collective-permute-start(bf16[64,2048]{1,0:T(8,128)(2,1)S(1)} %slice.607), channel_id=1, source_target_pairs={{0,8},{8,16},{16,24},{24,28},{28,20},{20,12},{12,4},{4,0},{1,9},{9... | collective-permute-start | bytes 786440 | tf_op jit(solution)/shard_map/ppermute | solution.py:456
  386.8 338.5 %reduce-scatter.6.cloned.1.call-start = ((), (), s32[]{:S(2)}) async-start(), calls=%async_computation.4 | async-start | bytes 6291456 | tf_op jit(solution)/shard_map/reduce_scatter | solution.py:1135
  504.5 66.8 %collective-permute-start.130 = (bf16[128,2048]{1,0:T(8,128)(2,1)}, bf16[128,2048]{1,0:T(8,128)(2,1)}, u32[]{:S(2)}, u32[]{:S(2)}) collective-permute-start(bf16[128,2048]{1,0:T(8,128)(2,1)} %get-tuple-element.957), channel_id=1, source_target_pairs={{0,2},{2,0},{1,3},{3,1},{4,6},{6,4},{5,7},{7,5},{8,10},{10,8},{9,1... | collective-permute-start | bytes 1572872 | tf_op jit(solution)/shard_map/ppermute | solution.py:451
  504.6 220.8 %reduce-scatter.8.cloned.1.call-start = ((), (), s32[]{:S(2)}) async-start(), calls=%async_computation.5 | async-start | bytes 6291456 | tf_op jit(solution)/shard_map/reduce_scatter | solution.py:1135
  594.9 37.2 %collective-permute-start.156 = (bf16[64,2048]{1,0:T(8,128)(2,1)}, bf16[64,2048]{1,0:T(8,128)(2,1)}, u32[]{:S(2)}, u32[]{:S(2)}) collective-permute-start(bf16[64,2048]{1,0:T(8,128)(2,1)} %fusion.24), channel_id=1, source_target_pairs={{0,1},{1,0},{2,3},{3,2},{4,5},{5,4},{6,7},{7,6},{8,9},{9,8},{10,11... | collective-permute-start | bytes 786440 | tf_op jit(solution)/shard_map/ppermute | solution.py:451
  631.6 39.7 %collective-permute-start.140 = (bf16[16,64,420]{2,1,0:T(8,128)(2,1)S(1)}, bf16[16,64,420]{2,1,0:T(8,128)(2,1)}, u32[]{:S(2)}, u32[]{:S(2)}) collective-permute-start(bf16[16,64,420]{2,1,0:T(8,128)(2,1)S(1)} %pad_maximum_fusion.2), channel_id=1, source_target_pairs={{0,1},{1,0},{2,3},{3,2},{4,5},{5,4},{6,7},{7,6},{8,9},{9,8},{10,11... | collective-permute-start | bytes 2580488 | tf_op jit(solution)/shard_map/ppermute | solution.py:451
  633.8 46.9 %collective-permute-start.136 = (bf16[128,2048]{1,0:T(8,128)(2,1)}, bf16[128,2048]{1,0:T(8,128)(2,1)}, u32[]{:S(2)}, u32[]{:S(2)}) collective-permute-start(bf16[128,2048]{1,0:T(8,128)(2,1)} %add_convert_fusion.12), channel_id=1, source_target_pairs={{0,8},{8,16},{16,24},{24,28},{28,20},{20,12},{12,4},{4,0},{1,9},{9... | collective-permute-start | bytes 1572872 | tf_op jit(solution)/shard_map/ppermute | solution.py:456
  634.6 46.1 %collective-permute-start.137 = (bf16[128,2048]{1,0:T(8,128)(2,1)}, bf16[128,2048]{1,0:T(8,128)(2,1)}, u32[]{:S(2)}, u32[]{:S(2)}) collective-permute-start(bf16[128,2048]{1,0:T(8,128)(2,1)} %add_convert_fusion.11), channel_id=1, source_target_pairs={{0,4},{8,0},{16,8},{24,16},{28,24},{20,28},{12,20},{4,12},{1,5},{9... | collective-permute-start | bytes 1572872 | tf_op jit(solution)/shard_map/ppermute | solution.py:456
  639.6 41.1 %collective-permute-start.138 = (bf16[128,2048]{1,0:T(8,128)(2,1)}, bf16[128,2048]{1,0:T(8,128)(2,1)}, u32[]{:S(2)}, u32[]{:S(2)}) collective-permute-start(bf16[128,2048]{1,0:T(8,128)(2,1)} %get-tuple-element.1143), channel_id=1, source_target_pairs={{0,2},{2,0},{1,3},{3,1},{4,6},{6,4},{5,7},{7,5},{8,10},{10,8},{9,1... | collective-permute-start | bytes 1572872 | tf_op jit(solution)/shard_map/ppermute | solution.py:451
  639.6 41.1 %collective-permute-start.139 = (bf16[128,2048]{1,0:T(8,128)(2,1)}, bf16[128,2048]{1,0:T(8,128)(2,1)}, u32[]{:S(2)}, u32[]{:S(2)}) collective-permute-start(bf16[128,2048]{1,0:T(8,128)(2,1)} %get-tuple-element.1141), channel_id=1, source_target_pairs={{0,2},{2,0},{1,3},{3,1},{4,6},{6,4},{5,7},{7,5},{8,10},{10,8},{9,1... | collective-permute-start | bytes 1572872 | tf_op jit(solution)/shard_map/ppermute | solution.py:451
  (302 other events, 3317.5 us)
Sparse Core Ops, SparseCore 0:
  9.6 79.3 all-gather.6
  90.5 56.9 all-gather.8
  158.8 56.7 all-gather.10
  387.0 51.5 reduce-scatter.3
  504.7 53.8 reduce-scatter.5
  592.7 71.6 reduce-scatter.7

commit v3 on v2

--- a/solution.py
+++ b/solution.py
@@ -445,6 +445,11 @@
 EXTRA = 8
 PLACES = [1, 7, 2, 6, 3, 5, 0, 4]
 CHUNKS = {1: (0, 2), 2: (2, 2), 3: (4, 2), 0: (6, 1), FAR: (7, 1)}
+LAST = -1
+WIDE_CHUNKS = {1: (0, 2), 2: (2, 2), 3: (4, 2), LAST: (6, 2)}
+
+
+BRIEF = pl.CostEstimate(flops=0, bytes_accessed=0, transcendentals=0)
 
 
 def swap(array, axis):
@@ -474,40 +479,47 @@
     return [list(function(*inputs)) for inputs, function in jobs]
 
 
-def ring_gather(arrays, job, jobs=None):
-    cut = arrays[0].shape[0] // 2 // 8 * 8
-    ahead, behind = list(arrays), list(arrays)
-    fresh = [[array] for array in arrays]
-    results = {}
-    for step in range(1, FAR + 1):
-        if step == FAR:
-            ahead, behind = [a[:cut] for a in ahead], [b[cut:] for b in behind]
-        ahead, behind, *fresh = fence(ahead, behind, *fresh)
-        ahead, opened = open_jobs(ahead, (jobs or {}).get(step, []))
-        ahead, behind = [shift(a, 1) for a in ahead], [shift(b, -1) for b in behind]
-        blocks = [[x for block in group for x in (block, swap(block, "core"))] for group in fresh]
-        made, keep = job(step - 1, blocks)
-        done = run_jobs(opened)
-        ahead, behind, made, *done = fence(ahead, behind, list(made), *done)
-        keep(made)
-        results[step] = done
-        fresh = [[b, a] for a, b in zip(ahead, behind)]
-    last = [jnp.concatenate([a, b], axis=0) for a, b in zip(ahead, behind)]
-    made, keep = job(FAR, [[block, swap(block, "core")] for block in last])
-    keep(list(made))
-    return results
+class Gather:
+    def __init__(self, block):
+        self.ahead = self.behind = block
+        self.cut = block.shape[0] // 2 // 8 * 8
+        self.fresh = [block]
+        self.step = 0
+        self.chunks = {}
+
+    def job(self):
+        ahead, behind = self.ahead, self.behind
+        if self.step + 1 == FAR:
+            ahead, behind = ahead[: self.cut], behind[self.cut :]
+
+        def function(ahead, behind, *fresh):
+            ahead, behind = shift(ahead, 1), shift(behind, -1)
+            self.now = [x for block in fresh for x in (block, swap(block, "core"))]
+            return [ahead, behind, *self.now]
+
+        return [ahead, behind, *self.fresh], function
+
+    def take(self, results):
+        self.ahead, self.behind, *self.chunks[self.step] = results
+        self.step += 1
+        if self.step == FAR:
+            last = jnp.concatenate([self.ahead, self.behind], axis=0)
+            self.chunks[FAR] = [last, swap(last, "core")]
+            self.chunks[LAST] = self.chunks[0] + self.chunks[FAR]
+        self.fresh = [self.behind, self.ahead]
 
 
 class Scatter:
     def __init__(self, make, inputs=()):
         self.make, self.inputs = make, list(inputs)
         self.step = 0
-        self.extras = {}
-        (mine, other), self.extras[FAR] = make(FAR, *self.inputs)
-        first = (mine.astype(jnp.float32) + swap(other, "core").astype(jnp.float32)).astype(
-            jnp.bfloat16
-        )
-        self.cut = first.shape[0] // 2 // 8 * 8
+        mine, other = make(FAR, *self.inputs)
+        first = mine
+        if other is not None:
+            first = mine.astype(jnp.float32) + swap(other, "core").astype(jnp.float32)
+            first = first.astype(jnp.bfloat16)
+        self.rows = first.shape[0]
+        self.cut = self.rows // 2 // 8 * 8
         self.carried = [first[: self.cut], first[self.cut :]]
 
     def job(self):
@@ -515,59 +527,65 @@
 
         def function(ahead, behind, *inputs):
             ahead, behind = shift(ahead, 1), shift(behind, -1)
-            terms, extras = self.make(near, *inputs)
-            terms = [t if i % 2 == 0 else swap(t, "core") for i, t in enumerate(terms)]
-            return [ahead, behind, *terms, *extras]
+            mine, other = self.make(near, *inputs)
+            return [ahead, behind, mine] + ([] if other is None else [swap(other, "core")])
 
         return self.carried + self.inputs, function
 
     def take(self, results):
         self.step += 1
-        near = FAR - self.step
         ahead, behind, *terms = results
-        count = 4 if near else 2
-        terms, self.extras[near] = terms[:count], terms[count:]
-        terms = [t.astype(jnp.float32) for t in terms]
         ahead, behind = ahead.astype(jnp.float32), behind.astype(jnp.float32)
-        if near == 0:
-            self.total = terms[0] + terms[1] + ahead + behind
+
+        def term(i):
+            span = slice(i * self.rows, (i + 1) * self.rows)
+            return sum(part[span].astype(jnp.float32) for part in terms)
+
+        if self.step == FAR:
+            self.total = term(0) + ahead + behind
             return
         if self.step == 1:
             ahead = jnp.concatenate([ahead, jnp.zeros_like(behind)], axis=0)
             behind = jnp.concatenate([jnp.zeros_like(ahead[: self.cut]), behind], axis=0)
         self.carried = [
-            (terms[0] + terms[1] + ahead).astype(jnp.bfloat16),
-            (terms[2] + terms[3] + behind).astype(jnp.bfloat16),
+            (term(0) + ahead).astype(jnp.bfloat16),
+            (term(1) + behind).astype(jnp.bfloat16),
         ]
 
 
-def window(scatters, jobs):
-    every = [scatter.job() for scatter in scatters] + list(jobs)
+def window(items, jobs=(), loose=()):
+    every = [item.job() for item in items] + list(jobs) + list(loose)
     _, opened = open_jobs([], every)
-    results = fence(*run_jobs(opened))
-    for scatter, result in zip(scatters, results):
-        scatter.take(result)
-    return results[len(scatters) :]
-
-
-def exchange_all(parts):
-    pair = jnp.stack([parts[:, 0], swap(parts[:, 1], "core")], axis=1)
-    got = {0: pair[0]}
-    for at in range(1, CHIPS):
-        got[CHIPS - at] = shift(pair[at], at)
-    return jnp.stack([got[at] for at in range(CHIPS)], axis=0)
+    results = run_jobs(opened)
+    count = len(items) + len(jobs)
+    results = fence(*results[:count]) + results[count:]
+    for item, result in zip(items, results):
+        item.take(result)
+    return results[len(items) :]
 
 
 def sum_all(values, jobs):
     (values,), jobs = open_jobs([values], jobs)
+    core = lax.axis_index("core")
     both = values + swap(values[:, :, ::-1], "core")
-    moved = [shift(both, at) for at in range(1, CHIPS)]
+
+    def heard(by):
+        pairs = [
+            (2 * RING[i] + c, 2 * RING[(i + (by if c == 0 else -by)) % CHIPS] + c)
+            for i in range(CHIPS)
+            for c in range(2)
+        ]
+        return lax.ppermute(both, ("chip", "core"), pairs)
+
+    moved = [heard(by) for by in range(1, FAR + 1)]
     done = run_jobs(jobs)
     moved, *done = fence(moved, *done)
-    total = both
-    for at in range(1, CHIPS):
-        total = total + jnp.roll(moved[at - 1], -at, axis=1)
-    return total, done
+    total = jnp.where(core == 0, both, jnp.roll(moved[-1], -FAR, axis=1))
+    for by in range(1, FAR):
+        total = total + jnp.where(
+            core == 0, jnp.roll(moved[by - 1], -by, axis=1), jnp.roll(moved[by - 1], by, axis=1)
+        )
+    return total + swap(total[:, :, ::-1], "core"), done
 
 
 def by_place(values, axis):
@@ -580,7 +598,16 @@
     return jnp.stack([lax.index_in_dim(values, at, axis, False) for at in PLACES], axis)
 
 
-def call(kernel, name, inputs, ins, outs, shapes, earlier=(), grid=(1,), scratch=(), cost=None, mib=56):
+def in_hbm(arrays, specs):
+    return [
+        array
+        if spec.memory_space == pltpu.SMEM
+        else pltpu.with_memory_space_constraint(array, pltpu.HBM)
+        for array, spec in zip(arrays, specs)
+    ]
+
+
+def call(kernel, name, inputs, ins, outs, shapes, earlier=(), grid=(1,), scratch=(), mib=56):
     return pl.pallas_call(
         kernel,
         grid=grid,
@@ -590,9 +617,9 @@
         scratch_shapes=list(scratch),
         input_output_aliases={len(ins) + i: i for i in range(len(earlier))},
         compiler_params=pltpu.CompilerParams(vmem_limit_bytes=mib << 20),
-        cost_estimate=pl.CostEstimate(flops=cost[0], bytes_accessed=cost[1], transcendentals=cost[2]),
+        cost_estimate=BRIEF,
         name=name,
-    )(*inputs, *earlier)
+    )(*in_hbm(inputs, ins), *earlier)
 
 
 def whole(array):
@@ -606,22 +633,23 @@
 
 
 def rows_of(step, tok_rows, cols):
-    first, count = CHUNKS[step]
+    first, count = WIDE_CHUNKS[step] if step == LAST else CHUNKS[step]
     index = first // count
     return pl.BlockSpec((2 * count * tok_rows, cols), lambda i: (index, 0))
 
 
-def lin_chunk(step, blocks, weight, place, tok_rows, earlier):
+def lin_chunk(step, blocks, weight, gain, place, tok_rows, earlier):
     count, width, cols = len(blocks), weight.shape[0], weight.shape[1]
     length = 2 * CHIPS * tok_rows
     rows, head = count * tok_rows, weight.shape[1] // 3
 
     def kernel(*refs):
-        block_refs, weight_ref, place_ref = refs[:count], refs[count], refs[count + 1]
+        block_refs, weight_ref, gain_ref, place_ref = refs[:count], *refs[count : count + 3]
         lin_ref, all_ref, sum_ref, tag_ref = refs[-4:]
         lanes = pl.ds(pl.multiple_of(place_ref[0] * tok_rows, tok_rows), tok_rows)
         for i in range(count):
-            all_ref[i * tok_rows : (i + 1) * tok_rows] = block_refs[i][:tok_rows]
+            normed, _ = rms_forward(block_refs[i][:tok_rows].astype(jnp.float32), gain_ref[...])
+            all_ref[i * tok_rows : (i + 1) * tok_rows] = normed.astype(jnp.bfloat16)
             levels = block_refs[i][tok_rows:, lanes].astype(jnp.float32)
             others = block_refs[i][tok_rows:, : 3 * tok_rows].astype(jnp.float32)
             tag_ref[i * EXTRA : (i + 1) * EXTRA] = jnp.concatenate(
@@ -650,8 +678,9 @@
     return call(
         kernel,
         "lin",
-        [*blocks, weight, place],
-        [whole(b) for b in blocks] + [whole(weight), pl.BlockSpec(memory_space=pltpu.SMEM)],
+        [*blocks, weight, gain, place],
+        [whole(b) for b in blocks]
+        + [whole(weight), whole(gain), pl.BlockSpec(memory_space=pltpu.SMEM)],
         [rows_of(step, tok_rows, cols), rows_of(step, tok_rows, width), whole(sums), whole(tags)],
         [
             jax.ShapeDtypeStruct((length, cols), jnp.float32),
@@ -660,15 +689,48 @@
             tags,
         ],
         earlier,
-        cost=(2 * rows * width * cols, 4 * rows * width + 2 * weight.size, 0),
-    )
-
-
-def attend_chunk(step, queries, keys, values, weight, tok_rows, score_scale):
+    )
+
+
+def both_halves(cosine, sine_part):
+    return (
+        jnp.concatenate([cosine, cosine], axis=-1),
+        jnp.concatenate([-sine_part, sine_part], axis=-1),
+    )
+
+
+def rotate_rows(lin, inverse, gains, cosine, sine_part):
+    length, cols = lin.shape
+    head = cols // 3
+    rows = length // 4
+
+    def kernel(lin_ref, inv_ref, gain_ref, cos_ref, sin_ref, q_ref, k_ref, v_ref):
+        cos, sin = both_halves(cos_ref[...], sin_ref[...])
+        for k, out_ref in enumerate((q_ref, k_ref)):
+            part = lin_ref[:, k * head : (k + 1) * head] * inv_ref[:, k : k + 1]
+            part = part * gain_ref[k : k + 1]
+            turned = pltpu.roll(part, head // 2, 1)
+            out_ref[...] = (part * cos + turned * sin).astype(jnp.bfloat16)
+        v_ref[...] = lin_ref[:, 2 * head :].astype(jnp.bfloat16)
+
+    row = lambda width: pl.BlockSpec((rows, width), lambda i: (i, 0))
+    return call(
+        kernel,
+        "rotate",
+        [lin, inverse, gains, cosine, sine_part],
+        [row(cols), row(2), whole(gains), row(head // 2), row(head // 2)],
+        [row(head)] * 3,
+        [jax.ShapeDtypeStruct((length, head), jnp.bfloat16)] * 3,
+        grid=(4,),
+        mib=16,
+    )
+
+
+def attend_chunk(step, queries, keys, values, tok_rows, score_scale):
     count = 2 * CHUNKS[step][1]
-    head, width, length = keys.shape[1], weight.shape[1], keys.shape[0]
-
-    def kernel(q_ref, k_ref, v_ref, w_ref, out_ref, lse_ref, *parts):
+    head = keys.shape[1]
+
+    def kernel(q_ref, k_ref, v_ref, out_ref, lse_ref, mine_ref, other_ref):
         for i in range(0, count, 2):
             span = pl.ds(i * tok_rows, 2 * tok_rows)
             scores = contract_cols(q_ref[span], k_ref[...]) * score_scale
@@ -679,49 +741,91 @@
             mixed = product(probs, v_ref[...]).astype(jnp.bfloat16)
             out_ref[span] = mixed
             lse_ref[span] = row_max + jnp.log(total)
-            term = product(mixed, w_ref[...]).astype(jnp.bfloat16)
-            parts[i][...] = term[:tok_rows]
-            parts[i + 1][...] = term[tok_rows:]
+            half = pl.ds(i // 2 * tok_rows, tok_rows)
+            mine_ref[half] = mixed[:tok_rows]
+            other_ref[half] = mixed[tok_rows:]
 
     rows = count * tok_rows
     shapes = [
         jax.ShapeDtypeStruct((rows, head), jnp.bfloat16),
         jax.ShapeDtypeStruct((rows, 1), jnp.float32),
-    ] + [jax.ShapeDtypeStruct((tok_rows, width), jnp.bfloat16)] * count
+    ] + [jax.ShapeDtypeStruct((rows // 2, head), jnp.bfloat16)] * 2
     return call(
         kernel,
         "attend",
-        [queries, keys, values, weight],
-        [rows_of(step, tok_rows, head), whole(keys), whole(values), whole(weight)],
+        [queries, keys, values],
+        [rows_of(step, tok_rows, head), whole(keys), whole(values)],
         [whole(shape) for shape in shapes],
         shapes,
-        cost=(
-            4 * rows * length * head + 2 * rows * head * width,
-            4 * length * head + 2 * rows * width,
-            rows * length,
-        ),
-    )
+        mib=40,
+    )
+
+
+def pair_product(left, right, left_weight, right_weight, transposed, name, step=None):
+    multiply = contract_cols if transposed else product
+    width = left_weight.shape[0] if transposed else left_weight.shape[1]
+    rows, block = left.shape[0], whole(left)
+    if step is not None:
+        first, count = CHUNKS[step]
+        rows, index = rows * count // CHIPS, first // count
+        block = pl.BlockSpec((rows, left.shape[1]), lambda i: (index, 0))
+
+    def kernel(left_ref, right_ref, left_weight_ref, right_weight_ref, out_ref):
+        total = multiply(left_ref[...], left_weight_ref[...])
+        total = total + multiply(right_ref[...], right_weight_ref[...])
+        out_ref[...] = total.astype(jnp.bfloat16)
+
+    shape = jax.ShapeDtypeStruct((rows, width), jnp.bfloat16)
+    arrays = [left, right, left_weight, right_weight]
+    return call(
+        kernel,
+        name,
+        arrays,
+        [block, block, whole(left_weight), whole(right_weight)],
+        [whole(shape)],
+        [shape],
+        mib=32,
+    )[0]
 
 
 def attend_back_chunk(
-    step, blocks, queries, lse, keys, values, weight, tok_rows, score_scale, earlier
+    step, blocks, queries, lse, keys, values, weight, lin, gains, cosine, sine_part, tok_rows,
+    score_scale, earlier, final
 ):
     count = len(blocks)
     length, head = keys.shape
     width = weight.shape[1]
     rows = count * tok_rows
 
+    def unspun(grad, cosine, sine_part, gain):
+        cos, sin = both_halves(cosine, sine_part)
+        return (grad * cos - pltpu.roll(grad, head // 2, 1) * sin) * gain
+
+    def line_sums(values):
+        ones = jnp.ones((8, head), jnp.float32)
+        return lax.dot_general(
+            ones,
+            values,
+            (((1,), (1,)), ((), ())),
+            precision=lax.Precision.HIGHEST,
+            preferred_element_type=jnp.float32,
+        )
+
     def kernel(*refs):
         block_refs = refs[:count]
-        q_ref, lse_ref, k_ref, v_ref, w_ref = refs[count : count + 5]
-        dq_ref, all_ref, dk_ref, dv_ref = refs[-4:]
+        q_ref, lse_ref, lin_ref, cos_ref, sin_ref = refs[count : count + 5]
+        k_ref, v_ref, w_ref, gain_ref = refs[count + 5 : count + 9]
+        rest = refs[count + 9 :]
+        if final:
+            k_lin_ref, cos_all, sin_all = rest[:3]
+            rest = rest[3:]
+        if earlier:
+            dk, dv = rest[0][...], rest[1][...]
+        else:
+            dk, dv = 0.0, 0.0
+        dq_ref, all_ref, dk_ref, dv_ref, q_sums = rest[-6:-1] if final else rest[-5:]
         for i in range(count):
             all_ref[i * tok_rows : (i + 1) * tok_rows] = block_refs[i][...]
-        if earlier:
-            dk_in, dv_in = refs[count + 5 : count + 7]
-            dk, dv = dk_in[...], dv_in[...]
-        else:
-            dk, dv = 0.0, 0.0
         for i in range(0, count, 2):
             span = pl.ds(i * tok_rows, 2 * tok_rows)
             queries = q_ref[span]
@@ -730,40 +834,51 @@
             dprobs = contract_cols(douts, v_ref[...])
             delta = jnp.sum(probs * dprobs, axis=-1, keepdims=True)
             dscores = (probs * (dprobs - delta)).astype(jnp.bfloat16)
-            dq_ref[span] = product(dscores, k_ref[...]) * score_scale
+            dq = product(dscores, k_ref[...]) * score_scale
+            dq = unspun(dq, cos_ref[span], sin_ref[span], gain_ref[:1])
+            dq_ref[span] = dq
+            q_sums[:, i * tok_rows : (i + 2) * tok_rows] = line_sums(dq * lin_ref[span])
             dk = dk + contract_rows(dscores, queries) * score_scale
             dv = dv + contract_rows(probs.astype(jnp.bfloat16), douts)
+        if final:
+            dk = unspun(dk, cos_all[...], sin_all[...], gain_ref[1:])
+            rest[-1][...] = line_sums(dk * k_lin_ref[...])
         dk_ref[...] = dk
         dv_ref[...] = dv
 
     total = jax.ShapeDtypeStruct((length, head), jnp.float32)
-    inputs = [*blocks, queries, lse, keys, values, weight]
+    inputs = [*blocks, queries, lse, lin, cosine, sine_part, keys, values, weight, gains]
     ins = [whole(b) for b in blocks] + [
         rows_of(step, tok_rows, head),
         rows_of(step, tok_rows, 1),
+        rows_of(step, tok_rows, head),
+        rows_of(step, tok_rows, head // 2),
+        rows_of(step, tok_rows, head // 2),
         whole(keys),
         whole(values),
         whole(weight),
+        whole(gains),
     ]
-    sums = list(earlier[2:])
+    sums = [jax.ShapeDtypeStruct((8, rows), jnp.float32)]
+    if final:
+        inputs += [lin, cosine, sine_part]
+        ins += [pl.BlockSpec((length, head), lambda i: (0, 1)), whole(cosine), whole(sine_part)]
+        sums += [jax.ShapeDtypeStruct((8, length), jnp.float32)]
+    so_far = list(earlier[2:4])
     return pl.pallas_call(
         kernel,
         grid=(1,),
         in_specs=ins
-        + [whole(s) for s in sums]
+        + [whole(part) for part in so_far]
         + [pl.BlockSpec(memory_space=pl.ANY)] * len(earlier[:2]),
         out_specs=[
             rows_of(step, tok_rows, head),
             rows_of(step, tok_rows, width),
             whole(total),
             whole(total),
-        ],
-        out_shape=[
-            total,
-            jax.ShapeDtypeStruct((length, width), jnp.bfloat16),
-            total,
-            total,
-        ],
+        ]
+        + [whole(part) for part in sums],
+        out_shape=[total, jax.ShapeDtypeStruct((length, width), jnp.bfloat16), total, total] + sums,
         input_output_aliases={
             len(ins): 2,
             len(ins) + 1: 3,
@@ -773,16 +888,41 @@
         if earlier
         else {},
         compiler_params=pltpu.CompilerParams(vmem_limit_bytes=56 << 20),
-        cost_estimate=pl.CostEstimate(
-            flops=10 * rows * length * head + 2 * rows * head * width,
-            bytes_accessed=16 * length * head + 4 * rows * width,
-            transcendentals=rows * length,
-        ),
+        cost_estimate=BRIEF,
         name="attend_back",
-    )(*inputs, *sums, *earlier[:2])
-
-
-EXPERT_COLS = 256
+    )(*in_hbm(inputs, ins), *so_far, *earlier[:2])
+
+
+def lin_back_rows(dq, dk, dv, lin, inverse, along, tok_rows):
+    length, cols = lin.shape
+    head = cols // 3
+    rows = 2 * tok_rows
+
+    def kernel(dq_ref, dk_ref, dv_ref, lin_ref, inv_ref, along_ref, out_ref, mine_ref, other_ref):
+        for k, grad_ref in enumerate((dq_ref, dk_ref)):
+            span = slice(k * head, (k + 1) * head)
+            inv = inv_ref[:, k : k + 1]
+            slope = inv * inv * inv * along_ref[:, k : k + 1]
+            out_ref[:, span] = (inv * grad_ref[...] - lin_ref[:, span] * slope).astype(jnp.bfloat16)
+        out_ref[:, 2 * head :] = dv_ref[...].astype(jnp.bfloat16)
+        mine_ref[...] = out_ref[:tok_rows]
+        other_ref[...] = out_ref[tok_rows:]
+
+    row = lambda width: pl.BlockSpec((rows, width), lambda i: (i, 0))
+    half = jax.ShapeDtypeStruct((length // 2, cols), jnp.bfloat16)
+    return call(
+        kernel,
+        "lin_back",
+        [dq, dk, dv, lin, inverse, along],
+        [row(head)] * 3 + [row(cols), row(2), row(2)],
+        [row(cols)] + [pl.BlockSpec((tok_rows, cols), lambda i: (i, 0))] * 2,
+        [jax.ShapeDtypeStruct((length, cols), jnp.bfloat16), half, half],
+        grid=(CHIPS,),
+        mib=16,
+    )
+
+
+EXPERT_COLS = 512
 
 
 def expert_chunk(step, h_blocks, g_blocks, place, kept, router, gate, up, down, tok_rows, earlier):
@@ -792,20 +932,32 @@
     rows = count * tok_rows
     length = 2 * CHIPS * tok_rows
     low = jnp.bfloat16
-    first, places = CHUNKS[step]
+    first, places = WIDE_CHUNKS[step]
     index = first // places
+    inner, outer = hidden // cols, width // cols
+    long_rows = tok_rows + EXTRA
+    per_tile = cols // tok_rows
+    apart = places if step == LAST else 1
+    together = places // apart
 
     def kernel(*refs):
         h_refs, g_refs = refs[:count], refs[count : 2 * count]
-        place_ref, kept_ref, router_ref, gate_ref, up_ref, down_ref = refs[
-            2 * count : 2 * count + 6
+        place_ref, kept_ref, router_ref = refs[2 * count : 2 * count + 3]
+        gate_ref, up_ref, down_ref, gate_rows, up_rows, down_cols = refs[
+            2 * count + 3 : 2 * count + 9
         ]
-        outs = refs[-(2 * count + 9) : -4]
-        act_ref, dgate_ref, dup_ref, h_all, g_all = outs[:5]
-        mix_refs, dx_refs = outs[5 : 5 + count], outs[5 + count :]
-        mix_sum, dx_sum, share_ref, dshare_ref = refs[-4:]
+        outs = refs[2 * count + 9 + len(earlier) : -8]
+        row_outs, (act_ref, dgate_ref, dup_ref) = outs[:2], outs[2:5]
+        mix_refs, dx_refs = outs[5 : 5 + 2 * apart], outs[5 + 2 * apart :]
+        h_all, g_all, act_all, dgate_all, dup_all, share_ref, dshare_ref, sems = refs[-8:]
         turn = pl.program_id(0)
-        last = pl.num_programs(0) - 1
+
+        def copies():
+            span = pl.ds(index * rows, rows)
+            return [
+                pltpu.make_async_copy(source, out.at[span], sems.at[i])
+                for i, (source, out) in enumerate(zip((h_all, g_all), row_outs))
+            ]
 
         @pl.when(turn == 0)
         def _():
@@ -820,92 +972,208 @@
                 jnp.where(lanes == place_ref[0], probs, 0.0), axis=-1, keepdims=True
             )
             share_ref[...] = chosen * kept_ref[...]
-
-        hidden_rows, grads, share = h_all[...], g_all[...], share_ref[...]
-        gate_lin = product(hidden_rows, gate_ref[...])
-        up_lin = product(hidden_rows, up_ref[...])
-        back = contract_cols(grads, down_ref[...])
-        sig = jax.nn.sigmoid(gate_lin)
-        silu = gate_lin * sig
-        act = silu * up_lin
-        dshare = jnp.sum(act * back, axis=-1, keepdims=True)
-        act_low = (act * share).astype(low)
-        back = back * share
-        dgate = (back * up_lin * (sig * (1.0 + gate_lin * (1.0 - sig)))).astype(low)
-        dup = (back * silu).astype(low)
-        act_ref[...] = act_low
-        dgate_ref[...] = dgate
-        dup_ref[...] = dup
-        mix = product(act_low, down_ref[...])
-        dx = contract_cols(dgate, gate_ref[...]) + contract_cols(dup, up_ref[...])
-
-        @pl.when(turn == 0)
+            dshare_ref[...] = jnp.zeros_like(dshare_ref)
+
+        @pl.when(turn == 1)
         def _():
-            dshare_ref[...] = dshare
-            mix_sum[...] = mix
-            dx_sum[...] = dx
-
-        @pl.when((turn > 0) & (turn < last))
+            for copy in copies():
+                copy.start()
+
+        @pl.when(turn < inner)
         def _():
-            dshare_ref[...] += dshare
-            mix_sum[...] += mix
-            dx_sum[...] += dx
-
-        @pl.when(turn == last)
+            share = share_ref[...]
+            gate_lin = product(h_all[...], gate_ref[...])
+            up_lin = product(h_all[...], up_ref[...])
+            back = contract_cols(g_all[...], down_ref[...])
+            sig = jax.nn.sigmoid(gate_lin)
+            silu = gate_lin * sig
+            act = silu * up_lin
+            dshare_ref[...] += jnp.sum(act * back, axis=-1, keepdims=True)
+            act_low = (act * share).astype(low)
+            back = back * share
+            dgate = (back * up_lin * (sig * (1.0 + gate_lin * (1.0 - sig)))).astype(low)
+            dup = (back * silu).astype(low)
+            span = pl.ds(pl.multiple_of(turn * cols, cols), cols)
+            for ref, everything, value in (
+                (act_ref, act_all, act_low),
+                (dgate_ref, dgate_all, dgate),
+                (dup_ref, dup_all, dup),
+            ):
+                ref[...] = value
+                everything[:, span] = value
+
+        @pl.when(turn >= inner)
         def _():
-            mix_low = (mix_sum[...] + mix).astype(low)
-            dx_low = (dx_sum[...] + dx).astype(low)
-            total = (dshare_ref[...] + dshare) * kept_ref[...]
+            mix = product(act_all[...], down_cols[...]).astype(low)
+            dx = contract_cols(dgate_all[...], gate_rows[...])
+            dx = (dx + contract_cols(dup_all[...], up_rows[...])).astype(low)
+            for i in range(count):
+                span = slice(i * tok_rows, (i + 1) * tok_rows)
+                to, at = i % 2 + i // 2 // together * 2, i // 2 % together
+                mix_refs[to][at * tok_rows : (at + 1) * tok_rows] = mix[span]
+                dx_refs[to][at * long_rows : at * long_rows + tok_rows] = dx[span]
+
+            total = dshare_ref[...] * kept_ref[...]
             same = lax.broadcasted_iota(jnp.int32, (tok_rows, tok_rows), 0) == (
                 lax.broadcasted_iota(jnp.int32, (tok_rows, tok_rows), 1)
             )
-            lanes = pl.ds(pl.multiple_of(place_ref[0] * tok_rows, tok_rows), tok_rows)
+            tile_lanes = lax.broadcasted_iota(jnp.int32, (EXTRA, cols), 1) // tok_rows
+            here = tile_lanes + (turn - inner) * per_tile == place_ref[0]
             for i in range(count):
-                span = slice(i * tok_rows, (i + 1) * tok_rows)
-                mix_refs[i][...] = mix_low[span]
-                dx_refs[i][:tok_rows] = dx_low[span]
-                line = jnp.sum(jnp.where(same, total[span], 0.0), axis=0, keepdims=True)
-                pieces, rest = [], line
+                rest = jnp.sum(
+                    jnp.where(same, total[i * tok_rows : (i + 1) * tok_rows], 0.0),
+                    axis=0,
+                    keepdims=True,
+                )
+                pieces = []
                 for _ in range(3):
-                    piece = rest.astype(low)
-                    rest = rest - piece.astype(jnp.float32)
-                    pieces.append(piece.astype(jnp.float32))
+                    piece = rest.astype(low).astype(jnp.float32)
+                    rest = rest - piece
+                    pieces.append(piece)
                 pieces.append(jnp.zeros((EXTRA - 3, tok_rows), jnp.float32))
-                dx_refs[i][tok_rows:] = jnp.zeros((EXTRA, width), low)
-                dx_refs[i][tok_rows:, lanes] = jnp.concatenate(pieces, axis=0).astype(low)
-
-    tile = pl.BlockSpec((rows, cols), lambda j: (index, j))
-    all_rows = pl.BlockSpec((rows, width), lambda j: (index, 0))
+                line = jnp.concatenate(pieces, axis=0)
+                line = jnp.concatenate([line] * per_tile, axis=1)
+                to, at = i % 2 + i // 2 // together * 2, i // 2 % together
+                at = at * long_rows + tok_rows
+                dx_refs[to][at : at + EXTRA] = jnp.where(here, line, 0.0).astype(low)
+
+        @pl.when(turn == inner + outer - 1)
+        def _():
+            for copy in copies():
+                copy.wait()
+
+    def inner_at(t):
+        return jnp.minimum(t, inner - 1)
+
+    def outer_at(t):
+        return jnp.maximum(t - inner, 0)
+
+    tile = pl.BlockSpec((rows, cols), lambda t: (index, inner_at(t)))
     wide = jax.ShapeDtypeStruct((length, hidden), low)
     full = jax.ShapeDtypeStruct((length, width), low)
-    block = jax.ShapeDtypeStruct((tok_rows, width), low)
-    longer = jax.ShapeDtypeStruct((tok_rows + EXTRA, width), low)
+    half = jax.ShapeDtypeStruct((together * tok_rows, width), low)
+    longer = jax.ShapeDtypeStruct((together * long_rows, width), low)
+    anywhere = pl.BlockSpec(memory_space=pl.ANY)
+    out_tile = lambda shape: pl.BlockSpec((shape.shape[0], cols), lambda t: (0, outer_at(t)))
     return call(
         kernel,
         "expert",
-        [*h_blocks, *g_blocks, place, kept, router, gate, up, down],
+        [*h_blocks, *g_blocks, place, kept, router, gate, up, down, gate, up, down],
         [once(b) for b in [*h_blocks, *g_blocks]]
         + [
             pl.BlockSpec(memory_space=pltpu.SMEM),
-            pl.BlockSpec((rows, 1), lambda j: (index, 0)),
+            pl.BlockSpec((rows, 1), lambda t: (index, 0)),
             whole(router),
-            pl.BlockSpec((width, cols), lambda j: (0, j)),
-            pl.BlockSpec((width, cols), lambda j: (0, j)),
-            pl.BlockSpec((cols, width), lambda j: (j, 0)),
+            pl.BlockSpec((width, cols), lambda t: (0, inner_at(t))),
+            pl.BlockSpec((width, cols), lambda t: (0, inner_at(t))),
+            pl.BlockSpec((cols, width), lambda t: (inner_at(t), 0)),
+            pl.BlockSpec((cols, hidden), lambda t: (outer_at(t), 0)),
+            pl.BlockSpec((cols, hidden), lambda t: (outer_at(t), 0)),
+            pl.BlockSpec((hidden, cols), lambda t: (0, outer_at(t))),
         ],
-        [tile] * 3 + [all_rows] * 2 + [whole(block)] * count + [whole(longer)] * count,
-        [wide] * 3 + [full] * 2 + [block] * count + [longer] * count,
+        [anywhere] * 2
+        + [tile] * 3
+        + [out_tile(half)] * (2 * apart)
+        + [out_tile(longer)] * (2 * apart),
+        [full] * 2 + [wide] * 3 + [half] * (2 * apart) + [longer] * (2 * apart),
         earlier,
-        grid=(hidden // cols,),
-        scratch=[pltpu.VMEM((rows, width), jnp.float32)] * 2
-        + [pltpu.VMEM((rows, 1), jnp.float32)] * 2,
-        cost=(
-            12 * rows * width * hidden,
-            6 * width * hidden + 12 * rows * width,
-            2 * rows * hidden,
-        ),
-        mib=60,
-    )
+        grid=(inner + outer,),
+        scratch=[pltpu.VMEM((rows, width), low)] * 2
+        + [pltpu.VMEM((rows, hidden), low)] * 3
+        + [pltpu.VMEM((rows, 1), jnp.float32)] * 2
+        + [pltpu.SemaphoreType.DMA((2,))],
+        mib=58,
+    )
+
+
+THIN = 128
+HALF_THIN = THIN // 2
+
+
+def split_parts(values):
+    high = values.astype(jnp.bfloat16).astype(jnp.float32)
+    return high, values - high
+
+
+def dense_chunk(rows_h, grads, weight, columns, gain, narrow, part, own_rows):
+    length, width = rows_h.shape
+    cols = grads.shape[1]
+    block = 256
+    runs = block // (2 * own_rows)
+    wide = narrow is not None
+    first_col, count_col = columns
+
+    def kernel(part_ref, h_ref, grads_ref, weight_ref, gain_ref, *refs):
+        kept_ref, sent_ref = refs[-2:] if wide else refs[-3:-1]
+        grads = contract_rows(h_ref[...], grads_ref[...])
+        weight = weight_ref[...].astype(jnp.float32)[:, first_col : first_col + count_col]
+        term = jnp.sum(grads * weight, axis=-1, keepdims=True) / gain_ref[...]
+        both = plain = grads
+        if wide:
+            narrow = refs[0][...]
+            lanes = lax.broadcasted_iota(jnp.int32, narrow.shape, 1)
+            narrow = jnp.where(lanes == 17, refs[1][...] + term, narrow)
+            high, rest = split_parts(narrow)
+            both = jnp.concatenate([both, high, rest], axis=-1)
+            plain = jnp.concatenate([plain, narrow, jnp.zeros_like(narrow)], axis=-1)
+        else:
+            refs[-1][...] = term
+        second = part_ref[0] == 1
+        for i in range(runs):
+            at = 2 * i * own_rows
+            first = slice(at, at + own_rows)
+            other = slice(at + own_rows, at + 2 * own_rows)
+            to = slice(i * own_rows, (i + 1) * own_rows)
+            kept_ref[to] = jnp.where(second, plain[other], plain[first])
+            sent_ref[to] = jnp.where(second, both[first], both[other]).astype(jnp.bfloat16)
+
+    full = cols + (THIN if wide else 0)
+    out = lambda kind: jax.ShapeDtypeStruct((width // 2, full), kind)
+    row = lambda size: pl.BlockSpec((block // 2, size), lambda i: (i, 0))
+    here = lambda size: pl.BlockSpec((block, size), lambda i: (i, 0))
+    return call(
+        kernel,
+        "dense",
+        [part, rows_h, grads, weight, gain] + (list(narrow) if wide else []),
+        [
+            pl.BlockSpec(memory_space=pltpu.SMEM),
+            pl.BlockSpec((length, block), lambda i: (0, i)),
+            whole(grads),
+            here(weight.shape[1]),
+            here(1),
+        ]
+        + ([here(HALF_THIN), here(1)] if wide else []),
+        [row(full), row(full)] + ([] if wide else [here(1)]),
+        [out(jnp.float32), out(jnp.bfloat16)]
+        + ([] if wide else [jax.ShapeDtypeStruct((width, 1), jnp.float32)]),
+        grid=(width // block,),
+        mib=40,
+    )
+
+
+def dense_sum(kept, got):
+    rows, full = kept.shape
+    cols = full - THIN
+    block = rows // 4
+
+    def kernel(kept_ref, got_ref, out_ref):
+        got = got_ref[...].astype(jnp.float32)
+        out_ref[:, :cols] = (kept_ref[:, :cols] + got[:, :cols]).astype(jnp.bfloat16)
+        narrow = kept_ref[:, cols : cols + HALF_THIN]
+        narrow = narrow + got[:, cols : cols + HALF_THIN] + got[:, cols + HALF_THIN :]
+        out_ref[:, cols:] = jnp.concatenate(split_parts(narrow), axis=-1).astype(jnp.bfloat16)
+
+    row = pl.BlockSpec((block, full), lambda i: (i, 0))
+    return call(
+        kernel,
+        "dense_sum",
+        [kept, got],
+        [row, row],
+        [row],
+        [jax.ShapeDtypeStruct((rows, full), jnp.bfloat16)],
+        grid=(4,),
+        mib=16,
+    )[0]
 
 
 def body(
@@ -965,16 +1233,6 @@
         ],
         axis=0,
     )
-    small_other = swap(small, "fsdp")
-    small_full = joined(small, small_other, 1)
-    r_weight = small_full[:expert_count]
-    g_attn = small_full[expert_count].astype(jnp.float32)
-    g_ffn = small_full[expert_count + 1].astype(jnp.float32)
-    here = part == place // per_half
-    g_heads = jnp.where(here, small[expert_count + 2], small_other[expert_count + 2]).astype(
-        jnp.float32
-    )
-    g_query, g_key = g_heads[:head_dim], g_heads[head_dim : 2 * head_dim]
     qkv_mine = jnp.concatenate(
         [
             lax.dynamic_slice_in_dim(w, place * head_dim, head_dim, 1)
@@ -982,13 +1240,7 @@
         ],
         axis=1,
     )
-    qkv_other = swap(qkv_mine, "fsdp")
-    qkv_weight = joined(qkv_mine, qkv_other, 0)
     out_mine = head_rows(w_out, head_dim)
-    out_weight = jnp.where(here, out_mine, swap(out_mine, "fsdp"))
-    gate_weight = lax.all_gather(w_gate[0], "fsdp", axis=0, tiled=True)
-    up_weight = lax.all_gather(w_up[0], "fsdp", axis=0, tiled=True)
-    down_weight = lax.all_gather(w_down[0], "fsdp", axis=1, tiled=True)
 
     hot = routes[0][:, :, None] == jnp.arange(expert_count, dtype=jnp.int32)[None, None, :]
     levels = jnp.sum(jnp.where(hot, priority[0][:, :, None] - LEVELS, 0), axis=1) + LEVELS
@@ -1006,43 +1258,76 @@
     ).astype(low)
 
     inputs = tokens[0].astype(jnp.float32)
-    normed, inv_one = rms_forward(inputs, g_attn)
+    inv_one = lax.rsqrt(jnp.mean(inputs * inputs, axis=-1, keepdims=True) + epsilon)
+    first_rows = jnp.concatenate([tokens[0], tags], axis=0)
     place_one = place.astype(jnp.int32).reshape(1)
     ready = ()
-    sum_parts, tag_parts, rope_parts = {}, {}, {}
+    sum_parts, tag_parts = {}, {}
 
     def lin_job(step, blocks):
-        made = lin_chunk(step, blocks[0], qkv_weight, place_one, tok_rows, ready)
-        lines = made[3].reshape(-1, EXTRA, tok_rows)
-        spots = (lines[:, 1] * 128.0 + lines[:, 2]).reshape(-1)
-        cosine, sine_part = rope_tables(spots, head_dim)
-        cosine, sine_part = cosine[:, 0], sine_part[:, 0]
-        tables = [
-            jnp.concatenate([cosine, cosine], axis=-1),
-            jnp.concatenate([-sine_part, sine_part], axis=-1),
-        ]
-
-        def keep(made):
-            nonlocal ready
-            ready = tuple(made[:2])
-            sum_parts[step], tag_parts[step] = made[2][:2], made[3]
-            rope_parts[step] = made[4:]
-
-        return [*made, *tables], keep
-
-    ring_gather([jnp.concatenate([normed.astype(low), tags], axis=0)], lin_job)
+        def function():
+            made = lin_chunk(
+                step, blocks(), qkv_weight, g_attn[None], place_one, tok_rows, ready
+            )
+            return made
+
+        return [], function
+
+    def lin_keep(step, made):
+        nonlocal ready
+        ready = tuple(made[:2])
+        sum_parts[step], tag_parts[step] = made[2][:2], made[3]
+
+    def other_core(array):
+        return (swap(array, "core"),)
+
+    rows_one = Gather(first_rows)
+
+    def to_other(*arrays):
+        return [swap(array, "fsdp") for array in arrays]
+
+    ((qkv_other, small_other),) = window([rows_one], loose=[([qkv_mine, small], to_other)])
+    small_full = joined(small, small_other, 1)
+    r_weight = small_full[:expert_count]
+    g_attn = small_full[expert_count].astype(jnp.float32)
+    g_ffn = small_full[expert_count + 1].astype(jnp.float32)
+    here = part == place // per_half
+    g_heads = jnp.where(here, small[expert_count + 2], small_other[expert_count + 2]).astype(
+        jnp.float32
+    )
+    g_query, g_key = g_heads[:head_dim], g_heads[head_dim : 2 * head_dim]
+    gain_col = g_attn[:, None]
+    qkv_weight = joined(qkv_mine, qkv_other, 0)
+
+    def expert_weights(_, *own):
+        return [lax.all_gather(w, "fsdp", axis=k, tiled=True) for w, k in zip(own, (0, 0, 1))]
+
+    made, expert_own = window(
+        [rows_one],
+        [lin_job(1, lambda: rows_one.now)],
+        loose=[([qkv_other, w_gate[0], w_up[0], w_down[0]], expert_weights)],
+    )
+    gate_weight, up_weight, down_weight = expert_own
+    lin_keep(1, made)
+    made, (qkv_pair,) = window(
+        [rows_one],
+        [lin_job(2, lambda: rows_one.now), ([qkv_weight], other_core)],
+    )
+    lin_keep(2, made)
+    made, (out_other,) = window(
+        [rows_one], [lin_job(3, lambda: rows_one.now)], loose=[([out_mine], to_other)]
+    )
+    out_weight = jnp.where(here, out_mine, out_other)
+    lin_keep(3, made)
+    lin_keep(LAST, lin_job(LAST, lambda: rows_one.chunks[LAST])[1]())
     lin, all_h_one = ready
-    q_lin, k_lin, v_lin = jnp.split(lin, 3, axis=1)
-    cos_full, sin_full = (
-        jnp.concatenate([rope_parts[step][k] for step in CHUNKS], axis=0) for k in range(2)
-    )
-    all_tags = jnp.concatenate([tag_parts[step] for step in CHUNKS], axis=0).reshape(
+    all_tags = jnp.concatenate([tag_parts[step] for step in WIDE_CHUNKS], axis=0).reshape(
         ctx_count, EXTRA, tok_rows
     )
 
     def token_sums(lines, jobs):
         total, done = sum_all(by_place(lines.reshape(-1, CHIPS, 2, tok_rows), 1), jobs)
-        return by_chunk(total, 1).reshape(-1, length, 1) / model_width, done
+        return by_chunk(total, 1).reshape(-1, length).T / model_width, done
 
     def rank_job(all_tags):
         mine, owner = all_tags[:, 0], all_tags[:, 3, :1]
@@ -1053,36 +1338,58 @@
         kept = (mine < LEVELS) & (ranks < capacity)
         return kept.astype(jnp.float32)[:, None], owner[:, 0].astype(jnp.int32)
 
-    square, _ = token_sums(
-        jnp.concatenate([sum_parts[step] for step in CHUNKS], axis=1),
-        [],
-    )
-    inv_query, inv_key = lax.rsqrt(square[0] + epsilon), lax.rsqrt(square[1] + epsilon)
-
-    def spin(matrix):
-        return jnp.concatenate([matrix[:, head_dim // 2 :], matrix[:, : head_dim // 2]], axis=-1)
-
-    q_normed = q_lin * inv_query * g_query
-    k_normed = k_lin * inv_key * g_key
-    q_rot = (q_normed * cos_full + spin(q_normed) * sin_full).astype(low)
-    k_rot = (k_normed * cos_full + spin(k_normed) * sin_full).astype(low)
-    v_low = v_lin.astype(low)
-
-    def attend_terms(step, queries, keys, values):
-        mixed, lse, *terms = attend_chunk(
-            step, queries, keys, values, out_weight, tok_rows, score_scale
-        )
-        return terms, [mixed, lse]
-
-    out_sum = Scatter(attend_terms, [q_rot, k_rot, v_low])
-    ((kept, owners),) = window([out_sum], [([all_tags], rank_job)])
-    for _ in range(FAR - 1):
-        window([out_sum], [])
+    def rope_job(all_tags):
+        spots = (all_tags[:, 1] * 128.0 + all_tags[:, 2]).reshape(-1)
+        return [table[:, 0] for table in rope_tables(spots, head_dim)]
+
+    square, ((cosine, sine_part),) = token_sums(
+        jnp.concatenate([sum_parts[step] for step in WIDE_CHUNKS], axis=1),
+        [([all_tags], rope_job)],
+    )
+    inverse = lax.rsqrt(square + epsilon)
+    gains = jnp.stack([g_query, g_key], axis=0)
+    q_rot, k_rot, v_low = rotate_rows(lin, inverse, gains, cosine, sine_part)
+
+    heads = {}
+
+    def attend_job(step):
+        return [q_rot, k_rot, v_low], lambda queries, keys, values: attend_chunk(
+            step, queries, keys, values, tok_rows, score_scale
+        )
+
+    def projected(step, made):
+        return pair_product(
+            made[2], swap(made[3], "core"), out_weight, out_pair, False, "project"
+        )
+
+    def first_job(queries, keys, values):
+        made = attend_job(FAR)[1](queries, keys, values)
+        return [*made, projected(FAR, made)]
+
+    (out_pair,) = other_core(out_weight)
+    grads_rows = Gather(cotangent[0])
+    (*heads[FAR], far_terms), heads[FAR - 1], (kept, owners) = window(
+        [grads_rows],
+        [([q_rot, k_rot, v_low], first_job), attend_job(FAR - 1), ([all_tags], rank_job)],
+    )
+
+    def out_terms(step, *parts):
+        return (far_terms if step == FAR else projected(step, parts)), None
+
+    out_sum = Scatter(out_terms)
+    for near in range(FAR - 1, -1, -1):
+        out_sum.inputs = heads[near]
+        jobs = [attend_job(near - 1)] if near else []
+        held = [([gate_weight], lambda weight: (weight,))] if near == 2 else []
+        made = window([out_sum], jobs + held)
+        if held:
+            (gate_weight,) = made[-1]
+        if near:
+            heads[near - 1] = made[0]
     mixed_low, lse = (
-        jnp.concatenate([out_sum.extras[step][k] for step in CHUNKS], axis=0) for k in range(2)
-    )
-    projected = out_sum.total
-    middle = inputs + projected
+        jnp.concatenate([heads[step][k] for step in CHUNKS], axis=0) for k in range(2)
+    )
+    middle = inputs + out_sum.total
 
     h_two_f, inv_two = rms_forward(middle, g_ffn)
     h_two = h_two_f.astype(low)
@@ -1090,11 +1397,14 @@
     filled = ()
     mix_terms, dx_terms = {}, {}
 
-    def expert_job(step, blocks):
-        made = expert_chunk(
+    rows_two = Gather(h_two)
+    window([rows_two])
+
+    def expert_job(step, h_blocks, g_blocks):
+        return [], lambda: expert_chunk(
             step,
-            blocks[0],
-            blocks[1],
+            h_blocks(),
+            g_blocks(),
             place_one,
             kept,
             r_weight,
@@ -1105,36 +1415,41 @@
             filled,
         )
 
-        def keep(made):
-            nonlocal filled
-            filled, terms = tuple(made[:5]), made[5:]
-            half = len(terms) // 2
-            mix_terms[step], dx_terms[step] = terms[:half], terms[half:]
-
-        return made, keep
-
-    ring_gather([h_two, cotangent[0]], expert_job)
-    act_low, gate_grad, up_grad, all_h_two, all_grads = filled
+    for step in list(range(1, FAR)) + [LAST]:
+        if step == LAST:
+            run = expert_job(step, lambda: rows_two.chunks[LAST], lambda: grads_rows.chunks[LAST])
+            made = run[1]()
+        else:
+            run = expert_job(step, lambda: rows_two.now, lambda: grads_rows.now)
+            (made,) = window([rows_two, grads_rows], [run])
+        filled, terms = tuple(made[:5]), made[5:]
+        if step == LAST:
+            mix_terms[0], mix_terms[FAR] = terms[:2], terms[2:4]
+            dx_terms[0], dx_terms[FAR] = terms[4:6], terms[6:]
+        else:
+            mix_terms[step], dx_terms[step] = terms[:2], terms[2:]
+    all_h_two, all_grads, act_low, gate_grad, up_grad = filled
 
     def wgrad(left, right):
         return (contract_rows(left, right).astype(low),)
+
+    def over_sequences(matrix, axis):
+        return lax.psum_scatter(matrix, "fsdp", scatter_dimension=axis, tiled=True)
 
     logits = contract_cols(h_two, r_weight)
     row_max = jnp.max(logits, axis=-1, keepdims=True)
     exps_raw = jnp.exp(logits - row_max)
     router_probs = exps_raw / jnp.sum(exps_raw, axis=-1, keepdims=True)
-    dx_sum = Scatter(lambda step: (dx_terms[step], []))
-    mix_sum = Scatter(lambda step: (mix_terms[step], []))
+    dx_sum = Scatter(lambda step: dx_terms[step])
+    mix_sum = Scatter(lambda step: mix_terms[step])
     ((gate_wgrad,),) = window([dx_sum, mix_sum], [([all_h_two, gate_grad], wgrad)])
+    s_gate = over_sequences(gate_wgrad, 0)
     ((up_wgrad,),) = window([dx_sum, mix_sum], [([all_h_two, up_grad], wgrad)])
-    window([dx_sum], [])
-    window([dx_sum], [])
+    s_up = over_sequences(up_wgrad, 0)
+    ((down_wgrad,),) = window([dx_sum], [([act_low, all_grads], wgrad)])
+    s_down = over_sequences(down_wgrad, 1)
+    window([dx_sum])
     hidden_sum = dx_sum.total
-
-    def over_sequences(matrix, axis):
-        return lax.psum_scatter(matrix, "fsdp", scatter_dimension=axis, tiled=True)
-
-    sums = [over_sequences(gate_wgrad, 0), over_sequences(up_wgrad, 0)]
 
     prob_grad = jnp.sum(hidden_sum[tok_rows : tok_rows + 3], axis=0)
     prob_grad = prob_grad.reshape(expert_count, tok_rows).T
@@ -1147,145 +1462,162 @@
 
     sofar = ()
 
+    q_sums = {}
+    rows_da = Gather(middle_grad.astype(low))
+
     def back_job(step, blocks):
-        made = attend_back_chunk(
+        return [], lambda: attend_back_chunk(
             step,
-            blocks[0],
+            blocks(),
             q_rot,
             lse,
             k_rot,
             v_low,
             out_weight,
+            lin,
+            gains,
+            cosine,
+            sine_part,
             tok_rows,
             score_scale,
             sofar,
-        )
-
-        def keep(made):
-            nonlocal sofar
-            sofar = tuple(made)
-
-        return made, keep
-
-    mix_step = mix_sum.job()
-    done = ring_gather(
-        [middle_grad.astype(low)],
-        back_job,
-        {2: [mix_step], 4: [([act_low, all_grads], wgrad)]},
-    )
-    mix_sum.take(done[2][0])
-    down_wgrad = done[4][0][0]
-    sums.append(over_sequences(down_wgrad, 1))
+            step == FAR,
+        )
+
+    def widen(array):
+        return (array.astype(jnp.float32),)
+
+    def narrow_job(h_two, logit_grad, ffn_gain_grad):
+        return (
+            jnp.concatenate(
+                [
+                    precise(h_two.astype(jnp.float32).T, logit_grad),
+                    ffn_gain_grad[:, None],
+                    jnp.zeros((model_width, HALF_THIN - expert_count - 1), jnp.float32),
+                ],
+                axis=1,
+            ),
+        )
+
+    besides = {0: [], 1: [mix_sum], 2: [], 3: []}
+    also = {1: [([h_two, logit_grad, ffn_gain_grad], narrow_job), ([s_gate], widen)]}
+    for step in range(FAR + 1):
+        if step == FAR:
+            *made, k_sums = back_job(step, lambda: rows_da.chunks[FAR])[1]()
+        else:
+            made, *wide = window(
+                [rows_da] + besides[step], [back_job(step, lambda: rows_da.now)] + also.get(step, [])
+            )
+            if step == 1:
+                (narrow,), (s_gate,) = wide
+        sofar, q_sums[step] = tuple(made[:4]), made[4]
     dq, all_branch, dk, dv = sofar
-    q_back = dq * cos_full - spin(dq) * sin_full
-    k_back = dk * cos_full - spin(dk) * sin_full
 
     def out_job(mixed_low, all_branch):
         return (contract_rows(mixed_low, all_branch),)
 
-    def router_job(h_two, logit_grad):
-        return (precise(h_two.astype(jnp.float32).T, logit_grad),)
-
-    along, ((out_wgrad,), (router_wgrad,), mixed) = token_sums(
+    own_rows = model_width // (2 * ctx_count)
+    part_one = part.astype(jnp.int32).reshape(1)
+
+    def value_job(all_h_one, dv):
+        return dense_chunk(
+            all_h_one, dv.astype(low), qkv_weight, (2 * head_dim, head_dim), gain_col, None,
+            part_one, own_rows,
+        )
+
+    along, ((v_kept, v_sent, v_term), mixed) = token_sums(
         jnp.stack(
+            [jnp.concatenate([q_sums[step][0] for step in CHUNKS], axis=0), k_sums[0]], axis=0
+        ),
+        [
+            ([all_h_one, dv], value_job),
+            mix_sum.job(),
+        ],
+    )
+    mix_sum.take(mixed)
+    layer_out = (middle + mix_sum.total).astype(low)
+    lin_grad, lin_mine, lin_theirs = lin_back_rows(dq, dk, dv, lin, inverse, along, tok_rows)
+    lin_theirs = swap(lin_theirs, "core")
+
+
+    def pick(blocks, index):
+        return lax.dynamic_index_in_dim(blocks, index, 1, False)
+
+    def dense_job(all_h_one, lin_grad, *narrow):
+        return dense_chunk(
+            all_h_one, lin_grad[:, : 2 * head_dim], qkv_weight, (0, 2 * head_dim), gain_col, narrow,
+            part_one, own_rows,
+        )
+
+    def out_swap_job(out_sent, dq, dk, lin):
+        gain_rows = jnp.stack(
             [
-                jnp.sum(q_back * g_query * q_lin, axis=-1),
-                jnp.sum(k_back * g_key * k_lin, axis=-1),
+                jnp.sum(
+                    grad * lin[:, k * head_dim : (k + 1) * head_dim] * inverse[:, k : k + 1], axis=0
+                )
+                for k, grad in enumerate((dq, dk))
             ],
             axis=0,
-        ),
+        )
+        gain_rows = (gain_rows / gains).reshape(2, 2, own_rows)
+        return swap(out_sent, "fsdp"), swap(pick(gain_rows, 1 - part), "fsdp"), pick(gain_rows, part)
+
+    def h_terms(step, lin_mine, lin_theirs):
+        return (
+            pair_product(lin_mine, lin_theirs, qkv_weight, qkv_pair, True, "h_terms", step),
+            None,
+        )
+
+    h_sum = Scatter(h_terms, [lin_mine, lin_theirs])
+    def swap_job(sent):
+        return (swap(sent, "fsdp"),)
+
+    def owners_job(payload):
+        blocks = payload.reshape(ctx_count, own_rows, -1)
+        return (lax.all_to_all(blocks, ("chip", "core"), 0, 0, tiled=True),)
+
+    (kept, sent), (s_down,), (v_got,) = window(
+        [h_sum],
+        [([all_h_one, lin_grad, narrow, v_term], dense_job), ([s_down], widen)],
+        loose=[([v_sent], swap_job)],
+    )
+    (got,), (out_wgrad,), (v_received,) = window(
+        [h_sum],
+        [([sent], swap_job), ([mixed_low, all_branch], out_job)],
+        loose=[([(v_kept + v_got.astype(jnp.float32)).astype(low)], owners_job)],
+    )
+    out_rows = out_wgrad.reshape(1, 2, own_rows, model_width)
+    (s_up,), (received,), (out_got, gain_got, gain_kept) = window(
+        [h_sum],
+        [([s_up], widen)],
+        loose=[
+            ([kept, got], lambda kept, got: owners_job(dense_sum(kept, got))),
+            ([pick(out_rows, 1 - part)[0].astype(low), dq, dk, lin], out_swap_job),
+        ],
+    )
+
+    def out_done_job(own, out_got, gain_kept, gain_got):
+        return own + out_got.astype(jnp.float32), gain_kept + gain_got
+
+    (v_received,), (received,), (d_out, gain_sum) = window(
+        [h_sum],
         [
-            ([mixed_low, all_branch], out_job),
-            ([h_two, logit_grad], router_job),
-            mix_sum.job(),
+            ([], lambda: (v_received,)),
+            ([], lambda: (received,)),
+            ([pick(out_rows, part)[0], out_got, gain_kept, gain_got], out_done_job),
         ],
     )
-    mix_sum.take(mixed)
-    layer_out = (middle + mix_sum.total).astype(low)
-    q_lin_grad = inv_query * (q_back * g_query) - q_lin * inv_query**3 * along[0]
-    k_lin_grad = inv_key * (k_back * g_key) - k_lin * inv_key**3 * along[1]
-    query_gain_grad = jnp.sum(q_back * q_lin * inv_query, axis=0)
-    key_gain_grad = jnp.sum(k_back * k_lin * inv_key, axis=0)
-    lin_grad = jnp.concatenate([q_lin_grad, k_lin_grad, dv], axis=1).astype(low)
-
-    own_rows = model_width // (2 * ctx_count)
-
-    def pick(blocks, index):
-        return lax.dynamic_index_in_dim(blocks, index, 1, False)
-
-    def split_low(values):
-        high = values.astype(low)
-        return jnp.concatenate([high, (values - high.astype(jnp.float32)).astype(low)], axis=-1)
-
-    wide_cols = 3 * head_dim
-    thin_cols = expert_count + 2
-    source_ids = by_place(owners.reshape(CHIPS, 2), 0)
-
-    def dense_job(all_h_one, lin_grad, router_wgrad, ffn_gain_grad):
-        wgrad = contract_rows(all_h_one, lin_grad)
-        attn_term = jnp.sum(wgrad * qkv_weight.astype(jnp.float32), axis=1) / g_attn
-        thin = jnp.concatenate(
-            [router_wgrad, ffn_gain_grad[:, None], attn_term[:, None]], axis=1
-        )
-
-        def by_owner(matrix):
-            return matrix.reshape(ctx_count, 2, own_rows, -1)
-
-        wide, thin = by_owner(wgrad), by_owner(thin)
-        sent = jnp.concatenate(
-            [pick(wide, 1 - part).astype(low), split_low(pick(thin, 1 - part))], axis=-1
-        )
-        return sent, pick(wide, part), pick(thin, part)
-
-    def pair_job(sent, wide, thin):
-        got = swap(sent, "fsdp").astype(jnp.float32)
-        wide = wide + got[..., :wide_cols]
-        thin = thin + (
-            got[..., wide_cols : wide_cols + thin_cols] + got[..., wide_cols + thin_cols :]
-        )
-        payload = jnp.concatenate([wide.astype(low), split_low(thin)], axis=-1)
-        return (payload[source_ids],)
-
-    out_rows = out_wgrad.reshape(1, 2, own_rows, model_width)
-    d_out = pick(out_rows, part)[0] + swap(pick(out_rows, 1 - part)[0].astype(low), "fsdp").astype(
-        jnp.float32
-    )
-    gain_rows = jnp.stack([query_gain_grad, key_gain_grad], axis=0).reshape(2, 2, own_rows)
-    gain_rows = pick(gain_rows, part) + swap(pick(gain_rows, 1 - part), "fsdp")
-    d_qgain, d_kgain = gain_rows[0], gain_rows[1]
-
-    def h_terms(step, lin_grad):
-        first, count = CHUNKS[step]
-        rows = lin_grad[2 * first * tok_rows : 2 * (first + count) * tok_rows]
-        term = contract_cols(rows, qkv_weight).astype(low)
-        return [term[k * tok_rows : (k + 1) * tok_rows] for k in range(2 * count)], []
-
-    h_sum = Scatter(h_terms, [lin_grad])
-    (made,) = window(
-        [h_sum], [([all_h_one, lin_grad, router_wgrad, ffn_gain_grad], dense_job)]
-    )
-    ((payload,),) = window([h_sum], [(made, pair_job)])
-    (sums,) = window(
-        [h_sum], [(sums, lambda *sums: [total.astype(jnp.float32) for total in sums])]
-    )
-    received = exchange_all(payload)
-    window([h_sum], [])
     h_grad = h_sum.total
-    s_gate, s_up, s_down = (total[None] for total in sums)
+    d_qgain, d_kgain = gain_sum[0], gain_sum[1]
+    s_gate, s_up, s_down = s_gate[None], s_up[None], s_down[None]
     in_norm_grad, _ = rms_backward(inputs, inv_one, g_attn, h_grad)
     input_grad = (middle_grad + in_norm_grad).astype(low)
-    received = received.reshape(ctx_count, own_rows, -1)
-    here_order = (
-        source_ids.reshape(1, -1) == jnp.arange(ctx_count, dtype=jnp.int32)[:, None]
-    ).astype(jnp.int32)
-    back_ids = jnp.sum(here_order * jnp.arange(ctx_count, dtype=jnp.int32)[None, :], axis=1)
-    dense = received[..., :wide_cols][back_ids].astype(jnp.float32)
-    dense = dense.reshape(ctx_count, own_rows, 3, head_dim)
     d_query, d_key, d_value = (
-        dense[:, :, i].transpose(1, 0, 2).reshape(own_rows, model_width) for i in range(3)
-    )
-    thin_sum = jnp.sum(received[..., wide_cols:].astype(jnp.float32), axis=0)
-    thin_sum = thin_sum[:, :thin_cols] + thin_sum[:, thin_cols:]
+        columns.transpose(1, 0, 2).reshape(own_rows, model_width).astype(jnp.float32)
+        for columns in (received[:, :, :head_dim], received[:, :, head_dim : 2 * head_dim], v_received)
+    )
+    thin_sum = jnp.sum(received[:, :, 2 * head_dim :].astype(jnp.float32), axis=0)
+    thin_sum = thin_sum[:, :HALF_THIN] + thin_sum[:, HALF_THIN:]
     d_router = thin_sum[:, :expert_count]
     d_ffn, d_attn = thin_sum[:, expert_count], thin_sum[:, expert_count + 1]
     return (

time: 782 us -> 692 us (0.88)
  Pallas kernels: 192 us -> 234 us
  waiting for transfers between devices: 169 us -> 134 us
  other arithmetic: 105 us -> 74.7 us
  local copies, waits for them, and re-layouts: 91.6 us -> 67.5 us
  starting transfers between devices: 131 us -> 110 us
  matrix products: 65.9 us -> 45.2 us
    ppermute x73 -> x61, waiting for transfers between devices: 65.8 us -> 22.2 us  [swap(): return lax.ppermute(array, axis, [(0, 1), (1, 0)])]
    ppermute x85 -> x64, starting transfers between devices: 109 us -> 66.4 us  [shift(): return lax.ppermute(array, 'chip', pairs)]
    pallas_call x15 -> x28, Pallas kernels: 155 us -> 192 us  [call(): pl.pallas_call(kernel, grid=grid, in_specs=ins + [pl.BlockSpec(memory_spa...]
    convert_element_type x38 -> x22, other arithmetic: 59 us -> 43.6 us  [the longest x12 25.9 us: take(): (term(1) + behind).astype(jnp.bfloat16)]
    all_to_all x0 -> x2, starting transfers between devices: none -> 12.4 us  [owners_job(): return (lax.all_to_all(blocks, ('chip', 'core'), 0, 0, tiled=True),)]
    dot_general x5 -> x4, matrix products: 55.7 us -> 43.3 us  [contract_rows(): lax.dot_general(left, right, (((0,), (0,)), ((), ())), preferred_element_...]
    ppermute x0 -> x8, starting transfers between devices: none -> 10.6 us  [heard(): return lax.ppermute(both, ('chip', 'core'), pairs)]
    ppermute x85 -> x64, waiting for transfers between devices: 92 us -> 100 us  [shift(): return lax.ppermute(array, 'chip', pairs)]
  transfers between devices with their start and end apart: 164 -> 141, of which waited for: 46 -> 50; matrix products, arithmetic and copies ran while one was open for 30% -> 20% of each run, Pallas kernels for 23% -> 31%
where the time goes in v3:
time: 692 us; the launch traced here: 682 us
  Pallas kernels  234 us (34%)
  waiting for transfers between devices  134 us (19%)
  starting transfers between devices  110 us (16%)
  other arithmetic  74.7 us (11%)
  local copies, waits for them, and re-layouts  67.5 us (10%)
  matrix products  45.2 us (7%)
  between operations  16.4 us (2%)
    pallas_call x28, Pallas kernels, call(): pl.pallas_call(kernel, grid=grid, in_specs=ins + [pl.BlockSpec(memory_spa...  192 us
    ppermute x64, waiting for transfers between devices, shift(): return lax.ppermute(array, 'chip', pairs)  100 us
    ppermute x64, starting transfers between devices, shift(): return lax.ppermute(array, 'chip', pairs)  66.4 us
    dot_general x4, matrix products, contract_rows(): lax.dot_general(left, right, (((0,), (0,)), ((), ())), preferred_element_...  43.3 us
    pallas_call x5, Pallas kernels, attend_back_chunk(): pl.pallas_call(kernel, grid=(1,), in_specs=ins + [whole(part) for part in...  42.1 us
    unnamed x231, local copies, waits for them, and re-layouts  31 us
    convert_element_type x12, other arithmetic, take(): (term(1) + behind).astype(jnp.bfloat16)  25.9 us
    ppermute x61, waiting for transfers between devices, swap(): return lax.ppermute(array, axis, [(0, 1), (1, 0)])  22.2 us
  transfers between devices with their start and end apart: 141, of which 50 were waited for; matrix products, arithmetic and copies ran while one was open for 20% of the time, Pallas kernels for 31%

profile of v3, /device:TPU:8, one launch (start us, length us, event | category | flops | bytes accessed | tf_op | source)
XLA Modules:
  0.0 681.7 jit_solution(808973558688661490)
XLA Ops:
  19.0 12.1 %collective-permute-done.refs_2_ = bf16[136,2048]{1,0:T(8,128)(2,1)S(1)} collective-permute-done((bf16[136,2048]{1,0:T(8,128)(2,1)S(1)}, bf16[136,2048]{1,0:T(8,128)(2,1)S(1)}, u32[]{:S(2)}, u32[]{:S(2)}) %collective-permute-start) | collective-permute-done | bytes 557088 | tf_op jit(solution)/shard_map/ppermute | solution.py:461
  183.9 6.5 collective-permute-done.40
  193.6 9.2 %collective-permute-done.43.refs_2_ = bf16[128,2048]{1,0:T(8,128)(2,1)} collective-permute-done((bf16[128,2048]{1,0:T(8,128)(2,1)S(1)}, bf16[128,2048]{1,0:T(8,128)(2,1)}, u32[]{:S(2)}, u32[]{:S(2)}) %collective-permute-start.43) | collective-permute-done | bytes 524320 | tf_op jit(solution)/shard_map/ppermute | solution.py:461
  213.7 24.3 %expert.4 = (bf16[2048,2048]{1,0:T(8,128)(2,1)}, bf16[2048,2048]{1,0:T(8,128)(2,1)}, bf16[2048,1024]{1,0:T(8,128)(2,1)}, bf16[2048,1024]{1,0:T(8,128)(2,1)}, bf1...) custom-call(bf16[128,2048]{1,0:T(8,128)(2,1)} %collective-permute-do, ...), custom_call_target="tpu_custom_call" | custom-call | tf_op jit(solution)/shard_map/expert/pallas_call | solution.py:611
  243.8 24.1 %expert.5 = (bf16[2048,2048]{1,0:T(8,128)(2,1)}, bf16[2048,2048]{1,0:T(8,128)(2,1)}, bf16[2048,1024]{1,0:T(8,128)(2,1)}, bf16[2048,1024]{1,0:T(8,128)(2,1)}, bf1...) custom-call(bf16[128,2048]{1,0:T(8,128)(2,1)} %collective-permute-do, ...), custom_call_target="tpu_custom_call", output_to_operand_aliasing={{0}: (17, {}), {1}: (18, {}), {2}: (19, {}), {3}: (20, {}),... | custom-call | tf_op jit(solution)/shard_map/expert/pallas_call | solution.py:611
  276.8 24.0 %expert.6 = (bf16[2048,2048]{1,0:T(8,128)(2,1)}, bf16[2048,2048]{1,0:T(8,128)(2,1)}, bf16[2048,1024]{1,0:T(8,128)(2,1)}, bf16[2048,1024]{1,0:T(8,128)(2,1)}, bf1...) custom-call(bf16[128,2048]{1,0:T(8,128)(2,1)} %copy-done.45, ...), custom_call_target="tpu_custom_call", output_to_operand_aliasing={{0}: (17, {}), {1}: (18, {}), {2}: (19, {}), {3}: (20, {}),... | custom-call | tf_op jit(solution)/shard_map/expert/pallas_call | solution.py:611
  307.8 24.0 %expert.7 = (bf16[2048,2048]{1,0:T(8,128)(2,1)}, bf16[2048,2048]{1,0:T(8,128)(2,1)}, bf16[2048,1024]{1,0:T(8,128)(2,1)}, bf16[2048,1024]{1,0:T(8,128)(2,1)}, bf1...) custom-call(bf16[128,2048]{1,0:T(8,128)(2,1)} %copy-done.25, ...), custom_call_target="tpu_custom_call", output_to_operand_aliasing={{0}: (17, {}), {1}: (18, {}), {2}: (19, {}), {3}: (20, {}),... | custom-call | tf_op jit(solution)/shard_map/expert/pallas_call | solution.py:611
  344.3 12.8 %convolution_convert_fusion.2 = bf16[2048,1024]{1,0:T(8,128)(2,1)} fusion(bf16[2048,2048]{1,0:T(8,128)(2,1)} %get-tuple-element.777, bf16[2048,1024]{1,0:T(8,128)(2,1)S(1)} %copy-done.15), kind=kOutput, calls=%fused_computation.3 | convolution fusion | flops 8592031744 | bytes 16777216 | tf_op jit(solution)/shard_map/dot_general | solution.py:39
  368.2 12.8 %convolution_convert_fusion.1 = bf16[2048,1024]{1,0:T(8,128)(2,1)} fusion(bf16[2048,2048]{1,0:T(8,128)(2,1)} %get-tuple-element.777, bf16[2048,1024]{1,0:T(8,128)(2,1)S(1)} %copy-done.16), kind=kOutput, calls=%fused_computation.2 | convolution fusion | flops 8592031744 | bytes 16777216 | tf_op jit(solution)/shard_map/dot_general | solution.py:39
  381.1 9.0 %collective-permute-done.83 = bf16[128,2048]{1,0:T(8,128)(2,1)} collective-permute-done((bf16[128,2048]{1,0:T(8,128)(2,1)}, bf16[128,2048]{1,0:T(8,128)(2,1)}, u32[]{:S(2)}, u32[]{:S(2)}) %collective-permute-start.83) | collective-permute-done | bytes 524320 | tf_op jit(solution)/shard_map/ppermute | solution.py:461
  396.9 13.0 %convolution_convert_fusion = bf16[1024,2048]{1,0:T(8,128)(2,1)} fusion(bf16[2048,1024]{1,0:T(8,128)(2,1)S(1)} %copy-done.14, bf16[2048,2048]{1,0:T(8,128)(2,1)} %get-tuple-element.790), kind=kOutput, calls=%fused_computation.1 | convolution fusion | flops 8592031744 | bytes 16777216 | tf_op jit(solution)/shard_map/dot_general | solution.py:39
  418.0 11.5 %collective-permute-done.89 = bf16[136,2048]{1,0:T(8,128)(2,1)} collective-permute-done((bf16[136,2048]{1,0:T(8,128)(2,1)}, bf16[136,2048]{1,0:T(8,128)(2,1)}, u32[]{:S(2)}, u32[]{:S(2)}) %collective-permute-start.89) | collective-permute-done | bytes 557088 | tf_op jit(solution)/shard_map/ppermute | solution.py:461
  440.0 5.8 attend_back.5
  461.8 9.3 %attend_back.6 = (f32[2048,128]{1,0:T(8,128)}, bf16[2048,2048]{1,0:T(8,128)(2,1)}, f32[2048,128]{1,0:T(8,128)}, f32[2048,128]{1,0:T(8,128)}, f32[8,512]{1,0:T(8,128)}) custom-call(bf16[128,2048]{1,0:T(8,128)(2,1)} %collective-permute-done.93.refs_0_, ...), custom_call_target="tpu_custom_call", output_to_operand_aliasing={{2}: (13, {}), {3}: (14, {}), {0}: (15, {}), {1}: (16, {})} | custom-call | tf_op jit(solution)/shard_map/attend_back/pallas_call | solution.py:868
  480.6 9.2 %attend_back.7 = (f32[2048,128]{1,0:T(8,128)}, bf16[2048,2048]{1,0:T(8,128)(2,1)}, f32[2048,128]{1,0:T(8,128)}, f32[2048,128]{1,0:T(8,128)}, f32[8,512]{1,0:T(8,128)}) custom-call(bf16[128,2048]{1,0:T(8,128)(2,1)} %collective-permute-done.96.refs_0_, ...), custom_call_target="tpu_custom_call", output_to_operand_aliasing={{2}: (13, {}), {3}: (14, {}), {0}: (15, {}), {1}: (16, {})} | custom-call | tf_op jit(solution)/shard_map/attend_back/pallas_call | solution.py:868
  498.3 10.0 %attend_back.8 = (f32[2048,128]{1,0:T(8,128)}, bf16[2048,2048]{1,0:T(8,128)(2,1)}, f32[2048,128]{1,0:T(8,128)}, f32[2048,128]{1,0:T(8,128)}, f32[8,512]{1,0:T(8,128)}) custom-call(bf16[128,2048]{1,0:T(8,128)(2,1)} %copy-done.51, bf16[128,2048]{1,0:T(8,128)(2,1)} %copy-done.83, ...), custom_call_target="tpu_custom_call", output_to_operand_aliasing={{2}: (13, {}), {3}: (14, {}), {0}: (15, {}), {1}: (16, {})} | custom-call | tf_op jit(solution)/shard_map/attend_back/pallas_call | solution.py:868
  516.9 7.7 %attend_back.9 = (f32[2048,128]{1,0:T(8,128)}, bf16[2048,2048]{1,0:T(8,128)(2,1)}, f32[2048,128]{1,0:T(8,128)}, f32[2048,128]{1,0:T(8,128)}, f32[8,256]{1,0:T(8,128)}, /*index=5*/f32[8,2048]{1,0:T(8,128)}) custom-call(bf16[128,2048]{1,0:T(8,128)(2,1)} %copy-done.52, ...), custom_call_target="tpu_custom_call", output_to_operand_aliasing={{2}: (14, {}), {3}: (15, {}), {0}: (16, {}), {1}: (17, {})} | custom-call | tf_op jit(solution)/shard_map/attend_back/pallas_call | solution.py:868
  532.9 8.2 %collective-permute-done.112 = f32[2,8,2,128]{3,1,2,0:T(8,128)S(1)} collective-permute-done((f32[2,8,2,128]{3,1,2,0:T(8,128)S(1)}, f32[2,8,2,128]{3,1,2,0:T(8,128)S(1)}, u32[]{:S(2)}, u32[]{:S(2)}) %collective-permute-start.112) | collective-permute-done | bytes 16416 | tf_op jit(solution)/shard_map/ppermute | solution.py:578
  544.7 8.7 %dense.2 = (f32[1024,128]{1,0:T(8,128)S(1)}, bf16[1024,128]{1,0:T(8,128)(2,1)S(1)}, f32[2048,1]{1,0:T(8,128)S(1)}) custom-call(s32[1]{0:T(128)} %bitcast.32.part_ref, bf16[2048,2048]{1,0:T(8,128)(2,1)} %get-tuple-element.920.h_ref, bf16[2048,128]{1,0:T(8,128)(2,1)} %convert_element_type.505.grads_ref, ...), custom_call_target="tpu_custom_call" | custom-call | tf_op jit(solution)/shard_map/dense/pallas_call | solution.py:611
  557.3 6.3 lin_back.1
  580.9 10.2 %dense.3 = (f32[1024,384]{1,0:T(8,128)S(1)}, bf16[1024,384]{1,0:T(8,128)(2,1)S(1)}) custom-call(s32[1]{0:T(128)} %bitcast.32.part_ref, bf16[2048,2048]{1,0:T(8,128)(2,1)} %get-tuple-element.920.h_ref, bf16[2048,256]{1,0:T(8,128)(2,1)} %slice.593.grads_ref, bf16[2048,384]{1,0:T(8,128)(2,1)} %maximum_select_fusion.refs_4_.weight_ref.left_weight_ref, ...), custom_call_target="tpu_custom_call" | custom-call | tf_op jit(solution)/shard_map/dense/pallas_call | solution.py:611
  598.0 6.6 all-to-all-start
  624.1 5.8 all-to-all-start.1
  649.3 10.0 %collective-permute-done.131 = bf16[128,2048]{1,0:T(8,128)(2,1)S(1)} collective-permute-done((bf16[128,2048]{1,0:T(8,128)(2,1)S(1)}, bf16[128,2048]{1,0:T(8,128)(2,1)S(1)}, u32[]{:S(2)}, u32[]{:S(2)}) %collective-permute-start.131) | collective-permute-done | bytes 524320 | tf_op jit(solution)/shard_map/ppermute | solution.py:461
  (713 shorter events, 384.2 us)
Async XLA Ops:
  7.2 139.8 %all-gather.4.cloned.1.call-start = ((), (), s32[]{:S(2)}) async-start(), calls=%async_computation.5 | async-start | bytes 6291456 | tf_op jit(solution)/shard_map/all_gather | solution.py:1303
  35.7 174.7 %all-gather.6.cloned.1.call-start = ((), (), s32[]{:S(2)}) async-start(), calls=%async_computation.6 | async-start | bytes 6291456 | tf_op jit(solution)/shard_map/all_gather | solution.py:1303
  85.6 128.2 %all-gather.8.cloned.1.call-start = ((), (), s32[]{:S(2)}) async-start(), calls=%async_computation.7 | async-start | bytes 6291456 | tf_op jit(solution)/shard_map/all_gather | solution.py:1303
  149.2 300.5 %reduce-scatter.4.cloned.1.call-start = ((), (), s32[]{:S(2)}) async-start(), calls=%async_computation.8 | async-start | bytes 6291456 | tf_op jit(solution)/shard_map/reduce_scatter | solution.py:1437
  205.3 32.8 %collective-permute-start.46 = (bf16[128,2048]{1,0:T(8,128)(2,1)}, bf16[128,2048]{1,0:T(8,128)(2,1)}, u32[]{:S(2)}, u32[]{:S(2)}) collective-permute-start(bf16[128,2048]{1,0:T(8,128)(2,1)} %collective-permute-done.43.refs_2_), channel_id=1, source_target_pairs={{0,8},{8,16},{16,24},{24,28},{28,20},{20,12},{12,4},{4,0},{1,9},{9... | collective-permute-start | bytes 1572872 | tf_op jit(solution)/shard_map/ppermute | solution.py:461
  206.5 31.6 %collective-permute-start.47 = (bf16[128,2048]{1,0:T(8,128)(2,1)}, bf16[128,2048]{1,0:T(8,128)(2,1)}, u32[]{:S(2)}, u32[]{:S(2)}) collective-permute-start(bf16[128,2048]{1,0:T(8,128)(2,1)} %collective-permute-done.44.refs_0_), channel_id=1, source_target_pairs={{0,4},{8,0},{16,8},{24,16},{28,24},{20,28},{12,20},{4,12},{1,5},{9... | collective-permute-start | bytes 1572872 | tf_op jit(solution)/shard_map/ppermute | solution.py:461
  207.6 30.5 %collective-permute-start.50 = (bf16[128,2048]{1,0:T(8,128)(2,1)}, bf16[128,2048]{1,0:T(8,128)(2,1)}, u32[]{:S(2)}, u32[]{:S(2)}) collective-permute-start(bf16[128,2048]{1,0:T(8,128)(2,1)} %collective-permute-done.25.refs_6_), channel_id=1, source_target_pairs={{0,8},{8,16},{16,24},{24,28},{28,20},{20,12},{12,4},{4,0},{1,9},{9... | collective-permute-start | bytes 1572872 | tf_op jit(solution)/shard_map/ppermute | solution.py:461
  208.5 29.6 %collective-permute-start.51 = (bf16[128,2048]{1,0:T(8,128)(2,1)}, bf16[128,2048]{1,0:T(8,128)(2,1)}, u32[]{:S(2)}, u32[]{:S(2)}) collective-permute-start(bf16[128,2048]{1,0:T(8,128)(2,1)} %collective-permute-done.26.refs_4_), channel_id=1, source_target_pairs={{0,4},{8,0},{16,8},{24,16},{28,24},{20,28},{12,20},{4,12},{1,5},{9... | collective-permute-start | bytes 1572872 | tf_op jit(solution)/shard_map/ppermute | solution.py:461
  239.2 28.7 %collective-permute-start.54 = (bf16[128,2048]{1,0:T(8,128)(2,1)}, bf16[128,2048]{1,0:T(8,128)(2,1)S(1)}, u32[]{:S(2)}, u32[]{:S(2)}) collective-permute-start(bf16[128,2048]{1,0:T(8,128)(2,1)} %collective-permute-done.46.refs_2_), channel_id=1, source_target_pairs={{0,8},{8,16},{16,24},{24,28},{28,20},{20,12},{12,4},{4,0},{1,9},{9... | collective-permute-start | bytes 1572872 | tf_op jit(solution)/shard_map/ppermute | solution.py:461
  240.7 27.3 %collective-permute-start.55 = (bf16[128,2048]{1,0:T(8,128)(2,1)}, bf16[128,2048]{1,0:T(8,128)(2,1)S(1)}, u32[]{:S(2)}, u32[]{:S(2)}) collective-permute-start(bf16[128,2048]{1,0:T(8,128)(2,1)} %collective-permute-done.47.refs_0_), channel_id=1, source_target_pairs={{0,4},{8,0},{16,8},{24,16},{28,24},{20,28},{12,20},{4,12},{1,5},{9... | collective-permute-start | bytes 1572872 | tf_op jit(solution)/shard_map/ppermute | solution.py:461
  241.8 26.2 %collective-permute-start.58 = (bf16[128,2048]{1,0:T(8,128)(2,1)}, bf16[128,2048]{1,0:T(8,128)(2,1)S(1)}, u32[]{:S(2)}, u32[]{:S(2)}) collective-permute-start(bf16[128,2048]{1,0:T(8,128)(2,1)} %collective-permute-done.50.refs_6_), channel_id=1, source_target_pairs={{0,8},{8,16},{16,24},{24,28},{28,20},{20,12},{12,4},{4,0},{1,9},{9... | collective-permute-start | bytes 1572872 | tf_op jit(solution)/shard_map/ppermute | solution.py:461
  271.4 29.5 %collective-permute-start.62 = (bf16[64,2048]{1,0:T(8,128)(2,1)}, bf16[64,2048]{1,0:T(8,128)(2,1)}, u32[]{:S(2)}, u32[]{:S(2)}) collective-permute-start(bf16[64,2048]{1,0:T(8,128)(2,1)} %slice.519), channel_id=1, source_target_pairs={{0,8},{8,16},{16,24},{24,28},{28,20},{20,12},{12,4},{4,0},{1,9},{9... | collective-permute-start | bytes 786440 | tf_op jit(solution)/shard_map/ppermute | solution.py:461
  272.9 28.0 %collective-permute-start.63 = (bf16[64,2048]{1,0:T(8,128)(2,1)}, bf16[64,2048]{1,0:T(8,128)(2,1)}, u32[]{:S(2)}, u32[]{:S(2)}) collective-permute-start(bf16[64,2048]{1,0:T(8,128)(2,1)} %slice.520), channel_id=1, source_target_pairs={{0,4},{8,0},{16,8},{24,16},{28,24},{20,28},{12,20},{4,12},{1,5},{9... | collective-permute-start | bytes 786440 | tf_op jit(solution)/shard_map/ppermute | solution.py:461
  273.8 27.1 %collective-permute-start.66 = (bf16[64,2048]{1,0:T(8,128)(2,1)}, bf16[64,2048]{1,0:T(8,128)(2,1)}, u32[]{:S(2)}, u32[]{:S(2)}) collective-permute-start(bf16[64,2048]{1,0:T(8,128)(2,1)} %slice.521), channel_id=1, source_target_pairs={{0,8},{8,16},{16,24},{24,28},{28,20},{20,12},{12,4},{4,0},{1,9},{9... | collective-permute-start | bytes 786440 | tf_op jit(solution)/shard_map/ppermute | solution.py:461
  357.2 214.3 %reduce-scatter.6.cloned.1.call-start = ((), (), s32[]{:S(2)}) async-start(), calls=%async_computation.9 | async-start | bytes 6291456 | tf_op jit(solution)/shard_map/reduce_scatter | solution.py:1437
  364.2 27.1 %collective-permute-start.80 = (bf16[136,2048]{1,0:T(8,128)(2,1)}, bf16[136,2048]{1,0:T(8,128)(2,1)}, u32[]{:S(2)}, u32[]{:S(2)}) collective-permute-start(bf16[136,2048]{1,0:T(8,128)(2,1)} %get-tuple-element.769), channel_id=1, source_target_pairs={{0,8},{8,16},{16,24},{24,28},{28,20},{20,12},{12,4},{4,0},{1,9},{9... | collective-permute-start | bytes 1671176 | tf_op jit(solution)/shard_map/ppermute | solution.py:461
  365.7 25.6 %collective-permute-start.81 = (bf16[136,2048]{1,0:T(8,128)(2,1)}, bf16[136,2048]{1,0:T(8,128)(2,1)}, u32[]{:S(2)}, u32[]{:S(2)}) collective-permute-start(bf16[136,2048]{1,0:T(8,128)(2,1)} %get-tuple-element.770), channel_id=1, source_target_pairs={{0,4},{8,0},{16,8},{24,16},{28,24},{20,28},{12,20},{4,12},{1,5},{9... | collective-permute-start | bytes 1671176 | tf_op jit(solution)/shard_map/ppermute | solution.py:461
  381.1 28.9 %collective-permute-start.88 = (bf16[272,2048]{1,0:T(8,128)(2,1)}, bf16[272,2048]{1,0:T(8,128)(2,1)}, u32[]{:S(2)}, u32[]{:S(2)}) collective-permute-start(bf16[272,2048]{1,0:T(8,128)(2,1)} %get-tuple-element.788), channel_id=1, source_target_pairs={{0,2},{2,0},{1,3},{3,1},{4,6},{6,4},{5,7},{7,5},{8,10},{10,8},{9,1... | collective-permute-start | bytes 3342344 | tf_op jit(solution)/shard_map/ppermute | solution.py:456
  410.0 205.8 %reduce-scatter.8.cloned.1.call-start = ((), (), s32[]{:S(2)}) async-start(), calls=%async_computation.10 | async-start | bytes 6291456 | tf_op jit(solution)/shard_map/reduce_scatter | solution.py:1437
  496.0 34.7 %collective-permute-start.118 = (bf16[128,2048]{1,0:T(8,128)(2,1)}, bf16[128,2048]{1,0:T(8,128)(2,1)S(1)}, u32[]{:S(2)}, u32[]{:S(2)}) collective-permute-start(bf16[128,2048]{1,0:T(8,128)(2,1)} %get-tuple-element.897), channel_id=1, source_target_pairs={{0,2},{2,0},{1,3},{3,1},{4,6},{6,4},{5,7},{7,5},{8,10},{10,8},{9,1... | collective-permute-start | bytes 1572872 | tf_op jit(solution)/shard_map/ppermute | solution.py:456
  526.3 28.1 %collective-permute-start.116 = (bf16[128,2048]{1,0:T(8,128)(2,1)}, bf16[128,2048]{1,0:T(8,128)(2,1)S(1)}, u32[]{:S(2)}, u32[]{:S(2)}) collective-permute-start(bf16[128,2048]{1,0:T(8,128)(2,1)} %get-tuple-element.894), channel_id=1, source_target_pairs={{0,8},{8,16},{16,24},{24,28},{28,20},{20,12},{12,4},{4,0},{1,9},{9... | collective-permute-start | bytes 1572872 | tf_op jit(solution)/shard_map/ppermute | solution.py:461
  527.2 27.2 %collective-permute-start.117 = (bf16[128,2048]{1,0:T(8,128)(2,1)}, bf16[128,2048]{1,0:T(8,128)(2,1)S(1)}, u32[]{:S(2)}, u32[]{:S(2)}) collective-permute-start(bf16[128,2048]{1,0:T(8,128)(2,1)} %get-tuple-element.895), channel_id=1, source_target_pairs={{0,4},{8,0},{16,8},{24,16},{28,24},{20,28},{12,20},{4,12},{1,5},{9... | collective-permute-start | bytes 1572872 | tf_op jit(solution)/shard_map/ppermute | solution.py:461
  598.0 26.1 %all-to-all-start = ((bf16[16,64,128]{2,1,0:T(8,128)(2,1)}), bf16[16,64,128]{2,1,0:T(8,128)(2,1)S(1)}, u32[]{:S(2)}, u32[]{:S(2)}) async-start(bf16[16,64,128]{2,1,0:T(8,128)(2,1)} %bitcast.43), calls=%async_computation.3 | async-start | bytes 524288 | tf_op jit(solution)/shard_map/all_to_all | solution.py:1577
  624.1 37.2 %all-to-all-start.1 = ((bf16[16,64,384]{2,1,0:T(8,128)(2,1)}), bf16[16,64,384]{2,1,0:T(8,128)(2,1)S(1)}, u32[]{:S(2)}, u32[]{:S(2)}) async-start(bf16[16,64,384]{2,1,0:T(8,128)(2,1)} %bitcast.44), calls=%async_computation.4 | async-start | bytes 1572864 | tf_op jit(solution)/shard_map/all_to_all | solution.py:1577
  (222 other events, 2169.8 us)
Sparse Core Ops, SparseCore 0:
  35.8 61.3 all-gather.3
  98.8 56.5 all-gather.5
  157.0 56.7 all-gather.7
  357.3 54.2 reduce-scatter.3
  414.5 54.3 reduce-scatter.5
  496.1 52.0 reduce-scatter.7

commit v4 on v3

--- a/solution.py
+++ b/solution.py
@@ -480,38 +480,44 @@
 
 
 class Gather:
-    def __init__(self, block):
-        self.ahead = self.behind = block
+    def __init__(self, block, far_by=0):
+        self.moving = {1: block, -1: block}
         self.cut = block.shape[0] // 2 // 8 * 8
+        self.far_by = far_by
         self.fresh = [block]
         self.step = 0
         self.chunks = {}
 
     def job(self):
-        ahead, behind = self.ahead, self.behind
-        if self.step + 1 == FAR:
-            ahead, behind = ahead[: self.cut], behind[self.cut :]
-
-        def function(ahead, behind, *fresh):
-            ahead, behind = shift(ahead, 1), shift(behind, -1)
-            self.now = [x for block in fresh for x in (block, swap(block, "core"))]
-            return [ahead, behind, *self.now]
-
-        return [ahead, behind, *self.fresh], function
+        moving, ways = self.moving, [1, -1]
+        if self.step + 1 == FAR and self.far_by:
+            ways = [self.far_by]
+        elif self.step + 1 == FAR:
+            moving = {1: moving[1][: self.cut], -1: moving[-1][self.cut :]}
+
+        def function(*arrays):
+            moved = [shift(array, by) for array, by in zip(arrays, ways)]
+            self.now = [x for block in arrays[len(ways) :] for x in (block, swap(block, "core"))]
+            return [*moved, *self.now]
+
+        return [moving[by] for by in ways] + self.fresh, function
 
     def take(self, results):
-        self.ahead, self.behind, *self.chunks[self.step] = results
         self.step += 1
         if self.step == FAR:
-            last = jnp.concatenate([self.ahead, self.behind], axis=0)
+            count = 1 if self.far_by else 2
+            last, self.chunks[FAR - 1] = results[:count], list(results[count:])
+            last = jnp.concatenate(last, axis=0) if count == 2 else last[0]
             self.chunks[FAR] = [last, swap(last, "core")]
             self.chunks[LAST] = self.chunks[0] + self.chunks[FAR]
-        self.fresh = [self.behind, self.ahead]
+            return
+        self.moving[1], self.moving[-1], *self.chunks[self.step - 1] = results
+        self.fresh = [self.moving[-1], self.moving[1]]
 
 
 class Scatter:
-    def __init__(self, make, inputs=()):
-        self.make, self.inputs = make, list(inputs)
+    def __init__(self, make, inputs=(), ready=False, far_by=0):
+        self.make, self.inputs, self.ready, self.far_by = make, list(inputs), ready, far_by
         self.step = 0
         mine, other = make(FAR, *self.inputs)
         first = mine
@@ -520,36 +526,48 @@
             first = first.astype(jnp.bfloat16)
         self.rows = first.shape[0]
         self.cut = self.rows // 2 // 8 * 8
-        self.carried = [first[: self.cut], first[self.cut :]]
+        self.carried = [first] if far_by else [first[: self.cut], first[self.cut :]]
 
     def job(self):
         near = FAR - self.step - 1
-
-        def function(ahead, behind, *inputs):
-            ahead, behind = shift(ahead, 1), shift(behind, -1)
-            mine, other = self.make(near, *inputs)
-            return [ahead, behind, mine] + ([] if other is None else [swap(other, "core")])
+        count = len(self.carried)
+        ways = [self.far_by] if count == 1 else [1, -1]
+
+        def function(*arrays):
+            moved = [shift(array, by) for array, by in zip(arrays, ways)]
+            mine, other = self.make(near, *arrays[count:])
+            self.mine = mine
+            terms = [] if self.ready else [mine]
+            return moved + terms + ([] if other is None else [swap(other, "core")])
 
         return self.carried + self.inputs, function
 
     def take(self, results):
         self.step += 1
-        ahead, behind, *terms = results
-        ahead, behind = ahead.astype(jnp.float32), behind.astype(jnp.float32)
+        count = len(self.carried)
+        moved, terms = list(results[:count]), list(results[count:])
+        if self.ready:
+            terms = [self.mine] + terms
 
         def term(i):
             span = slice(i * self.rows, (i + 1) * self.rows)
             return sum(part[span].astype(jnp.float32) for part in terms)
 
+        moved = [array.astype(jnp.float32) for array in moved]
         if self.step == FAR:
-            self.total = term(0) + ahead + behind
+            self.last = [*results[:count], *terms]
+            self.total = term(0) + moved[0] + moved[1]
             return
-        if self.step == 1:
+        if count == 1:
+            moved = [moved[0], 0.0] if self.far_by == 1 else [0.0, moved[0]]
+        elif self.step == 1:
+            ahead, behind = moved
             ahead = jnp.concatenate([ahead, jnp.zeros_like(behind)], axis=0)
             behind = jnp.concatenate([jnp.zeros_like(ahead[: self.cut]), behind], axis=0)
+            moved = [ahead, behind]
         self.carried = [
-            (term(0) + ahead).astype(jnp.bfloat16),
-            (term(1) + behind).astype(jnp.bfloat16),
+            (term(0) + moved[0]).astype(jnp.bfloat16),
+            (term(1) + moved[1]).astype(jnp.bfloat16),
         ]
 
 
@@ -598,16 +616,19 @@
     return jnp.stack([lax.index_in_dim(values, at, axis, False) for at in PLACES], axis)
 
 
-def in_hbm(arrays, specs):
+def in_hbm(arrays, specs=None):
     return [
         array
-        if spec.memory_space == pltpu.SMEM
+        if specs and specs[i].memory_space == pltpu.SMEM
         else pltpu.with_memory_space_constraint(array, pltpu.HBM)
-        for array, spec in zip(arrays, specs)
+        for i, array in enumerate(arrays)
     ]
 
 
-def call(kernel, name, inputs, ins, outs, shapes, earlier=(), grid=(1,), scratch=(), mib=56):
+def call(
+    kernel, name, inputs, ins, outs, shapes, earlier=(), grid=(1,), scratch=(), mib=56, cost=None,
+    free=0,
+):
     return pl.pallas_call(
         kernel,
         grid=grid,
@@ -617,9 +638,9 @@
         scratch_shapes=list(scratch),
         input_output_aliases={len(ins) + i: i for i in range(len(earlier))},
         compiler_params=pltpu.CompilerParams(vmem_limit_bytes=mib << 20),
-        cost_estimate=BRIEF,
+        cost_estimate=BRIEF if cost is None else cost,
         name=name,
-    )(*in_hbm(inputs, ins), *earlier)
+    )(*inputs[:free], *in_hbm(inputs[free:], ins[free:]), *in_hbm(earlier))
 
 
 def whole(array):
@@ -689,6 +710,8 @@
             tags,
         ],
         earlier,
+        free=count,
+        mib=36,
     )
 
 
@@ -720,7 +743,7 @@
         [lin, inverse, gains, cosine, sine_part],
         [row(cols), row(2), whole(gains), row(head // 2), row(head // 2)],
         [row(head)] * 3,
-        [jax.ShapeDtypeStruct((length, head), jnp.bfloat16)] * 3,
+        [pltpu.HBM((length, head), jnp.bfloat16)] * 3,
         grid=(4,),
         mib=16,
     )
@@ -757,7 +780,7 @@
         [rows_of(step, tok_rows, head), whole(keys), whole(values)],
         [whole(shape) for shape in shapes],
         shapes,
-        mib=40,
+        mib=28,
     )
 
 
@@ -784,7 +807,7 @@
         [block, block, whole(left_weight), whole(right_weight)],
         [whole(shape)],
         [shape],
-        mib=32,
+        mib=16,
     )[0]
 
 
@@ -850,7 +873,7 @@
     inputs = [*blocks, queries, lse, lin, cosine, sine_part, keys, values, weight, gains]
     ins = [whole(b) for b in blocks] + [
         rows_of(step, tok_rows, head),
-        rows_of(step, tok_rows, 1),
+        whole(lse),
         rows_of(step, tok_rows, head),
         rows_of(step, tok_rows, head // 2),
         rows_of(step, tok_rows, head // 2),
@@ -887,16 +910,17 @@
         }
         if earlier
         else {},
-        compiler_params=pltpu.CompilerParams(vmem_limit_bytes=56 << 20),
+        compiler_params=pltpu.CompilerParams(vmem_limit_bytes=42 << 20),
         cost_estimate=BRIEF,
         name="attend_back",
-    )(*in_hbm(inputs, ins), *so_far, *earlier[:2])
+    )(*blocks, *in_hbm(inputs[count:], ins[count:]), *so_far, *in_hbm(earlier[:2]))
 
 
 def lin_back_rows(dq, dk, dv, lin, inverse, along, tok_rows):
     length, cols = lin.shape
     head = cols // 3
-    rows = 2 * tok_rows
+    places = 2
+    rows = 2 * places * tok_rows
 
     def kernel(dq_ref, dk_ref, dv_ref, lin_ref, inv_ref, along_ref, out_ref, mine_ref, other_ref):
         for k, grad_ref in enumerate((dq_ref, dk_ref)):
@@ -905,8 +929,10 @@
             slope = inv * inv * inv * along_ref[:, k : k + 1]
             out_ref[:, span] = (inv * grad_ref[...] - lin_ref[:, span] * slope).astype(jnp.bfloat16)
         out_ref[:, 2 * head :] = dv_ref[...].astype(jnp.bfloat16)
-        mine_ref[...] = out_ref[:tok_rows]
-        other_ref[...] = out_ref[tok_rows:]
+        for i in range(places):
+            to, at = slice(i * tok_rows, (i + 1) * tok_rows), 2 * i * tok_rows
+            mine_ref[to] = out_ref[at : at + tok_rows]
+            other_ref[to] = out_ref[at + tok_rows : at + 2 * tok_rows]
 
     row = lambda width: pl.BlockSpec((rows, width), lambda i: (i, 0))
     half = jax.ShapeDtypeStruct((length // 2, cols), jnp.bfloat16)
@@ -915,9 +941,9 @@
         "lin_back",
         [dq, dk, dv, lin, inverse, along],
         [row(head)] * 3 + [row(cols), row(2), row(2)],
-        [row(cols)] + [pl.BlockSpec((tok_rows, cols), lambda i: (i, 0))] * 2,
-        [jax.ShapeDtypeStruct((length, cols), jnp.bfloat16), half, half],
-        grid=(CHIPS,),
+        [row(cols)] + [pl.BlockSpec((places * tok_rows, cols), lambda i: (i, 0))] * 2,
+        [pltpu.HBM((length, cols), jnp.bfloat16), pltpu.HBM(half.shape, half.dtype), half],
+        grid=(CHIPS // places,),
         mib=16,
     )
 
@@ -1082,8 +1108,34 @@
         + [pltpu.VMEM((rows, hidden), low)] * 3
         + [pltpu.VMEM((rows, 1), jnp.float32)] * 2
         + [pltpu.SemaphoreType.DMA((2,))],
-        mib=58,
-    )
+        mib=46,
+        free=2 * count,
+    )
+
+
+def input_grad_rows(parts, tokens, inverse, gain, grads):
+    def kernel(ahead_ref, behind_ref, mine_ref, tokens_ref, inv_ref, gain_ref, grads_ref, out_ref):
+        upstream = mine_ref[...].astype(jnp.float32) + ahead_ref[...].astype(jnp.float32)
+        upstream = upstream + behind_ref[...].astype(jnp.float32)
+        rows = tokens_ref[...].astype(jnp.float32)
+        inv = inv_ref[...]
+        scaled = upstream * gain_ref[...]
+        along = jnp.mean(scaled * rows, axis=-1, keepdims=True)
+        norm = inv * scaled - rows * inv * inv * inv * along
+        out_ref[...] = (grads_ref[...] + norm).astype(jnp.bfloat16)
+
+    arrays = [*parts, tokens, inverse, gain, grads]
+    shape = jax.ShapeDtypeStruct(tokens.shape, jnp.bfloat16)
+    return call(
+        kernel,
+        "input_grad",
+        arrays,
+        [whole(a) for a in arrays],
+        [whole(shape)],
+        [shape],
+        mib=24,
+        free=len(arrays),
+    )[0]
 
 
 THIN = 128
@@ -1095,7 +1147,7 @@
     return high, values - high
 
 
-def dense_chunk(rows_h, grads, weight, columns, gain, narrow, part, own_rows):
+def dense_chunk(rows_h, grads, weight, columns, narrow, part, own_rows):
     length, width = rows_h.shape
     cols = grads.shape[1]
     block = 256
@@ -1103,11 +1155,11 @@
     wide = narrow is not None
     first_col, count_col = columns
 
-    def kernel(part_ref, h_ref, grads_ref, weight_ref, gain_ref, *refs):
+    def kernel(part_ref, h_ref, grads_ref, weight_ref, *refs):
         kept_ref, sent_ref = refs[-2:] if wide else refs[-3:-1]
-        grads = contract_rows(h_ref[...], grads_ref[...])
+        grads = contract_rows(h_ref[...], grads_ref[...].astype(jnp.bfloat16))
         weight = weight_ref[...].astype(jnp.float32)[:, first_col : first_col + count_col]
-        term = jnp.sum(grads * weight, axis=-1, keepdims=True) / gain_ref[...]
+        term = jnp.sum(grads * weight, axis=-1, keepdims=True)
         both = plain = grads
         if wide:
             narrow = refs[0][...]
@@ -1134,20 +1186,24 @@
     return call(
         kernel,
         "dense",
-        [part, rows_h, grads, weight, gain] + (list(narrow) if wide else []),
+        [part, rows_h, grads, weight] + (list(narrow) if wide else []),
         [
             pl.BlockSpec(memory_space=pltpu.SMEM),
             pl.BlockSpec((length, block), lambda i: (0, i)),
             whole(grads),
             here(weight.shape[1]),
-            here(1),
         ]
         + ([here(HALF_THIN), here(1)] if wide else []),
         [row(full), row(full)] + ([] if wide else [here(1)]),
         [out(jnp.float32), out(jnp.bfloat16)]
         + ([] if wide else [jax.ShapeDtypeStruct((width, 1), jnp.float32)]),
         grid=(width // block,),
-        mib=40,
+        mib=24,
+        cost=pl.CostEstimate(
+            flops=2 * length * width * cols,
+            bytes_accessed=2 * length * width + 6 * width * full,
+            transcendentals=0,
+        ),
     )
 
 
@@ -1286,7 +1342,9 @@
     def to_other(*arrays):
         return [swap(array, "fsdp") for array in arrays]
 
-    ((qkv_other, small_other),) = window([rows_one], loose=[([qkv_mine, small], to_other)])
+    (small_other,), (qkv_other,) = window(
+        [rows_one], [([small], to_other)], loose=[([qkv_mine], to_other)]
+    )
     small_full = joined(small, small_other, 1)
     r_weight = small_full[:expert_count]
     g_attn = small_full[expert_count].astype(jnp.float32)
@@ -1296,7 +1354,6 @@
         jnp.float32
     )
     g_query, g_key = g_heads[:head_dim], g_heads[head_dim : 2 * head_dim]
-    gain_col = g_attn[:, None]
     qkv_weight = joined(qkv_mine, qkv_other, 0)
 
     def expert_weights(_, *own):
@@ -1336,7 +1393,7 @@
         code = mine * length + order.reshape(length)
         ranks = jnp.sum((code[None, :] < code[:, None]).astype(jnp.float32), axis=1)
         kept = (mine < LEVELS) & (ranks < capacity)
-        return kept.astype(jnp.float32)[:, None], owner[:, 0].astype(jnp.int32)
+        return (kept.astype(jnp.float32)[:, None],)
 
     def rope_job(all_tags):
         spots = (all_tags[:, 1] * 128.0 + all_tags[:, 2]).reshape(-1)
@@ -1367,10 +1424,9 @@
         return [*made, projected(FAR, made)]
 
     (out_pair,) = other_core(out_weight)
-    grads_rows = Gather(cotangent[0])
-    (*heads[FAR], far_terms), heads[FAR - 1], (kept, owners) = window(
-        [grads_rows],
-        [([q_rot, k_rot, v_low], first_job), attend_job(FAR - 1), ([all_tags], rank_job)],
+    grads_rows = Gather(cotangent[0], -1)
+    (*heads[FAR], far_terms), heads[FAR - 1] = window(
+        [grads_rows], [([q_rot, k_rot, v_low], first_job), attend_job(FAR - 1)]
     )
 
     def out_terms(step, *parts):
@@ -1380,15 +1436,13 @@
     for near in range(FAR - 1, -1, -1):
         out_sum.inputs = heads[near]
         jobs = [attend_job(near - 1)] if near else []
-        held = [([gate_weight], lambda weight: (weight,))] if near == 2 else []
-        made = window([out_sum], jobs + held)
-        if held:
-            (gate_weight,) = made[-1]
+        held = [([gate_weight], lambda weight: (weight,)), ([all_tags], rank_job)]
+        made = window([out_sum], jobs + (held if near == 2 else []))
+        if near == 2:
+            (gate_weight,), (kept,) = made[-2:]
         if near:
             heads[near - 1] = made[0]
-    mixed_low, lse = (
-        jnp.concatenate([heads[step][k] for step in CHUNKS], axis=0) for k in range(2)
-    )
+    mixed_low = jnp.concatenate([heads[step][0] for step in CHUNKS], axis=0)
     middle = inputs + out_sum.total
 
     h_two_f, inv_two = rms_forward(middle, g_ffn)
@@ -1397,7 +1451,7 @@
     filled = ()
     mix_terms, dx_terms = {}, {}
 
-    rows_two = Gather(h_two)
+    rows_two = Gather(h_two, 1)
     window([rows_two])
 
     def expert_job(step, h_blocks, g_blocks):
@@ -1440,8 +1494,8 @@
     row_max = jnp.max(logits, axis=-1, keepdims=True)
     exps_raw = jnp.exp(logits - row_max)
     router_probs = exps_raw / jnp.sum(exps_raw, axis=-1, keepdims=True)
-    dx_sum = Scatter(lambda step: dx_terms[step])
-    mix_sum = Scatter(lambda step: mix_terms[step])
+    dx_sum = Scatter(lambda step: dx_terms[step], ready=True, far_by=1)
+    mix_sum = Scatter(lambda step: mix_terms[step], ready=True, far_by=-1)
     ((gate_wgrad,),) = window([dx_sum, mix_sum], [([all_h_two, gate_grad], wgrad)])
     s_gate = over_sequences(gate_wgrad, 0)
     ((up_wgrad,),) = window([dx_sum, mix_sum], [([all_h_two, up_grad], wgrad)])
@@ -1470,7 +1524,7 @@
             step,
             blocks(),
             q_rot,
-            lse,
+            heads[step][1],
             k_rot,
             v_low,
             out_weight,
@@ -1499,7 +1553,7 @@
             ),
         )
 
-    besides = {0: [], 1: [mix_sum], 2: [], 3: []}
+    besides = {0: [], 1: [mix_sum], 2: [], 3: [mix_sum]}
     also = {1: [([h_two, logit_grad, ffn_gain_grad], narrow_job), ([s_gate], widen)]}
     for step in range(FAR + 1):
         if step == FAR:
@@ -1521,20 +1575,18 @@
 
     def value_job(all_h_one, dv):
         return dense_chunk(
-            all_h_one, dv.astype(low), qkv_weight, (2 * head_dim, head_dim), gain_col, None,
+            all_h_one, dv, qkv_weight, (2 * head_dim, head_dim), None,
             part_one, own_rows,
         )
 
-    along, ((v_kept, v_sent, v_term), mixed) = token_sums(
+    along, ((v_kept, v_sent, v_term),) = token_sums(
         jnp.stack(
             [jnp.concatenate([q_sums[step][0] for step in CHUNKS], axis=0), k_sums[0]], axis=0
         ),
         [
             ([all_h_one, dv], value_job),
-            mix_sum.job(),
         ],
     )
-    mix_sum.take(mixed)
     layer_out = (middle + mix_sum.total).astype(low)
     lin_grad, lin_mine, lin_theirs = lin_back_rows(dq, dk, dv, lin, inverse, along, tok_rows)
     lin_theirs = swap(lin_theirs, "core")
@@ -1545,7 +1597,7 @@
 
     def dense_job(all_h_one, lin_grad, *narrow):
         return dense_chunk(
-            all_h_one, lin_grad[:, : 2 * head_dim], qkv_weight, (0, 2 * head_dim), gain_col, narrow,
+            all_h_one, lin_grad[:, : 2 * head_dim], qkv_weight, (0, 2 * head_dim), narrow,
             part_one, own_rows,
         )
 
@@ -1576,9 +1628,9 @@
         blocks = payload.reshape(ctx_count, own_rows, -1)
         return (lax.all_to_all(blocks, ("chip", "core"), 0, 0, tiled=True),)
 
-    (kept, sent), (s_down,), (v_got,) = window(
+    (kept, sent), (v_got,) = window(
         [h_sum],
-        [([all_h_one, lin_grad, narrow, v_term], dense_job), ([s_down], widen)],
+        [([all_h_one, lin_grad, narrow, v_term], dense_job)],
         loose=[([v_sent], swap_job)],
     )
     (got,), (out_wgrad,), (v_received,) = window(
@@ -1587,31 +1639,29 @@
         loose=[([(v_kept + v_got.astype(jnp.float32)).astype(low)], owners_job)],
     )
     out_rows = out_wgrad.reshape(1, 2, own_rows, model_width)
-    (s_up,), (received,), (out_got, gain_got, gain_kept) = window(
+    (received,), (out_got, gain_got, gain_kept) = window(
         [h_sum],
-        [([s_up], widen)],
         loose=[
             ([kept, got], lambda kept, got: owners_job(dense_sum(kept, got))),
             ([pick(out_rows, 1 - part)[0].astype(low), dq, dk, lin], out_swap_job),
         ],
     )
 
-    def out_done_job(own, out_got, gain_kept, gain_got):
-        return own + out_got.astype(jnp.float32), gain_kept + gain_got
-
-    (v_received,), (received,), (d_out, gain_sum) = window(
+    (v_received,), (received,), (out_got, gain_got), (s_up,), (s_down,) = window(
         [h_sum],
         [
             ([], lambda: (v_received,)),
             ([], lambda: (received,)),
-            ([pick(out_rows, part)[0], out_got, gain_kept, gain_got], out_done_job),
+            ([], lambda: (out_got, gain_got)),
+            ([s_up], widen),
+            ([s_down], widen),
         ],
     )
-    h_grad = h_sum.total
+    d_out = pick(out_rows, part)[0] + out_got.astype(jnp.float32)
+    gain_sum = gain_kept + gain_got
     d_qgain, d_kgain = gain_sum[0], gain_sum[1]
     s_gate, s_up, s_down = s_gate[None], s_up[None], s_down[None]
-    in_norm_grad, _ = rms_backward(inputs, inv_one, g_attn, h_grad)
-    input_grad = (middle_grad + in_norm_grad).astype(low)
+    input_grad = input_grad_rows(h_sum.last, tokens[0], inv_one, g_attn[None], middle_grad)
     d_query, d_key, d_value = (
         columns.transpose(1, 0, 2).reshape(own_rows, model_width).astype(jnp.float32)
         for columns in (received[:, :, :head_dim], received[:, :, head_dim : 2 * head_dim], v_received)
@@ -1619,7 +1669,8 @@
     thin_sum = jnp.sum(received[:, :, 2 * head_dim :].astype(jnp.float32), axis=0)
     thin_sum = thin_sum[:, :HALF_THIN] + thin_sum[:, HALF_THIN:]
     d_router = thin_sum[:, :expert_count]
-    d_ffn, d_attn = thin_sum[:, expert_count], thin_sum[:, expert_count + 1]
+    own_gain = lax.dynamic_slice_in_dim(g_attn, (2 * place + part) * own_rows, own_rows, 0)
+    d_ffn, d_attn = thin_sum[:, expert_count], thin_sum[:, expert_count + 1] / own_gain
     return (
         layer_out[None],
         input_grad[None],

time: 692 us -> 664 us (0.960)
  Pallas kernels: 234 us -> 221 us
  local copies, waits for them, and re-layouts: 67.5 us -> 57.2 us
    ppermute x61, waiting for transfers between devices: 22.2 us -> 32.4 us  [swap(): return lax.ppermute(array, axis, [(0, 1), (1, 0)])]
    ppermute x8, waiting for transfers between devices: 8.25 us -> 0.02 us  [heard(): return lax.ppermute(both, ('chip', 'core'), pairs)]
    ppermute x64 -> x60, waiting for transfers between devices: 100 us -> 93.4 us  [shift(): return lax.ppermute(array, 'chip', pairs)]
    pallas_call x28 -> x29, Pallas kernels: 192 us -> 185 us  [call(): pl.pallas_call(kernel, grid=grid, in_specs=ins + [pl.BlockSpec(memory_spa...]
    unnamed x231 -> x207, local copies, waits for them, and re-layouts: 31 us -> 34.7 us
    ppermute x64 -> x60, starting transfers between devices: 66.4 us -> 63.1 us  [shift(): return lax.ppermute(array, 'chip', pairs)]
    convert_element_type x15 -> x13, other arithmetic: 30 us -> 28.3 us  [the longest x12 27 us: take(): (term(1) + moved[1]).astype(jnp.bfloat16)]
  transfers between devices with their start and end apart: 141 -> 137, of which waited for: 50 -> 47; matrix products, arithmetic and copies ran while one was open for 20% -> 20% of each run, Pallas kernels for 31% -> 30%
where the time goes in v4:
time: 664 us; the launch traced here: 654 us
  Pallas kernels  221 us (33%)
  waiting for transfers between devices  134 us (20%)
  starting transfers between devices  106 us (16%)
  other arithmetic  71.7 us (11%)
  local copies, waits for them, and re-layouts  57.2 us (9%)
  matrix products  48.4 us (7%)
  between operations  16.3 us (2%)
    pallas_call x29, Pallas kernels, call(): pl.pallas_call(kernel, grid=grid, in_specs=ins + [pl.BlockSpec(memory_spa...  185 us
    ppermute x60, waiting for transfers between devices, shift(): return lax.ppermute(array, 'chip', pairs)  93.4 us
    ppermute x60, starting transfers between devices, shift(): return lax.ppermute(array, 'chip', pairs)  63.1 us
    dot_general x4, matrix products, contract_rows(): lax.dot_general(left, right, (((0,), (0,)), ((), ())), preferred_element_...  45.6 us
    pallas_call x5, Pallas kernels, attend_back_chunk(): pl.pallas_call(kernel, grid=(1,), in_specs=ins + [whole(part) for part in...  36.1 us
    unnamed x207, local copies, waits for them, and re-layouts  34.7 us
    ppermute x61, waiting for transfers between devices, swap(): return lax.ppermute(array, axis, [(0, 1), (1, 0)])  32.4 us
    convert_element_type x12, other arithmetic, take(): (term(1) + moved[1]).astype(jnp.bfloat16)  27 us
  transfers between devices with their start and end apart: 137, of which 47 were waited for; matrix products, arithmetic and copies ran while one was open for 20% of the time, Pallas kernels for 30%

profile of v4, /device:TPU:8, one launch (start us, length us, event | category | flops | bytes accessed | tf_op | source)
XLA Modules:
  0.0 654.0 jit_solution(15899706643576464539)
XLA Ops:
  19.0 16.3 %collective-permute-done.3 = bf16[19,1024]{1,0:T(8,128)(2,1)S(1)} collective-permute-done((bf16[19,1024]{1,0:T(8,128)(2,1)S(1)}, bf16[19,1024]{1,0:T(8,128)(2,1)S(1)}, u32[]{:S(2)}, u32[]{:S(2)}) %collective-permute-start.3) | collective-permute-done | bytes 38944 | tf_op jit(solution)/shard_map/ppermute | solution.py:456
  63.4 6.5 collective-permute-done.10.refs_0_
  182.2 6.6 %collective-permute-done.40 = bf16[128,2048]{1,0:T(8,128)(2,1)S(1)} collective-permute-done((bf16[128,2048]{1,0:T(8,128)(2,1)S(1)}, bf16[128,2048]{1,0:T(8,128)(2,1)S(1)}, u32[]{:S(2)}, u32[]{:S(2)}) %collective-permute-start.40) | collective-permute-done | bytes 524320 | tf_op jit(solution)/shard_map/ppermute | solution.py:461
  192.2 9.2 %collective-permute-done.43.refs_2_ = bf16[128,2048]{1,0:T(8,128)(2,1)} collective-permute-done((bf16[128,2048]{1,0:T(8,128)(2,1)S(1)}, bf16[128,2048]{1,0:T(8,128)(2,1)}, u32[]{:S(2)}, u32[]{:S(2)}) %collective-permute-start.43) | collective-permute-done | bytes 524320 | tf_op jit(solution)/shard_map/ppermute | solution.py:461
  210.6 8.1 %all-gather.8.cloned.1.call-done.refs_13_.refs_16_ = bf16[1024,2048]{1,0:T(8,128)(2,1)} async-done(((bf16[1024,1024]{1,0:T(8,128)(2,1)}), bf16[1024,2048]{1,0:T(8,128)(2,1)}) %all-gather.8.cloned.1.call-update) | async-done | bytes 4194320 | tf_op jit(solution)/shard_map/all_gather | solution.py:1360
  221.8 23.1 %expert.4 = (bf16[2048,2048]{1,0:T(8,128)(2,1)}, bf16[2048,2048]{1,0:T(8,128)(2,1)}, bf16[2048,1024]{1,0:T(8,128)(2,1)}, bf16[2048,1024]{1,0:T(8,128)(2,1)}, bf1...) custom-call(bf16[128,2048]{1,0:T(8,128)(2,1)} %collective-permute-do, ...), custom_call_target="tpu_custom_call" | custom-call | tf_op jit(solution)/shard_map/expert/pallas_call | solution.py:632
  253.5 23.0 %expert.5 = (bf16[2048,2048]{1,0:T(8,128)(2,1)}, bf16[2048,2048]{1,0:T(8,128)(2,1)}, bf16[2048,1024]{1,0:T(8,128)(2,1)}, bf16[2048,1024]{1,0:T(8,128)(2,1)}, bf1...) custom-call(bf16[128,2048]{1,0:T(8,128)(2,1)} %collective-permute-do, ...), custom_call_target="tpu_custom_call", output_to_operand_aliasing={{0}: (17, {}), {1}: (18, {}), {2}: (19, {}), {3}: (20, {}),... | custom-call | tf_op jit(solution)/shard_map/expert/pallas_call | solution.py:632
  282.7 22.5 %expert.6 = (bf16[2048,2048]{1,0:T(8,128)(2,1)}, bf16[2048,2048]{1,0:T(8,128)(2,1)}, bf16[2048,1024]{1,0:T(8,128)(2,1)}, bf16[2048,1024]{1,0:T(8,128)(2,1)}, bf1...) custom-call(bf16[128,2048]{1,0:T(8,128)(2,1)S(1)} %collective-permut, ...), custom_call_target="tpu_custom_call", output_to_operand_aliasing={{0}: (17, {}), {1}: (18, {}), {2}: (19, {}), {3}: (20, {}),... | custom-call | tf_op jit(solution)/shard_map/expert/pallas_call | solution.py:632
  308.9 22.5 %expert.7 = (bf16[2048,2048]{1,0:T(8,128)(2,1)}, bf16[2048,2048]{1,0:T(8,128)(2,1)}, bf16[2048,1024]{1,0:T(8,128)(2,1)}, bf16[2048,1024]{1,0:T(8,128)(2,1)}, bf1...) custom-call(bf16[128,2048]{1,0:T(8,128)(2,1)S(1)} %multiply_convert_, ...), custom_call_target="tpu_custom_call", output_to_operand_aliasing={{0}: (17, {}), {1}: (18, {}), {2}: (19, {}), {3}: (20, {}),... | custom-call | tf_op jit(solution)/shard_map/expert/pallas_call | solution.py:632
  338.4 14.0 %convolution_convert_fusion.2 = bf16[2048,1024]{1,0:T(8,128)(2,1)} fusion(bf16[2048,2048]{1,0:T(8,128)(2,1)} %get-tuple-element.751, bf16[2048,1024]{1,0:T(8,128)(2,1)} %get-tuple-element.738), kind=kOutput, calls=%fused_computation.3 | convolution fusion | flops 8592031744 | bytes 16777216 | tf_op jit(solution)/shard_map/dot_general | solution.py:39
  363.7 12.8 %convolution_convert_fusion.1 = bf16[2048,1024]{1,0:T(8,128)(2,1)} fusion(bf16[2048,2048]{1,0:T(8,128)(2,1)} %get-tuple-element.751, bf16[2048,1024]{1,0:T(8,128)(2,1)S(1)} %copy-done.58), kind=kOutput, calls=%fused_computation.2 | convolution fusion | flops 8592031744 | bytes 16777216 | tf_op jit(solution)/shard_map/dot_general | solution.py:39
  376.5 9.2 %collective-permute-done.79 = bf16[128,2048]{1,0:T(8,128)(2,1)} collective-permute-done((bf16[128,2048]{1,0:T(8,128)(2,1)}, bf16[128,2048]{1,0:T(8,128)(2,1)}, u32[]{:S(2)}, u32[]{:S(2)}) %collective-permute-start.79) | collective-permute-done | bytes 524320 | tf_op jit(solution)/shard_map/ppermute | solution.py:461
  392.8 14.1 %convolution_convert_fusion = bf16[1024,2048]{1,0:T(8,128)(2,1)} fusion(bf16[2048,1024]{1,0:T(8,128)(2,1)} %get-tuple-element.761, bf16[2048,2048]{1,0:T(8,128)(2,1)} %get-tuple-element.762), kind=kOutput, calls=%fused_computation.1 | convolution fusion | flops 8592031744 | bytes 16777216 | tf_op jit(solution)/shard_map/dot_general | solution.py:39
  412.0 11.0 %collective-permute-done.85 = bf16[136,2048]{1,0:T(8,128)(2,1)S(1)} collective-permute-done((bf16[136,2048]{1,0:T(8,128)(2,1)S(1)}, bf16[136,2048]{1,0:T(8,128)(2,1)S(1)}, u32[]{:S(2)}, u32[]{:S(2)}) %collective-permute-start.85) | collective-permute-done | bytes 557088 | tf_op jit(solution)/shard_map/ppermute | solution.py:461
  458.9 7.7 %attend_back.6 = (f32[2048,128]{1,0:T(8,128)}, bf16[2048,2048]{1,0:T(8,128)(2,1)}, f32[2048,128]{1,0:T(8,128)S(1)}, f32[2048,128]{1,0:T(8,128)S(1)}, f32[8,512]{1,0:T(8,128)S(1)}) custom-call(bf16[128,2048]{1,0:T(8,128)(2,1)} %collective-permute-done.89.refs_0_, ...), custom_call_target="tpu_custom_call", output_to_operand_aliasing={{2}: (13, {}), {3}: (14, {}), {0}: (15, {}), {1}: (16, {})} | custom-call | tf_op jit(solution)/shard_map/attend_back/pallas_call | solution.py:891
  476.0 8.6 %attend_back.7 = (f32[2048,128]{1,0:T(8,128)}, bf16[2048,2048]{1,0:T(8,128)(2,1)}, f32[2048,128]{1,0:T(8,128)S(1)}, f32[2048,128]{1,0:T(8,128)S(1)}, f32[8,512]{1,0:T(8,128)S(1)}) custom-call(bf16[128,2048]{1,0:T(8,128)(2,1)} %collective-permute-done.92.refs_0_, ...), custom_call_target="tpu_custom_call", output_to_operand_aliasing={{2}: (13, {}), {3}: (14, {}), {0}: (15, {}), {1}: (16, {})} | custom-call | tf_op jit(solution)/shard_map/attend_back/pallas_call | solution.py:891
  491.2 8.4 %attend_back.8 = (f32[2048,128]{1,0:T(8,128)}, bf16[2048,2048]{1,0:T(8,128)(2,1)}, f32[2048,128]{1,0:T(8,128)S(1)}, f32[2048,128]{1,0:T(8,128)S(1)}, f32[8,512]{1,0:T(8,128)S(1)}) custom-call(bf16[128,2048]{1,0:T(8,128)(2,1)S(1)} %collective-permute-done.99.refs_0_, ...), custom_call_target="tpu_custom_call", output_to_operand_aliasing={{2}: (13, {}), {3}: (14, {}), {0}: (15, {}), {1}: (16, {})} | custom-call | tf_op jit(solution)/shard_map/attend_back/pallas_call | solution.py:891
  499.7 7.2 %collective-permute-done.102 = bf16[64,2048]{1,0:T(8,128)(2,1)S(1)} collective-permute-done((bf16[64,2048]{1,0:T(8,128)(2,1)S(1)}, bf16[64,2048]{1,0:T(8,128)(2,1)S(1)}, u32[]{:S(2)}, u32[]{:S(2)}) %collective-permute-start.102) | collective-permute-done | bytes 262176 | tf_op jit(solution)/shard_map/ppermute | solution.py:461
  510.1 7.0 %attend_back.9 = (f32[2048,128]{1,0:T(8,128)}, bf16[2048,2048]{1,0:T(8,128)(2,1)}, f32[2048,128]{1,0:T(8,128)S(1)}, f32[2048,128]{1,0:T(8,128)S(1)}, f32[8,256]{1,0:T(8,128)S(1)}, /*index=5*/f32[8,2048]{1,0:T(8,128)S(1)}) custom-call(bf16[128,2048]{1,0:T(8,128)(2,1)S(1)} %constant_dynamic-, ...), custom_call_target="tpu_custom_call", output_to_operand_aliasing={{2}: (14, {}), {3}: (15, {}), {0}: (16, {}), {1}: (17, {})} | custom-call | tf_op jit(solution)/shard_map/attend_back/pallas_call | solution.py:891
  525.2 9.0 %dense.2 = (f32[1024,128]{1,0:T(8,128)S(1)}, bf16[1024,128]{1,0:T(8,128)(2,1)S(1)}, f32[2048,1]{1,0:T(8,128)S(1)}) custom-call(s32[1]{0:T(128)} %bitcast.34.part_ref, bf16[2048,2048]{1,0:T(8,128)(2,1)} %get-tuple-element.885.h_ref, f32[2048,128]{1,0:T(8,128)} %copy-done.5, bf16[2048,384]{1,0:T(8,128)(2,1)} %maximum_select_fusion.refs_4_.weight_ref.left_weight_ref), custom_call_target="tpu_custom_call" | custom-call | flops 1073741824 | bytes 9961472 | tf_op jit(solution)/shard_map/dense/pallas_call | solution.py:632
  538.1 5.9 lin_back.1
  557.4 10.2 %dense.3 = (f32[1024,384]{1,0:T(8,128)S(1)}, bf16[1024,384]{1,0:T(8,128)(2,1)S(1)}) custom-call(s32[1]{0:T(128)} %bitcast.34.part_ref, bf16[2048,2048]{1,0:T(8,128)(2,1)} %get-tuple-element.885.h_ref, bf16[2048,256]{1,0:T(8,128)(2,1)} %slice.561.grads_ref, bf16[2048,384]{1,0:T(8,128)(2,1)} %maximum_select_fusion.refs_4_.weight_ref.left_weight_ref, ...), custom_call_target="tpu_custom_call" | custom-call | flops 2147483648 | bytes 13107200 | tf_op jit(solution)/shard_map/dense/pallas_call | solution.py:632
  574.7 6.0 all-to-all-start
  627.0 6.9 %collective-permute-done.125.ahead_ref = bf16[128,2048]{1,0:T(8,128)(2,1)S(1)} collective-permute-done((bf16[128,2048]{1,0:T(8,128)(2,1)}, bf16[128,2048]{1,0:T(8,128)(2,1)S(1)}, u32[]{:S(2)}, u32[]{:S(2)}) %collective-permute-start.125) | collective-permute-done | bytes 524320 | tf_op jit(solution)/shard_map/ppermute | solution.py:461
  (663 shorter events, 361.7 us)
Async XLA Ops:
  7.2 134.9 %all-gather.4.cloned.1.call-start = ((), (), s32[]{:S(2)}) async-start(), calls=%async_computation.5 | async-start | bytes 6291456 | tf_op jit(solution)/shard_map/all_gather | solution.py:1360
  36.8 173.8 %all-gather.6.cloned.1.call-start = ((), (), s32[]{:S(2)}) async-start(), calls=%async_computation.6 | async-start | bytes 6291456 | tf_op jit(solution)/shard_map/all_gather | solution.py:1360
  83.9 134.7 %all-gather.8.cloned.1.call-start = ((), (), s32[]{:S(2)}) async-start(), calls=%async_computation.7 | async-start | bytes 6291456 | tf_op jit(solution)/shard_map/all_gather | solution.py:1360
  133.3 310.4 %reduce-scatter.4.cloned.1.call-start = ((), (), s32[]{:S(2)}) async-start(), calls=%async_computation.8 | async-start | bytes 6291456 | tf_op jit(solution)/shard_map/reduce_scatter | solution.py:1491
  202.7 45.3 %collective-permute-start.46 = (bf16[128,2048]{1,0:T(8,128)(2,1)}, bf16[128,2048]{1,0:T(8,128)(2,1)S(1)}, u32[]{:S(2)}, u32[]{:S(2)}) collective-permute-start(bf16[128,2048]{1,0:T(8,128)(2,1)} %collective-permute-done.43.refs_2_), channel_id=1, source_target_pairs={{0,8},{8,16},{16,24},{24,28},{28,20},{20,12},{12,4},{4,0},{1,9},{9... | collective-permute-start | bytes 1572872 | tf_op jit(solution)/shard_map/ppermute | solution.py:461
  204.5 43.4 %collective-permute-start.47 = (bf16[128,2048]{1,0:T(8,128)(2,1)}, bf16[128,2048]{1,0:T(8,128)(2,1)}, u32[]{:S(2)}, u32[]{:S(2)}) collective-permute-start(bf16[128,2048]{1,0:T(8,128)(2,1)} %collective-permute-done.44.refs_0_), channel_id=1, source_target_pairs={{0,4},{8,0},{16,8},{24,16},{28,24},{20,28},{12,20},{4,12},{1,5},{9... | collective-permute-start | bytes 1572872 | tf_op jit(solution)/shard_map/ppermute | solution.py:461
  206.9 41.0 %collective-permute-start.50 = (bf16[128,2048]{1,0:T(8,128)(2,1)S(1)}, bf16[128,2048]{1,0:T(8,128)(2,1)}, u32[]{:S(2)}, u32[]{:S(2)}) collective-permute-start(bf16[128,2048]{1,0:T(8,128)(2,1)S(1)} %collective-permute-done.25.refs_6_), channel_id=1, source_target_pairs={{0,8},{8,16},{16,24},{24,28},{28,20},{20,12},{12,4},{4,0},{1,9},{9... | collective-permute-start | bytes 1572872 | tf_op jit(solution)/shard_map/ppermute | solution.py:461
  208.2 39.8 %collective-permute-start.51 = (bf16[128,2048]{1,0:T(8,128)(2,1)S(1)}, bf16[128,2048]{1,0:T(8,128)(2,1)}, u32[]{:S(2)}, u32[]{:S(2)}) collective-permute-start(bf16[128,2048]{1,0:T(8,128)(2,1)S(1)} %collective-permute-done.26.refs_4_), channel_id=1, source_target_pairs={{0,4},{8,0},{16,8},{24,16},{28,24},{20,28},{12,20},{4,12},{1,5},{9... | collective-permute-start | bytes 1572872 | tf_op jit(solution)/shard_map/ppermute | solution.py:461
  249.1 29.4 %collective-permute-start.54 = (bf16[128,2048]{1,0:T(8,128)(2,1)S(1)}, bf16[128,2048]{1,0:T(8,128)(2,1)S(1)}, u32[]{:S(2)}, u32[]{:S(2)}) collective-permute-start(bf16[128,2048]{1,0:T(8,128)(2,1)S(1)} %collective-permute-done.46.refs_2_), channel_id=1, source_target_pairs={{0,8},{8,16},{16,24},{24,28},{28,20},{20,12},{12,4},{4,0},{1,9},{9... | collective-permute-start | bytes 1572872 | tf_op jit(solution)/shard_map/ppermute | solution.py:461
  250.6 27.9 %collective-permute-start.55 = (bf16[128,2048]{1,0:T(8,128)(2,1)}, bf16[128,2048]{1,0:T(8,128)(2,1)S(1)}, u32[]{:S(2)}, u32[]{:S(2)}) collective-permute-start(bf16[128,2048]{1,0:T(8,128)(2,1)} %collective-permute-done.47.refs_0_), channel_id=1, source_target_pairs={{0,4},{8,0},{16,8},{24,16},{28,24},{20,28},{12,20},{4,12},{1,5},{9... | collective-permute-start | bytes 1572872 | tf_op jit(solution)/shard_map/ppermute | solution.py:461
  251.5 27.0 %collective-permute-start.58 = (bf16[128,2048]{1,0:T(8,128)(2,1)}, bf16[128,2048]{1,0:T(8,128)(2,1)S(1)}, u32[]{:S(2)}, u32[]{:S(2)}) collective-permute-start(bf16[128,2048]{1,0:T(8,128)(2,1)} %collective-permute-done.50.refs_6_), channel_id=1, source_target_pairs={{0,8},{8,16},{16,24},{24,28},{28,20},{20,12},{12,4},{4,0},{1,9},{9... | collective-permute-start | bytes 1572872 | tf_op jit(solution)/shard_map/ppermute | solution.py:461
  253.0 25.6 %collective-permute-start.59 = (bf16[128,2048]{1,0:T(8,128)(2,1)}, bf16[128,2048]{1,0:T(8,128)(2,1)S(1)}, u32[]{:S(2)}, u32[]{:S(2)}) collective-permute-start(bf16[128,2048]{1,0:T(8,128)(2,1)} %collective-permute-done.51.refs_4_), channel_id=1, source_target_pairs={{0,4},{8,0},{16,8},{24,16},{28,24},{20,28},{12,20},{4,12},{1,5},{9... | collective-permute-start | bytes 1572872 | tf_op jit(solution)/shard_map/ppermute | solution.py:461
  279.6 26.6 %collective-permute-start.62 = (bf16[128,2048]{1,0:T(8,128)(2,1)S(1)}, bf16[128,2048]{1,0:T(8,128)(2,1)S(1)}, u32[]{:S(2)}, u32[]{:S(2)}) collective-permute-start(bf16[128,2048]{1,0:T(8,128)(2,1)S(1)} %collective-permute-done.54.refs_2_), channel_id=1, source_target_pairs={{0,8},{8,16},{16,24},{24,28},{28,20},{20,12},{12,4},{4,0},{1,9},{9... | collective-permute-start | bytes 1572872 | tf_op jit(solution)/shard_map/ppermute | solution.py:461
  281.1 25.2 %collective-permute-start.65 = (bf16[128,2048]{1,0:T(8,128)(2,1)S(1)}, bf16[128,2048]{1,0:T(8,128)(2,1)S(1)}, u32[]{:S(2)}, u32[]{:S(2)}) collective-permute-start(bf16[128,2048]{1,0:T(8,128)(2,1)S(1)} %collective-permute-done.59.refs_4_), channel_id=1, source_target_pairs={{0,4},{8,0},{16,8},{24,16},{28,24},{20,28},{12,20},{4,12},{1,5},{9... | collective-permute-start | bytes 1572872 | tf_op jit(solution)/shard_map/ppermute | solution.py:461
  352.5 262.0 %reduce-scatter.6.cloned.1.call-start = ((), (), s32[]{:S(2)}) async-start(), calls=%async_computation.9 | async-start | bytes 6291456 | tf_op jit(solution)/shard_map/reduce_scatter | solution.py:1491
  359.7 27.4 %collective-permute-start.76 = (bf16[136,2048]{1,0:T(8,128)(2,1)}, bf16[136,2048]{1,0:T(8,128)(2,1)}, u32[]{:S(2)}, u32[]{:S(2)}) collective-permute-start(bf16[136,2048]{1,0:T(8,128)(2,1)} %get-tuple-element.745), channel_id=1, source_target_pairs={{0,8},{8,16},{16,24},{24,28},{28,20},{20,12},{12,4},{4,0},{1,9},{9... | collective-permute-start | bytes 1671176 | tf_op jit(solution)/shard_map/ppermute | solution.py:461
  361.1 25.9 %collective-permute-start.77 = (bf16[136,2048]{1,0:T(8,128)(2,1)}, bf16[136,2048]{1,0:T(8,128)(2,1)}, u32[]{:S(2)}, u32[]{:S(2)}) collective-permute-start(bf16[136,2048]{1,0:T(8,128)(2,1)} %get-tuple-element.746), channel_id=1, source_target_pairs={{0,4},{8,0},{16,8},{24,16},{28,24},{20,28},{12,20},{4,12},{1,5},{9... | collective-permute-start | bytes 1671176 | tf_op jit(solution)/shard_map/ppermute | solution.py:461
  361.7 24.1 %collective-permute-start.79 = (bf16[128,2048]{1,0:T(8,128)(2,1)}, bf16[128,2048]{1,0:T(8,128)(2,1)}, u32[]{:S(2)}, u32[]{:S(2)}) collective-permute-start(bf16[128,2048]{1,0:T(8,128)(2,1)} %get-tuple-element.748), channel_id=1, source_target_pairs={{0,8},{8,16},{16,24},{24,28},{28,20},{20,12},{12,4},{4,0},{1,9},{9... | collective-permute-start | bytes 1572872 | tf_op jit(solution)/shard_map/ppermute | solution.py:461
  363.2 23.8 %collective-permute-start.80 = (bf16[128,2048]{1,0:T(8,128)(2,1)S(1)}, bf16[128,2048]{1,0:T(8,128)(2,1)}, u32[]{:S(2)}, u32[]{:S(2)}) collective-permute-start(bf16[128,2048]{1,0:T(8,128)(2,1)S(1)} %get-tuple-element.749), channel_id=1, source_target_pairs={{0,4},{8,0},{16,8},{24,16},{28,24},{20,28},{12,20},{4,12},{1,5},{9... | collective-permute-start | bytes 1572872 | tf_op jit(solution)/shard_map/ppermute | solution.py:461
  376.5 30.4 %collective-permute-start.84 = (bf16[272,2048]{1,0:T(8,128)(2,1)}, bf16[272,2048]{1,0:T(8,128)(2,1)}, u32[]{:S(2)}, u32[]{:S(2)}) collective-permute-start(bf16[272,2048]{1,0:T(8,128)(2,1)} %get-tuple-element.760), channel_id=1, source_target_pairs={{0,2},{2,0},{1,3},{3,1},{4,6},{6,4},{5,7},{7,5},{8,10},{10,8},{9,1... | collective-permute-start | bytes 3342344 | tf_op jit(solution)/shard_map/ppermute | solution.py:456
  385.8 26.2 %collective-permute-start.87 = (bf16[136,2048]{1,0:T(8,128)(2,1)S(1)}, bf16[136,2048]{1,0:T(8,128)(2,1)}, u32[]{:S(2)}, u32[]{:S(2)}) collective-permute-start(bf16[136,2048]{1,0:T(8,128)(2,1)S(1)} %copy-done.52), channel_id=1, source_target_pairs={{0,2},{2,0},{1,3},{3,1},{4,6},{6,4},{5,7},{7,5},{8,10},{10,8},{9,1... | collective-permute-start | bytes 1671176 | tf_op jit(solution)/shard_map/ppermute | solution.py:456
  392.6 221.9 %reduce-scatter.8.cloned.1.call-start = ((), (), s32[]{:S(2)}) async-start(), calls=%async_computation.10 | async-start | bytes 6291456 | tf_op jit(solution)/shard_map/reduce_scatter | solution.py:1491
  574.7 24.1 %all-to-all-start = ((bf16[16,64,128]{2,1,0:T(8,128)(2,1)}), bf16[16,64,128]{2,1,0:T(8,128)(2,1)S(1)}, u32[]{:S(2)}, u32[]{:S(2)}) async-start(bf16[16,64,128]{2,1,0:T(8,128)(2,1)} %bitcast.39), calls=%async_computation.3 | async-start | bytes 524288 | tf_op jit(solution)/shard_map/all_to_all | solution.py:1629
  598.7 37.3 %all-to-all-start.1 = ((bf16[16,64,384]{2,1,0:T(8,128)(2,1)}), bf16[16,64,384]{2,1,0:T(8,128)(2,1)}, u32[]{:S(2)}, u32[]{:S(2)}) async-start(bf16[16,64,384]{2,1,0:T(8,128)(2,1)} %bitcast.153), calls=%async_computation.4 | async-start | bytes 1572864 | tf_op jit(solution)/shard_map/all_to_all | solution.py:1629
  (209 other events, 1887.0 us)
Sparse Core Ops, SparseCore 0:
  36.9 65.2 all-gather.3
  103.8 56.5 all-gather.5
  161.9 56.7 all-gather.7
  352.6 54.2 reduce-scatter.3
  409.8 54.3 reduce-scatter.5
  508.3 58.0 reduce-scatter.7

commit v5 on v4

--- a/solution.py
+++ b/solution.py
@@ -1403,6 +1403,10 @@
         jnp.concatenate([sum_parts[step] for step in WIDE_CHUNKS], axis=1),
         [([all_tags], rope_job)],
     )
+    grads_rows = Gather(cotangent[0], -1)
+    grads_inputs, grads_step = grads_rows.job()
+    (square,), grads_inputs = fence([square], grads_inputs)
+    grads_moved = grads_step(*grads_inputs)
     inverse = lax.rsqrt(square + epsilon)
     gains = jnp.stack([g_query, g_key], axis=0)
     q_rot, k_rot, v_low = rotate_rows(lin, inverse, gains, cosine, sine_part)
@@ -1424,10 +1428,15 @@
         return [*made, projected(FAR, made)]
 
     (out_pair,) = other_core(out_weight)
-    grads_rows = Gather(cotangent[0], -1)
-    (*heads[FAR], far_terms), heads[FAR - 1] = window(
-        [grads_rows], [([q_rot, k_rot, v_low], first_job), attend_job(FAR - 1)]
-    )
+    (*heads[FAR], far_terms), heads[FAR - 1], grads_moved = window(
+        [],
+        [
+            ([q_rot, k_rot, v_low], first_job),
+            attend_job(FAR - 1),
+            ([], lambda: grads_moved),
+        ],
+    )
+    grads_rows.take(grads_moved)
 
     def out_terms(step, *parts):
         return (far_terms if step == FAR else projected(step, parts)), None
@@ -1498,7 +1507,7 @@
     mix_sum = Scatter(lambda step: mix_terms[step], ready=True, far_by=-1)
     ((gate_wgrad,),) = window([dx_sum, mix_sum], [([all_h_two, gate_grad], wgrad)])
     s_gate = over_sequences(gate_wgrad, 0)
-    ((up_wgrad,),) = window([dx_sum, mix_sum], [([all_h_two, up_grad], wgrad)])
+    ((up_wgrad,),) = window([dx_sum], [([all_h_two, up_grad], wgrad)])
     s_up = over_sequences(up_wgrad, 0)
     ((down_wgrad,),) = window([dx_sum], [([act_low, all_grads], wgrad)])
     s_down = over_sequences(down_wgrad, 1)
@@ -1554,7 +1563,7 @@
         )
 
     besides = {0: [], 1: [mix_sum], 2: [], 3: [mix_sum]}
-    also = {1: [([h_two, logit_grad, ffn_gain_grad], narrow_job), ([s_gate], widen)]}
+    also = {0: [([s_gate], widen)], 1: [([h_two, logit_grad, ffn_gain_grad], narrow_job)]}
     for step in range(FAR + 1):
         if step == FAR:
             *made, k_sums = back_job(step, lambda: rows_da.chunks[FAR])[1]()
@@ -1562,8 +1571,10 @@
             made, *wide = window(
                 [rows_da] + besides[step], [back_job(step, lambda: rows_da.now)] + also.get(step, [])
             )
+            if step == 0:
+                ((s_gate,),) = wide
             if step == 1:
-                (narrow,), (s_gate,) = wide
+                ((narrow,),) = wide
         sofar, q_sums[step] = tuple(made[:4]), made[4]
     dq, all_branch, dk, dv = sofar
 
@@ -1587,7 +1598,9 @@
             ([all_h_one, dv], value_job),
         ],
     )
-    layer_out = (middle + mix_sum.total).astype(low)
+    mix_inputs, mix_step = mix_sum.job()
+    (along,), mix_inputs = fence([along], mix_inputs)
+    mix_moved = mix_step(*mix_inputs)
     lin_grad, lin_mine, lin_theirs = lin_back_rows(dq, dk, dv, lin, inverse, along, tok_rows)
     lin_theirs = swap(lin_theirs, "core")
 
@@ -1628,11 +1641,13 @@
         blocks = payload.reshape(ctx_count, own_rows, -1)
         return (lax.all_to_all(blocks, ("chip", "core"), 0, 0, tiled=True),)
 
-    (kept, sent), (v_got,) = window(
+    (kept, sent), mix_moved, (v_got,) = window(
         [h_sum],
-        [([all_h_one, lin_grad, narrow, v_term], dense_job)],
+        [([all_h_one, lin_grad, narrow, v_term], dense_job), ([], lambda: mix_moved)],
         loose=[([v_sent], swap_job)],
     )
+    mix_sum.take(mix_moved)
+    layer_out = (middle + mix_sum.total).astype(low)
     (got,), (out_wgrad,), (v_received,) = window(
         [h_sum],
         [([sent], swap_job), ([mixed_low, all_branch], out_job)],

time: 664 us -> 652 us (0.982)
  waiting for transfers between devices: 134 us -> 119 us
    ppermute x60, waiting for transfers between devices: 93.4 us -> 81.3 us  [shift(): return lax.ppermute(array, 'chip', pairs)]
    unnamed x207 -> x213, local copies, waits for them, and re-layouts: 34.7 us -> 33 us
  transfers between devices with their start and end apart: 137 -> 137, of which waited for: 47 -> 42; matrix products, arithmetic and copies ran while one was open for 20% -> 21% of each run, Pallas kernels for 30% -> 30%
where the time goes in v5:
time: 652 us; the launch traced here: 642 us
  Pallas kernels  220 us (34%)
  waiting for transfers between devices  119 us (18%)
  starting transfers between devices  107 us (16%)
  other arithmetic  73.5 us (11%)
  local copies, waits for them, and re-layouts  55.7 us (9%)
  matrix products  50 us (8%)
  between operations  16.4 us (3%)
    pallas_call x29, Pallas kernels, call(): pl.pallas_call(kernel, grid=grid, in_specs=ins + [pl.BlockSpec(memory_spa...  183 us
    ppermute x60, waiting for transfers between devices, shift(): return lax.ppermute(array, 'chip', pairs)  81.3 us
    ppermute x60, starting transfers between devices, shift(): return lax.ppermute(array, 'chip', pairs)  63.6 us
    dot_general x4, matrix products, contract_rows(): lax.dot_general(left, right, (((0,), (0,)), ((), ())), preferred_element_...  47.2 us
    pallas_call x5, Pallas kernels, attend_back_chunk(): pl.pallas_call(kernel, grid=(1,), in_specs=ins + [whole(part) for part in...  36.2 us
    unnamed x213, local copies, waits for them, and re-layouts  33 us
    ppermute x61, waiting for transfers between devices, swap(): return lax.ppermute(array, axis, [(0, 1), (1, 0)])  29.4 us
    convert_element_type x12, other arithmetic, take(): (term(1) + moved[1]).astype(jnp.bfloat16)  26.5 us
  transfers between devices with their start and end apart: 137, of which 42 were waited for; matrix products, arithmetic and copies ran while one was open for 21% of the time, Pallas kernels for 30%

profile of v5, /device:TPU:8, one launch (start us, length us, event | category | flops | bytes accessed | tf_op | source)
XLA Modules:
  0.0 641.6 jit_solution(5141779427682292845)
XLA Ops:
  19.0 16.3 %collective-permute-done.3 = bf16[19,1024]{1,0:T(8,128)(2,1)S(1)} collective-permute-done((bf16[19,1024]{1,0:T(8,128)(2,1)S(1)}, bf16[19,1024]{1,0:T(8,128)(2,1)S(1)}, u32[]{:S(2)}, u32[]{:S(2)}) %collective-permute-start.3) | collective-permute-done | bytes 38944 | tf_op jit(solution)/shard_map/ppermute | solution.py:456
  63.3 6.5 %collective-permute-done.10.refs_0_ = bf16[136,2048]{1,0:T(8,128)(2,1)S(1)} collective-permute-done((bf16[136,2048]{1,0:T(8,128)(2,1)S(1)}, bf16[136,2048]{1,0:T(8,128)(2,1)S(1)}, u32[]{:S(2)}, u32[]{:S(2)}) %collective-permute-start.10) | collective-permute-done | bytes 557088 | tf_op jit(solution)/shard_map/ppermute | solution.py:461
  168.3 6.0 collective-permute-done.37
  181.4 6.5 %collective-permute-done.40 = bf16[128,2048]{1,0:T(8,128)(2,1)S(1)} collective-permute-done((bf16[128,2048]{1,0:T(8,128)(2,1)S(1)}, bf16[128,2048]{1,0:T(8,128)(2,1)S(1)}, u32[]{:S(2)}, u32[]{:S(2)}) %collective-permute-start.40) | collective-permute-done | bytes 524320 | tf_op jit(solution)/shard_map/ppermute | solution.py:461
  192.4 9.0 %collective-permute-done.43.refs_2_ = bf16[128,2048]{1,0:T(8,128)(2,1)} collective-permute-done((bf16[128,2048]{1,0:T(8,128)(2,1)S(1)}, bf16[128,2048]{1,0:T(8,128)(2,1)}, u32[]{:S(2)}, u32[]{:S(2)}) %collective-permute-start.43) | collective-permute-done | bytes 524320 | tf_op jit(solution)/shard_map/ppermute | solution.py:461
  210.5 8.1 %all-gather.8.cloned.1.call-done.refs_13_.refs_16_ = bf16[1024,2048]{1,0:T(8,128)(2,1)} async-done(((bf16[1024,1024]{1,0:T(8,128)(2,1)}), bf16[1024,2048]{1,0:T(8,128)(2,1)}) %all-gather.8.cloned.1.call-update) | async-done | bytes 4194320 | tf_op jit(solution)/shard_map/all_gather | solution.py:1360
  221.8 22.9 %expert.4 = (bf16[2048,2048]{1,0:T(8,128)(2,1)}, bf16[2048,2048]{1,0:T(8,128)(2,1)}, bf16[2048,1024]{1,0:T(8,128)(2,1)}, bf16[2048,1024]{1,0:T(8,128)(2,1)}, bf1...) custom-call(bf16[128,2048]{1,0:T(8,128)(2,1)} %collective-permute-do, ...), custom_call_target="tpu_custom_call" | custom-call | tf_op jit(solution)/shard_map/expert/pallas_call | solution.py:632
  253.2 22.9 %expert.5 = (bf16[2048,2048]{1,0:T(8,128)(2,1)}, bf16[2048,2048]{1,0:T(8,128)(2,1)}, bf16[2048,1024]{1,0:T(8,128)(2,1)}, bf16[2048,1024]{1,0:T(8,128)(2,1)}, bf1...) custom-call(bf16[128,2048]{1,0:T(8,128)(2,1)} %collective-permute-do, ...), custom_call_target="tpu_custom_call", output_to_operand_aliasing={{0}: (17, {}), {1}: (18, {}), {2}: (19, {}), {3}: (20, {}),... | custom-call | tf_op jit(solution)/shard_map/expert/pallas_call | solution.py:632
  281.4 22.3 %expert.6 = (bf16[2048,2048]{1,0:T(8,128)(2,1)}, bf16[2048,2048]{1,0:T(8,128)(2,1)}, bf16[2048,1024]{1,0:T(8,128)(2,1)}, bf16[2048,1024]{1,0:T(8,128)(2,1)}, bf1...) custom-call(bf16[128,2048]{1,0:T(8,128)(2,1)S(1)} %collective-permut, ...), custom_call_target="tpu_custom_call", output_to_operand_aliasing={{0}: (17, {}), {1}: (18, {}), {2}: (19, {}), {3}: (20, {}),... | custom-call | tf_op jit(solution)/shard_map/expert/pallas_call | solution.py:632
  307.4 22.4 %expert.7 = (bf16[2048,2048]{1,0:T(8,128)(2,1)}, bf16[2048,2048]{1,0:T(8,128)(2,1)}, bf16[2048,1024]{1,0:T(8,128)(2,1)}, bf16[2048,1024]{1,0:T(8,128)(2,1)}, bf1...) custom-call(bf16[128,2048]{1,0:T(8,128)(2,1)S(1)} %multiply_convert_, ...), custom_call_target="tpu_custom_call", output_to_operand_aliasing={{0}: (17, {}), {1}: (18, {}), {2}: (19, {}), {3}: (20, {}),... | custom-call | tf_op jit(solution)/shard_map/expert/pallas_call | solution.py:632
  337.0 14.0 %convolution_convert_fusion.2 = bf16[2048,1024]{1,0:T(8,128)(2,1)} fusion(bf16[2048,2048]{1,0:T(8,128)(2,1)} %get-tuple-element.748, bf16[2048,1024]{1,0:T(8,128)(2,1)} %get-tuple-element.741), kind=kOutput, calls=%fused_computation.3 | convolution fusion | flops 8592031744 | bytes 16777216 | tf_op jit(solution)/shard_map/dot_general | solution.py:39
  357.1 14.4 %convolution_convert_fusion.1 = bf16[2048,1024]{1,0:T(8,128)(2,1)} fusion(bf16[2048,2048]{1,0:T(8,128)(2,1)} %get-tuple-element.748, bf16[2048,1024]{1,0:T(8,128)(2,1)} %get-tuple-element.749), kind=kOutput, calls=%fused_computation.2 | convolution fusion | flops 8592031744 | bytes 16777216 | tf_op jit(solution)/shard_map/dot_general | solution.py:39
  377.5 14.1 %convolution_convert_fusion = bf16[1024,2048]{1,0:T(8,128)(2,1)} fusion(bf16[2048,1024]{1,0:T(8,128)(2,1)} %get-tuple-element.758, bf16[2048,2048]{1,0:T(8,128)(2,1)} %get-tuple-element.759), kind=kOutput, calls=%fused_computation.1 | convolution fusion | flops 8592031744 | bytes 16777216 | tf_op jit(solution)/shard_map/dot_general | solution.py:39
  396.6 11.6 %collective-permute-done.82 = bf16[136,2048]{1,0:T(8,128)(2,1)S(1)} collective-permute-done((bf16[136,2048]{1,0:T(8,128)(2,1)S(1)}, bf16[136,2048]{1,0:T(8,128)(2,1)S(1)}, u32[]{:S(2)}, u32[]{:S(2)}) %collective-permute-start.82) | collective-permute-done | bytes 557088 | tf_op jit(solution)/shard_map/ppermute | solution.py:461
  441.5 7.8 %attend_back.6 = (f32[2048,128]{1,0:T(8,128)}, bf16[2048,2048]{1,0:T(8,128)(2,1)}, f32[2048,128]{1,0:T(8,128)S(1)}, f32[2048,128]{1,0:T(8,128)S(1)}, f32[8,512]{1,0:T(8,128)S(1)}) custom-call(bf16[128,2048]{1,0:T(8,128)(2,1)} %collective-permute-done.86.refs_0_, ...), custom_call_target="tpu_custom_call", output_to_operand_aliasing={{2}: (13, {}), {3}: (14, {}), {0}: (15, {}), {1}: (16, {})} | custom-call | tf_op jit(solution)/shard_map/attend_back/pallas_call | solution.py:891
  449.5 5.9 collective-permute-done.92
  461.3 8.7 %attend_back.7 = (f32[2048,128]{1,0:T(8,128)}, bf16[2048,2048]{1,0:T(8,128)(2,1)}, f32[2048,128]{1,0:T(8,128)S(1)}, f32[2048,128]{1,0:T(8,128)S(1)}, f32[8,512]{1,0:T(8,128)S(1)}) custom-call(bf16[128,2048]{1,0:T(8,128)(2,1)} %collective-permute-done.89.refs_0_, ...), custom_call_target="tpu_custom_call", output_to_operand_aliasing={{2}: (13, {}), {3}: (14, {}), {0}: (15, {}), {1}: (16, {})} | custom-call | tf_op jit(solution)/shard_map/attend_back/pallas_call | solution.py:891
  476.3 8.5 %attend_back.8 = (f32[2048,128]{1,0:T(8,128)}, bf16[2048,2048]{1,0:T(8,128)(2,1)}, f32[2048,128]{1,0:T(8,128)S(1)}, f32[2048,128]{1,0:T(8,128)S(1)}, f32[8,512]{1,0:T(8,128)S(1)}) custom-call(bf16[128,2048]{1,0:T(8,128)(2,1)S(1)} %collective-permute-done.96.refs_0_, ...), custom_call_target="tpu_custom_call", output_to_operand_aliasing={{2}: (13, {}), {3}: (14, {}), {0}: (15, {}), {1}: (16, {})} | custom-call | tf_op jit(solution)/shard_map/attend_back/pallas_call | solution.py:891
  484.8 7.1 %collective-permute-done.100 = bf16[64,2048]{1,0:T(8,128)(2,1)S(1)} collective-permute-done((bf16[64,2048]{1,0:T(8,128)(2,1)S(1)}, bf16[64,2048]{1,0:T(8,128)(2,1)S(1)}, u32[]{:S(2)}, u32[]{:S(2)}) %collective-permute-start.100) | collective-permute-done | bytes 262176 | tf_op jit(solution)/shard_map/ppermute | solution.py:461
  494.9 6.9 %attend_back.9 = (f32[2048,128]{1,0:T(8,128)}, bf16[2048,2048]{1,0:T(8,128)(2,1)}, f32[2048,128]{1,0:T(8,128)S(1)}, f32[2048,128]{1,0:T(8,128)S(1)}, f32[8,256]{1,0:T(8,128)S(1)}, /*index=5*/f32[8,2048]{1,0:T(8,128)S(1)}) custom-call(bf16[128,2048]{1,0:T(8,128)(2,1)S(1)} %constant_dynamic-, ...), custom_call_target="tpu_custom_call", output_to_operand_aliasing={{2}: (14, {}), {3}: (15, {}), {0}: (16, {}), {1}: (17, {})} | custom-call | tf_op jit(solution)/shard_map/attend_back/pallas_call | solution.py:891
  510.0 9.0 %dense.2 = (f32[1024,128]{1,0:T(8,128)S(1)}, bf16[1024,128]{1,0:T(8,128)(2,1)S(1)}, f32[2048,1]{1,0:T(8,128)S(1)}) custom-call(s32[1]{0:T(128)} %bitcast.32.part_ref, bf16[2048,2048]{1,0:T(8,128)(2,1)} %get-tuple-element.883.h_ref, f32[2048,128]{1,0:T(8,128)} %copy-done.5, bf16[2048,384]{1,0:T(8,128)(2,1)} %maximum_select_fusion.refs_4_.weight_ref.left_weight_ref), custom_call_target="tpu_custom_call" | custom-call | flops 1073741824 | bytes 9961472 | tf_op jit(solution)/shard_map/dense/pallas_call | solution.py:632
  545.2 10.2 %dense.3 = (f32[1024,384]{1,0:T(8,128)S(1)}, bf16[1024,384]{1,0:T(8,128)(2,1)S(1)}) custom-call(s32[1]{0:T(128)} %bitcast.32.part_ref, bf16[2048,2048]{1,0:T(8,128)(2,1)} %get-tuple-element.883.h_ref, bf16[2048,256]{1,0:T(8,128)(2,1)} %slice.561.grads_ref, bf16[2048,384]{1,0:T(8,128)(2,1)} %maximum_select_fusion.refs_4_.weight_ref.left_weight_ref, ...), custom_call_target="tpu_custom_call" | custom-call | flops 2147483648 | bytes 13107200 | tf_op jit(solution)/shard_map/dense/pallas_call | solution.py:632
  562.1 6.1 all-to-all-start
  614.8 6.6 %collective-permute-done.125.ahead_ref = bf16[128,2048]{1,0:T(8,128)(2,1)S(1)} collective-permute-done((bf16[128,2048]{1,0:T(8,128)(2,1)}, bf16[128,2048]{1,0:T(8,128)(2,1)S(1)}, u32[]{:S(2)}, u32[]{:S(2)}) %collective-permute-start.125) | collective-permute-done | bytes 524320 | tf_op jit(solution)/shard_map/ppermute | solution.py:461
  (670 shorter events, 351.0 us)
Async XLA Ops:
  7.2 133.7 %all-gather.4.cloned.1.call-start = ((), (), s32[]{:S(2)}) async-start(), calls=%async_computation.5 | async-start | bytes 6291456 | tf_op jit(solution)/shard_map/all_gather | solution.py:1360
  36.8 173.7 %all-gather.6.cloned.1.call-start = ((), (), s32[]{:S(2)}) async-start(), calls=%async_computation.6 | async-start | bytes 6291456 | tf_op jit(solution)/shard_map/all_gather | solution.py:1360
  84.0 134.6 %all-gather.8.cloned.1.call-start = ((), (), s32[]{:S(2)}) async-start(), calls=%async_computation.7 | async-start | bytes 6291456 | tf_op jit(solution)/shard_map/all_gather | solution.py:1360
  132.0 281.3 %reduce-scatter.4.cloned.1.call-start = ((), (), s32[]{:S(2)}) async-start(), calls=%async_computation.8 | async-start | bytes 6291456 | tf_op jit(solution)/shard_map/reduce_scatter | solution.py:1500
  202.7 45.0 %collective-permute-start.46 = (bf16[128,2048]{1,0:T(8,128)(2,1)}, bf16[128,2048]{1,0:T(8,128)(2,1)S(1)}, u32[]{:S(2)}, u32[]{:S(2)}) collective-permute-start(bf16[128,2048]{1,0:T(8,128)(2,1)} %collective-permute-done.43.refs_2_), channel_id=1, source_target_pairs={{0,8},{8,16},{16,24},{24,28},{28,20},{20,12},{12,4},{4,0},{1,9},{9... | collective-permute-start | bytes 1572872 | tf_op jit(solution)/shard_map/ppermute | solution.py:461
  204.6 43.1 %collective-permute-start.47 = (bf16[128,2048]{1,0:T(8,128)(2,1)}, bf16[128,2048]{1,0:T(8,128)(2,1)}, u32[]{:S(2)}, u32[]{:S(2)}) collective-permute-start(bf16[128,2048]{1,0:T(8,128)(2,1)} %collective-permute-done.44.refs_0_), channel_id=1, source_target_pairs={{0,4},{8,0},{16,8},{24,16},{28,24},{20,28},{12,20},{4,12},{1,5},{9... | collective-permute-start | bytes 1572872 | tf_op jit(solution)/shard_map/ppermute | solution.py:461
  206.9 40.9 %collective-permute-start.50 = (bf16[128,2048]{1,0:T(8,128)(2,1)S(1)}, bf16[128,2048]{1,0:T(8,128)(2,1)}, u32[]{:S(2)}, u32[]{:S(2)}) collective-permute-start(bf16[128,2048]{1,0:T(8,128)(2,1)S(1)} %collective-permute-done.28.refs_6_), channel_id=1, source_target_pairs={{0,8},{8,16},{16,24},{24,28},{28,20},{20,12},{12,4},{4,0},{1,9},{9... | collective-permute-start | bytes 1572872 | tf_op jit(solution)/shard_map/ppermute | solution.py:461
  208.4 39.3 %collective-permute-start.51 = (bf16[128,2048]{1,0:T(8,128)(2,1)S(1)}, bf16[128,2048]{1,0:T(8,128)(2,1)}, u32[]{:S(2)}, u32[]{:S(2)}) collective-permute-start(bf16[128,2048]{1,0:T(8,128)(2,1)S(1)} %collective-permute-done.29.refs_4_), channel_id=1, source_target_pairs={{0,4},{8,0},{16,8},{24,16},{28,24},{20,28},{12,20},{4,12},{1,5},{9... | collective-permute-start | bytes 1572872 | tf_op jit(solution)/shard_map/ppermute | solution.py:461
  248.8 28.3 %collective-permute-start.54 = (bf16[128,2048]{1,0:T(8,128)(2,1)S(1)}, bf16[128,2048]{1,0:T(8,128)(2,1)S(1)}, u32[]{:S(2)}, u32[]{:S(2)}) collective-permute-start(bf16[128,2048]{1,0:T(8,128)(2,1)S(1)} %collective-permute-done.46.refs_2_), channel_id=1, source_target_pairs={{0,8},{8,16},{16,24},{24,28},{28,20},{20,12},{12,4},{4,0},{1,9},{9... | collective-permute-start | bytes 1572872 | tf_op jit(solution)/shard_map/ppermute | solution.py:461
  250.3 26.8 %collective-permute-start.55 = (bf16[128,2048]{1,0:T(8,128)(2,1)}, bf16[128,2048]{1,0:T(8,128)(2,1)S(1)}, u32[]{:S(2)}, u32[]{:S(2)}) collective-permute-start(bf16[128,2048]{1,0:T(8,128)(2,1)} %collective-permute-done.47.refs_0_), channel_id=1, source_target_pairs={{0,4},{8,0},{16,8},{24,16},{28,24},{20,28},{12,20},{4,12},{1,5},{9... | collective-permute-start | bytes 1572872 | tf_op jit(solution)/shard_map/ppermute | solution.py:461
  251.2 26.0 %collective-permute-start.58 = (bf16[128,2048]{1,0:T(8,128)(2,1)}, bf16[128,2048]{1,0:T(8,128)(2,1)S(1)}, u32[]{:S(2)}, u32[]{:S(2)}) collective-permute-start(bf16[128,2048]{1,0:T(8,128)(2,1)} %collective-permute-done.50.refs_6_), channel_id=1, source_target_pairs={{0,8},{8,16},{16,24},{24,28},{28,20},{20,12},{12,4},{4,0},{1,9},{9... | collective-permute-start | bytes 1572872 | tf_op jit(solution)/shard_map/ppermute | solution.py:461
  252.7 24.5 %collective-permute-start.59 = (bf16[128,2048]{1,0:T(8,128)(2,1)}, bf16[128,2048]{1,0:T(8,128)(2,1)S(1)}, u32[]{:S(2)}, u32[]{:S(2)}) collective-permute-start(bf16[128,2048]{1,0:T(8,128)(2,1)} %collective-permute-done.51.refs_4_), channel_id=1, source_target_pairs={{0,4},{8,0},{16,8},{24,16},{28,24},{20,28},{12,20},{4,12},{1,5},{9... | collective-permute-start | bytes 1572872 | tf_op jit(solution)/shard_map/ppermute | solution.py:461
  278.3 26.5 %collective-permute-start.62 = (bf16[128,2048]{1,0:T(8,128)(2,1)S(1)}, bf16[128,2048]{1,0:T(8,128)(2,1)S(1)}, u32[]{:S(2)}, u32[]{:S(2)}) collective-permute-start(bf16[128,2048]{1,0:T(8,128)(2,1)S(1)} %collective-permute-done.54.refs_2_), channel_id=1, source_target_pairs={{0,8},{8,16},{16,24},{24,28},{28,20},{20,12},{12,4},{4,0},{1,9},{9... | collective-permute-start | bytes 1572872 | tf_op jit(solution)/shard_map/ppermute | solution.py:461
  279.8 25.0 %collective-permute-start.65 = (bf16[128,2048]{1,0:T(8,128)(2,1)S(1)}, bf16[128,2048]{1,0:T(8,128)(2,1)S(1)}, u32[]{:S(2)}, u32[]{:S(2)}) collective-permute-start(bf16[128,2048]{1,0:T(8,128)(2,1)S(1)} %collective-permute-done.59.refs_4_), channel_id=1, source_target_pairs={{0,4},{8,0},{16,8},{24,16},{28,24},{20,28},{12,20},{4,12},{1,5},{9... | collective-permute-start | bytes 1572872 | tf_op jit(solution)/shard_map/ppermute | solution.py:461
  351.1 250.9 %reduce-scatter.6.cloned.1.call-start = ((), (), s32[]{:S(2)}) async-start(), calls=%async_computation.9 | async-start | bytes 6291456 | tf_op jit(solution)/shard_map/reduce_scatter | solution.py:1500
  351.1 40.5 %collective-permute-start.81 = (bf16[272,2048]{1,0:T(8,128)(2,1)}, bf16[272,2048]{1,0:T(8,128)(2,1)}, u32[]{:S(2)}, u32[]{:S(2)}) collective-permute-start(bf16[272,2048]{1,0:T(8,128)(2,1)} %get-tuple-element.757), channel_id=1, source_target_pairs={{0,2},{2,0},{1,3},{3,1},{4,6},{6,4},{5,7},{7,5},{8,10},{10,8},{9,1... | collective-permute-start | bytes 3342344 | tf_op jit(solution)/shard_map/ppermute | solution.py:456
  351.7 44.9 %collective-permute-start.84 = (bf16[136,2048]{1,0:T(8,128)(2,1)}, bf16[136,2048]{1,0:T(8,128)(2,1)}, u32[]{:S(2)}, u32[]{:S(2)}) collective-permute-start(bf16[136,2048]{1,0:T(8,128)(2,1)} %copy-done.51), channel_id=1, source_target_pairs={{0,2},{2,0},{1,3},{3,1},{4,6},{6,4},{5,7},{7,5},{8,10},{10,8},{9,1... | collective-permute-start | bytes 1671176 | tf_op jit(solution)/shard_map/ppermute | solution.py:456
  377.3 224.7 %reduce-scatter.8.cloned.1.call-start = ((), (), s32[]{:S(2)}) async-start(), calls=%async_computation.10 | async-start | bytes 6291456 | tf_op jit(solution)/shard_map/reduce_scatter | solution.py:1500
  432.4 23.0 %collective-permute-start.92 = (bf16[128,2048]{1,0:T(8,128)(2,1)}, bf16[128,2048]{1,0:T(8,128)(2,1)}, u32[]{:S(2)}, u32[]{:S(2)}) collective-permute-start(bf16[128,2048]{1,0:T(8,128)(2,1)} %get-tuple-element.788), channel_id=1, source_target_pairs={{0,8},{8,16},{16,24},{24,28},{28,20},{20,12},{12,4},{4,0},{1,9},{9... | collective-permute-start | bytes 1572872 | tf_op jit(solution)/shard_map/ppermute | solution.py:461
  449.4 35.4 %collective-permute-start.105 = (bf16[256,2048]{1,0:T(8,128)(2,1)S(1)}, bf16[256,2048]{1,0:T(8,128)(2,1)S(1)}, u32[]{:S(2)}, u32[]{:S(2)}) collective-permute-start(bf16[256,2048]{1,0:T(8,128)(2,1)S(1)} %copy-done.50), channel_id=1, source_target_pairs={{0,2},{2,0},{1,3},{3,1},{4,6},{6,4},{5,7},{7,5},{8,10},{10,8},{9,1... | collective-permute-start | bytes 3145736 | tf_op jit(solution)/shard_map/ppermute | solution.py:456
  531.6 23.8 %collective-permute-start.116 = (bf16[128,2048]{1,0:T(8,128)(2,1)}, bf16[128,2048]{1,0:T(8,128)(2,1)S(1)}, u32[]{:S(2)}, u32[]{:S(2)}) collective-permute-start(bf16[128,2048]{1,0:T(8,128)(2,1)} %get-tuple-element.889), channel_id=1, source_target_pairs={{0,8},{8,16},{16,24},{24,28},{28,20},{20,12},{12,4},{4,0},{1,9},{9... | collective-permute-start | bytes 1572872 | tf_op jit(solution)/shard_map/ppermute | solution.py:461
  532.8 22.7 %collective-permute-start.117 = (bf16[128,2048]{1,0:T(8,128)(2,1)}, bf16[128,2048]{1,0:T(8,128)(2,1)S(1)}, u32[]{:S(2)}, u32[]{:S(2)}) collective-permute-start(bf16[128,2048]{1,0:T(8,128)(2,1)} %get-tuple-element.890), channel_id=1, source_target_pairs={{0,4},{8,0},{16,8},{24,16},{28,24},{20,28},{12,20},{4,12},{1,5},{9... | collective-permute-start | bytes 1572872 | tf_op jit(solution)/shard_map/ppermute | solution.py:461
  562.1 24.0 %all-to-all-start = ((bf16[16,64,128]{2,1,0:T(8,128)(2,1)}), bf16[16,64,128]{2,1,0:T(8,128)(2,1)S(1)}, u32[]{:S(2)}, u32[]{:S(2)}) async-start(bf16[16,64,128]{2,1,0:T(8,128)(2,1)} %bitcast.38), calls=%async_computation.3 | async-start | bytes 524288 | tf_op jit(solution)/shard_map/all_to_all | solution.py:1642
  586.1 37.5 %all-to-all-start.1 = ((bf16[16,64,384]{2,1,0:T(8,128)(2,1)}), bf16[16,64,384]{2,1,0:T(8,128)(2,1)}, u32[]{:S(2)}, u32[]{:S(2)}) async-start(bf16[16,64,384]{2,1,0:T(8,128)(2,1)} %bitcast.153), calls=%async_computation.4 | async-start | bytes 1572864 | tf_op jit(solution)/shard_map/all_to_all | solution.py:1642
  (212 other events, 1907.8 us)
Sparse Core Ops, SparseCore 0:
  36.9 65.1 all-gather.3
  103.7 56.5 all-gather.5
  161.8 56.7 all-gather.7
  351.2 54.2 reduce-scatter.3
  408.4 54.2 reduce-scatter.5
  493.1 56.1 reduce-scatter.7

commit v6 on v5

--- a/solution.py
+++ b/solution.py
@@ -1641,9 +1641,13 @@
         blocks = payload.reshape(ctx_count, own_rows, -1)
         return (lax.all_to_all(blocks, ("chip", "core"), 0, 0, tiled=True),)
 
-    (kept, sent), mix_moved, (v_got,) = window(
+    (kept, sent), mix_moved, (s_up,), (v_got,) = window(
         [h_sum],
-        [([all_h_one, lin_grad, narrow, v_term], dense_job), ([], lambda: mix_moved)],
+        [
+            ([all_h_one, lin_grad, narrow, v_term], dense_job),
+            ([], lambda: mix_moved),
+            ([s_up], widen),
+        ],
         loose=[([v_sent], swap_job)],
     )
     mix_sum.take(mix_moved)
@@ -1662,13 +1666,12 @@
         ],
     )
 
-    (v_received,), (received,), (out_got, gain_got), (s_up,), (s_down,) = window(
+    (v_received,), (received,), (out_got, gain_got), (s_down,) = window(
         [h_sum],
         [
             ([], lambda: (v_received,)),
             ([], lambda: (received,)),
             ([], lambda: (out_got, gain_got)),
-            ([s_up], widen),
             ([s_down], widen),
         ],
     )

time: 652 us -> 657 us (level)
    unnamed x213 -> x203, local copies, waits for them, and re-layouts: 33 us -> 33 us
where the time goes in v6:
time: 657 us; the launch traced here: 647 us
  Pallas kernels  219 us (33%)
  waiting for transfers between devices  121 us (18%)
  starting transfers between devices  108 us (16%)
  other arithmetic  73.8 us (11%)
  local copies, waits for them, and re-layouts  58.4 us (9%)
  matrix products  50.1 us (8%)
  between operations  16.4 us (2%)
    pallas_call x29, Pallas kernels, call(): pl.pallas_call(kernel, grid=grid, in_specs=ins + [pl.BlockSpec(memory_spa...  183 us
    ppermute x60, waiting for transfers between devices, shift(): return lax.ppermute(array, 'chip', pairs)  83.3 us
    ppermute x60, starting transfers between devices, shift(): return lax.ppermute(array, 'chip', pairs)  63.5 us
    dot_general x4, matrix products, contract_rows(): lax.dot_general(left, right, (((0,), (0,)), ((), ())), preferred_element_...  47.2 us
    pallas_call x5, Pallas kernels, attend_back_chunk(): pl.pallas_call(kernel, grid=(1,), in_specs=ins + [whole(part) for part in...  36.2 us
    unnamed x203, local copies, waits for them, and re-layouts  33 us
    ppermute x61, waiting for transfers between devices, swap(): return lax.ppermute(array, axis, [(0, 1), (1, 0)])  29.5 us
    convert_element_type x12, other arithmetic, take(): (term(1) + moved[1]).astype(jnp.bfloat16)  26.5 us
  transfers between devices with their start and end apart: 137, of which 42 were waited for; matrix products, arithmetic and copies ran while one was open for 21% of the time, Pallas kernels for 30%

profile of v6, /device:TPU:8, one launch (start us, length us, event | category | flops | bytes accessed | tf_op | source)
XLA Modules:
  0.0 646.8 jit_solution(8996169788370599467)
XLA Ops:
  19.0 16.3 %collective-permute-done.3 = bf16[19,1024]{1,0:T(8,128)(2,1)S(1)} collective-permute-done((bf16[19,1024]{1,0:T(8,128)(2,1)S(1)}, bf16[19,1024]{1,0:T(8,128)(2,1)S(1)}, u32[]{:S(2)}, u32[]{:S(2)}) %collective-permute-start.3) | collective-permute-done | bytes 38944 | tf_op jit(solution)/shard_map/ppermute | solution.py:456
  63.4 6.5 collective-permute-done.10.refs_0_
  168.3 6.0 collective-permute-done.37
  181.5 6.5 %collective-permute-done.40 = bf16[128,2048]{1,0:T(8,128)(2,1)S(1)} collective-permute-done((bf16[128,2048]{1,0:T(8,128)(2,1)S(1)}, bf16[128,2048]{1,0:T(8,128)(2,1)S(1)}, u32[]{:S(2)}, u32[]{:S(2)}) %collective-permute-start.40) | collective-permute-done | bytes 524320 | tf_op jit(solution)/shard_map/ppermute | solution.py:461
  192.4 9.0 %collective-permute-done.43.refs_2_ = bf16[128,2048]{1,0:T(8,128)(2,1)} collective-permute-done((bf16[128,2048]{1,0:T(8,128)(2,1)S(1)}, bf16[128,2048]{1,0:T(8,128)(2,1)}, u32[]{:S(2)}, u32[]{:S(2)}) %collective-permute-start.43) | collective-permute-done | bytes 524320 | tf_op jit(solution)/shard_map/ppermute | solution.py:461
  210.5 8.2 %all-gather.8.cloned.1.call-done.refs_13_.refs_16_ = bf16[1024,2048]{1,0:T(8,128)(2,1)} async-done(((bf16[1024,1024]{1,0:T(8,128)(2,1)}), bf16[1024,2048]{1,0:T(8,128)(2,1)}) %all-gather.8.cloned.1.call-update) | async-done | bytes 4194320 | tf_op jit(solution)/shard_map/all_gather | solution.py:1360
  221.8 22.9 %expert.4 = (bf16[2048,2048]{1,0:T(8,128)(2,1)}, bf16[2048,2048]{1,0:T(8,128)(2,1)}, bf16[2048,1024]{1,0:T(8,128)(2,1)}, bf16[2048,1024]{1,0:T(8,128)(2,1)}, bf1...) custom-call(bf16[128,2048]{1,0:T(8,128)(2,1)} %collective-permute-do, ...), custom_call_target="tpu_custom_call" | custom-call | tf_op jit(solution)/shard_map/expert/pallas_call | solution.py:632
  253.3 22.8 %expert.5 = (bf16[2048,2048]{1,0:T(8,128)(2,1)}, bf16[2048,2048]{1,0:T(8,128)(2,1)}, bf16[2048,1024]{1,0:T(8,128)(2,1)}, bf16[2048,1024]{1,0:T(8,128)(2,1)}, bf1...) custom-call(bf16[128,2048]{1,0:T(8,128)(2,1)} %collective-permute-do, ...), custom_call_target="tpu_custom_call", output_to_operand_aliasing={{0}: (17, {}), {1}: (18, {}), {2}: (19, {}), {3}: (20, {}),... | custom-call | tf_op jit(solution)/shard_map/expert/pallas_call | solution.py:632
  281.4 22.4 %expert.6 = (bf16[2048,2048]{1,0:T(8,128)(2,1)}, bf16[2048,2048]{1,0:T(8,128)(2,1)}, bf16[2048,1024]{1,0:T(8,128)(2,1)}, bf16[2048,1024]{1,0:T(8,128)(2,1)}, bf1...) custom-call(bf16[128,2048]{1,0:T(8,128)(2,1)S(1)} %collective-permut, ...), custom_call_target="tpu_custom_call", output_to_operand_aliasing={{0}: (17, {}), {1}: (18, {}), {2}: (19, {}), {3}: (20, {}),... | custom-call | tf_op jit(solution)/shard_map/expert/pallas_call | solution.py:632
  307.5 22.3 %expert.7 = (bf16[2048,2048]{1,0:T(8,128)(2,1)}, bf16[2048,2048]{1,0:T(8,128)(2,1)}, bf16[2048,1024]{1,0:T(8,128)(2,1)}, bf16[2048,1024]{1,0:T(8,128)(2,1)}, bf1...) custom-call(bf16[128,2048]{1,0:T(8,128)(2,1)S(1)} %multiply_convert_, ...), custom_call_target="tpu_custom_call", output_to_operand_aliasing={{0}: (17, {}), {1}: (18, {}), {2}: (19, {}), {3}: (20, {}),... | custom-call | tf_op jit(solution)/shard_map/expert/pallas_call | solution.py:632
  337.0 14.0 %convolution_convert_fusion.2 = bf16[2048,1024]{1,0:T(8,128)(2,1)} fusion(bf16[2048,2048]{1,0:T(8,128)(2,1)} %get-tuple-element.748, bf16[2048,1024]{1,0:T(8,128)(2,1)} %get-tuple-element.741), kind=kOutput, calls=%fused_computation.3 | convolution fusion | flops 8592031744 | bytes 16777216 | tf_op jit(solution)/shard_map/dot_general | solution.py:39
  357.2 14.4 %convolution_convert_fusion.1 = bf16[2048,1024]{1,0:T(8,128)(2,1)} fusion(bf16[2048,2048]{1,0:T(8,128)(2,1)} %get-tuple-element.748, bf16[2048,1024]{1,0:T(8,128)(2,1)} %get-tuple-element.749), kind=kOutput, calls=%fused_computation.2 | convolution fusion | flops 8592031744 | bytes 16777216 | tf_op jit(solution)/shard_map/dot_general | solution.py:39
  377.6 14.2 %convolution_convert_fusion = bf16[1024,2048]{1,0:T(8,128)(2,1)} fusion(bf16[2048,1024]{1,0:T(8,128)(2,1)} %get-tuple-element.758, bf16[2048,2048]{1,0:T(8,128)(2,1)} %get-tuple-element.759), kind=kOutput, calls=%fused_computation.1 | convolution fusion | flops 8592031744 | bytes 16777216 | tf_op jit(solution)/shard_map/dot_general | solution.py:39
  396.7 11.6 %collective-permute-done.82 = bf16[136,2048]{1,0:T(8,128)(2,1)S(1)} collective-permute-done((bf16[136,2048]{1,0:T(8,128)(2,1)S(1)}, bf16[136,2048]{1,0:T(8,128)(2,1)S(1)}, u32[]{:S(2)}, u32[]{:S(2)}) %collective-permute-start.82) | collective-permute-done | bytes 557088 | tf_op jit(solution)/shard_map/ppermute | solution.py:461
  441.6 7.8 %attend_back.6 = (f32[2048,128]{1,0:T(8,128)}, bf16[2048,2048]{1,0:T(8,128)(2,1)}, f32[2048,128]{1,0:T(8,128)S(1)}, f32[2048,128]{1,0:T(8,128)S(1)}, f32[8,512]{1,0:T(8,128)S(1)}) custom-call(bf16[128,2048]{1,0:T(8,128)(2,1)} %collective-permute-done.86.refs_0_, ...), custom_call_target="tpu_custom_call", output_to_operand_aliasing={{2}: (13, {}), {3}: (14, {}), {0}: (15, {}), {1}: (16, {})} | custom-call | tf_op jit(solution)/shard_map/attend_back/pallas_call | solution.py:891
  461.4 8.7 %attend_back.7 = (f32[2048,128]{1,0:T(8,128)}, bf16[2048,2048]{1,0:T(8,128)(2,1)}, f32[2048,128]{1,0:T(8,128)S(1)}, f32[2048,128]{1,0:T(8,128)S(1)}, f32[8,512]{1,0:T(8,128)S(1)}) custom-call(bf16[128,2048]{1,0:T(8,128)(2,1)} %collective-permute-done.89.refs_0_, ...), custom_call_target="tpu_custom_call", output_to_operand_aliasing={{2}: (13, {}), {3}: (14, {}), {0}: (15, {}), {1}: (16, {})} | custom-call | tf_op jit(solution)/shard_map/attend_back/pallas_call | solution.py:891
  476.4 8.5 %attend_back.8 = (f32[2048,128]{1,0:T(8,128)}, bf16[2048,2048]{1,0:T(8,128)(2,1)}, f32[2048,128]{1,0:T(8,128)S(1)}, f32[2048,128]{1,0:T(8,128)S(1)}, f32[8,512]{1,0:T(8,128)S(1)}) custom-call(bf16[128,2048]{1,0:T(8,128)(2,1)S(1)} %collective-permute-done.96.refs_0_, ...), custom_call_target="tpu_custom_call", output_to_operand_aliasing={{2}: (13, {}), {3}: (14, {}), {0}: (15, {}), {1}: (16, {})} | custom-call | tf_op jit(solution)/shard_map/attend_back/pallas_call | solution.py:891
  484.9 7.1 %collective-permute-done.100 = bf16[64,2048]{1,0:T(8,128)(2,1)S(1)} collective-permute-done((bf16[64,2048]{1,0:T(8,128)(2,1)S(1)}, bf16[64,2048]{1,0:T(8,128)(2,1)S(1)}, u32[]{:S(2)}, u32[]{:S(2)}) %collective-permute-start.100) | collective-permute-done | bytes 262176 | tf_op jit(solution)/shard_map/ppermute | solution.py:461
  495.0 6.9 %attend_back.9 = (f32[2048,128]{1,0:T(8,128)}, bf16[2048,2048]{1,0:T(8,128)(2,1)}, f32[2048,128]{1,0:T(8,128)S(1)}, f32[2048,128]{1,0:T(8,128)S(1)}, f32[8,256]{1,0:T(8,128)S(1)}, /*index=5*/f32[8,2048]{1,0:T(8,128)S(1)}) custom-call(bf16[128,2048]{1,0:T(8,128)(2,1)S(1)} %constant_dynamic-, ...), custom_call_target="tpu_custom_call", output_to_operand_aliasing={{2}: (14, {}), {3}: (15, {}), {0}: (16, {}), {1}: (17, {})} | custom-call | tf_op jit(solution)/shard_map/attend_back/pallas_call | solution.py:891
  510.1 9.0 %dense.2 = (f32[1024,128]{1,0:T(8,128)S(1)}, bf16[1024,128]{1,0:T(8,128)(2,1)S(1)}, f32[2048,1]{1,0:T(8,128)S(1)}) custom-call(s32[1]{0:T(128)} %bitcast.32.part_ref, bf16[2048,2048]{1,0:T(8,128)(2,1)} %get-tuple-element.884.h_ref, f32[2048,128]{1,0:T(8,128)} %copy-done.5, bf16[2048,384]{1,0:T(8,128)(2,1)} %maximum_select_fusion.refs_4_.weight_ref.left_weight_ref), custom_call_target="tpu_custom_call" | custom-call | flops 1073741824 | bytes 9961472 | tf_op jit(solution)/shard_map/dense/pallas_call | solution.py:632
  550.2 10.2 %dense.3 = (f32[1024,384]{1,0:T(8,128)S(1)}, bf16[1024,384]{1,0:T(8,128)(2,1)S(1)}) custom-call(s32[1]{0:T(128)} %bitcast.32.part_ref, bf16[2048,2048]{1,0:T(8,128)(2,1)} %get-tuple-element.884.h_ref, bf16[2048,256]{1,0:T(8,128)(2,1)} %slice.561.grads_ref, bf16[2048,384]{1,0:T(8,128)(2,1)} %maximum_select_fusion.refs_4_.weight_ref.left_weight_ref, ...), custom_call_target="tpu_custom_call" | custom-call | flops 2147483648 | bytes 13107200 | tf_op jit(solution)/shard_map/dense/pallas_call | solution.py:632
  567.1 6.2 all-to-all-start
  590.9 6.0 all-to-all-start.1
  617.6 9.0 %collective-permute-done.125.ahead_ref = bf16[128,2048]{1,0:T(8,128)(2,1)S(1)} collective-permute-done((bf16[128,2048]{1,0:T(8,128)(2,1)}, bf16[128,2048]{1,0:T(8,128)(2,1)S(1)}, u32[]{:S(2)}, u32[]{:S(2)}) %collective-permute-start.125) | collective-permute-done | bytes 524320 | tf_op jit(solution)/shard_map/ppermute | solution.py:461
  (660 shorter events, 353.9 us)
Async XLA Ops:
  7.2 133.7 %all-gather.4.cloned.1.call-start = ((), (), s32[]{:S(2)}) async-start(), calls=%async_computation.5 | async-start | bytes 6291456 | tf_op jit(solution)/shard_map/all_gather | solution.py:1360
  36.8 173.7 %all-gather.6.cloned.1.call-start = ((), (), s32[]{:S(2)}) async-start(), calls=%async_computation.6 | async-start | bytes 6291456 | tf_op jit(solution)/shard_map/all_gather | solution.py:1360
  83.9 134.8 %all-gather.8.cloned.1.call-start = ((), (), s32[]{:S(2)}) async-start(), calls=%async_computation.7 | async-start | bytes 6291456 | tf_op jit(solution)/shard_map/all_gather | solution.py:1360
  132.0 281.4 %reduce-scatter.4.cloned.1.call-start = ((), (), s32[]{:S(2)}) async-start(), calls=%async_computation.8 | async-start | bytes 6291456 | tf_op jit(solution)/shard_map/reduce_scatter | solution.py:1500
  202.7 45.0 %collective-permute-start.46 = (bf16[128,2048]{1,0:T(8,128)(2,1)}, bf16[128,2048]{1,0:T(8,128)(2,1)S(1)}, u32[]{:S(2)}, u32[]{:S(2)}) collective-permute-start(bf16[128,2048]{1,0:T(8,128)(2,1)} %collective-permute-done.43.refs_2_), channel_id=1, source_target_pairs={{0,8},{8,16},{16,24},{24,28},{28,20},{20,12},{12,4},{4,0},{1,9},{9... | collective-permute-start | bytes 1572872 | tf_op jit(solution)/shard_map/ppermute | solution.py:461
  204.6 43.1 %collective-permute-start.47 = (bf16[128,2048]{1,0:T(8,128)(2,1)}, bf16[128,2048]{1,0:T(8,128)(2,1)}, u32[]{:S(2)}, u32[]{:S(2)}) collective-permute-start(bf16[128,2048]{1,0:T(8,128)(2,1)} %collective-permute-done.44.refs_0_), channel_id=1, source_target_pairs={{0,4},{8,0},{16,8},{24,16},{28,24},{20,28},{12,20},{4,12},{1,5},{9... | collective-permute-start | bytes 1572872 | tf_op jit(solution)/shard_map/ppermute | solution.py:461
  206.9 40.9 %collective-permute-start.50 = (bf16[128,2048]{1,0:T(8,128)(2,1)S(1)}, bf16[128,2048]{1,0:T(8,128)(2,1)}, u32[]{:S(2)}, u32[]{:S(2)}) collective-permute-start(bf16[128,2048]{1,0:T(8,128)(2,1)S(1)} %collective-permute-done.28.refs_6_), channel_id=1, source_target_pairs={{0,8},{8,16},{16,24},{24,28},{28,20},{20,12},{12,4},{4,0},{1,9},{9... | collective-permute-start | bytes 1572872 | tf_op jit(solution)/shard_map/ppermute | solution.py:461
  208.4 39.4 %collective-permute-start.51 = (bf16[128,2048]{1,0:T(8,128)(2,1)S(1)}, bf16[128,2048]{1,0:T(8,128)(2,1)}, u32[]{:S(2)}, u32[]{:S(2)}) collective-permute-start(bf16[128,2048]{1,0:T(8,128)(2,1)S(1)} %collective-permute-done.29.refs_4_), channel_id=1, source_target_pairs={{0,4},{8,0},{16,8},{24,16},{28,24},{20,28},{12,20},{4,12},{1,5},{9... | collective-permute-start | bytes 1572872 | tf_op jit(solution)/shard_map/ppermute | solution.py:461
  248.9 28.3 %collective-permute-start.54 = (bf16[128,2048]{1,0:T(8,128)(2,1)S(1)}, bf16[128,2048]{1,0:T(8,128)(2,1)S(1)}, u32[]{:S(2)}, u32[]{:S(2)}) collective-permute-start(bf16[128,2048]{1,0:T(8,128)(2,1)S(1)} %collective-permute-done.46.refs_2_), channel_id=1, source_target_pairs={{0,8},{8,16},{16,24},{24,28},{28,20},{20,12},{12,4},{4,0},{1,9},{9... | collective-permute-start | bytes 1572872 | tf_op jit(solution)/shard_map/ppermute | solution.py:461
  250.4 26.8 %collective-permute-start.55 = (bf16[128,2048]{1,0:T(8,128)(2,1)}, bf16[128,2048]{1,0:T(8,128)(2,1)S(1)}, u32[]{:S(2)}, u32[]{:S(2)}) collective-permute-start(bf16[128,2048]{1,0:T(8,128)(2,1)} %collective-permute-done.47.refs_0_), channel_id=1, source_target_pairs={{0,4},{8,0},{16,8},{24,16},{28,24},{20,28},{12,20},{4,12},{1,5},{9... | collective-permute-start | bytes 1572872 | tf_op jit(solution)/shard_map/ppermute | solution.py:461
  251.3 25.9 %collective-permute-start.58 = (bf16[128,2048]{1,0:T(8,128)(2,1)}, bf16[128,2048]{1,0:T(8,128)(2,1)S(1)}, u32[]{:S(2)}, u32[]{:S(2)}) collective-permute-start(bf16[128,2048]{1,0:T(8,128)(2,1)} %collective-permute-done.50.refs_6_), channel_id=1, source_target_pairs={{0,8},{8,16},{16,24},{24,28},{28,20},{20,12},{12,4},{4,0},{1,9},{9... | collective-permute-start | bytes 1572872 | tf_op jit(solution)/shard_map/ppermute | solution.py:461
  252.7 24.4 %collective-permute-start.59 = (bf16[128,2048]{1,0:T(8,128)(2,1)}, bf16[128,2048]{1,0:T(8,128)(2,1)S(1)}, u32[]{:S(2)}, u32[]{:S(2)}) collective-permute-start(bf16[128,2048]{1,0:T(8,128)(2,1)} %collective-permute-done.51.refs_4_), channel_id=1, source_target_pairs={{0,4},{8,0},{16,8},{24,16},{28,24},{20,28},{12,20},{4,12},{1,5},{9... | collective-permute-start | bytes 1572872 | tf_op jit(solution)/shard_map/ppermute | solution.py:461
  278.3 26.5 %collective-permute-start.62 = (bf16[128,2048]{1,0:T(8,128)(2,1)S(1)}, bf16[128,2048]{1,0:T(8,128)(2,1)S(1)}, u32[]{:S(2)}, u32[]{:S(2)}) collective-permute-start(bf16[128,2048]{1,0:T(8,128)(2,1)S(1)} %collective-permute-done.54.refs_2_), channel_id=1, source_target_pairs={{0,8},{8,16},{16,24},{24,28},{28,20},{20,12},{12,4},{4,0},{1,9},{9... | collective-permute-start | bytes 1572872 | tf_op jit(solution)/shard_map/ppermute | solution.py:461
  279.7 25.1 %collective-permute-start.65 = (bf16[128,2048]{1,0:T(8,128)(2,1)S(1)}, bf16[128,2048]{1,0:T(8,128)(2,1)S(1)}, u32[]{:S(2)}, u32[]{:S(2)}) collective-permute-start(bf16[128,2048]{1,0:T(8,128)(2,1)S(1)} %collective-permute-done.59.refs_4_), channel_id=1, source_target_pairs={{0,4},{8,0},{16,8},{24,16},{28,24},{20,28},{12,20},{4,12},{1,5},{9... | collective-permute-start | bytes 1572872 | tf_op jit(solution)/shard_map/ppermute | solution.py:461
  351.1 187.6 %reduce-scatter.6.cloned.1.call-start = ((), (), s32[]{:S(2)}) async-start(), calls=%async_computation.9 | async-start | bytes 6291456 | tf_op jit(solution)/shard_map/reduce_scatter | solution.py:1500
  351.2 40.6 %collective-permute-start.81 = (bf16[272,2048]{1,0:T(8,128)(2,1)}, bf16[272,2048]{1,0:T(8,128)(2,1)}, u32[]{:S(2)}, u32[]{:S(2)}) collective-permute-start(bf16[272,2048]{1,0:T(8,128)(2,1)} %get-tuple-element.757), channel_id=1, source_target_pairs={{0,2},{2,0},{1,3},{3,1},{4,6},{6,4},{5,7},{7,5},{8,10},{10,8},{9,1... | collective-permute-start | bytes 3342344 | tf_op jit(solution)/shard_map/ppermute | solution.py:456
  351.8 45.0 %collective-permute-start.84 = (bf16[136,2048]{1,0:T(8,128)(2,1)}, bf16[136,2048]{1,0:T(8,128)(2,1)}, u32[]{:S(2)}, u32[]{:S(2)}) collective-permute-start(bf16[136,2048]{1,0:T(8,128)(2,1)} %copy-done.51), channel_id=1, source_target_pairs={{0,2},{2,0},{1,3},{3,1},{4,6},{6,4},{5,7},{7,5},{8,10},{10,8},{9,1... | collective-permute-start | bytes 1671176 | tf_op jit(solution)/shard_map/ppermute | solution.py:456
  377.4 229.8 %reduce-scatter.8.cloned.1.call-start = ((), (), s32[]{:S(2)}) async-start(), calls=%async_computation.10 | async-start | bytes 6291456 | tf_op jit(solution)/shard_map/reduce_scatter | solution.py:1500
  432.5 23.1 %collective-permute-start.92 = (bf16[128,2048]{1,0:T(8,128)(2,1)}, bf16[128,2048]{1,0:T(8,128)(2,1)}, u32[]{:S(2)}, u32[]{:S(2)}) collective-permute-start(bf16[128,2048]{1,0:T(8,128)(2,1)} %get-tuple-element.788), channel_id=1, source_target_pairs={{0,8},{8,16},{16,24},{24,28},{28,20},{20,12},{12,4},{4,0},{1,9},{9... | collective-permute-start | bytes 1572872 | tf_op jit(solution)/shard_map/ppermute | solution.py:461
  449.4 35.4 %collective-permute-start.105 = (bf16[256,2048]{1,0:T(8,128)(2,1)S(1)}, bf16[256,2048]{1,0:T(8,128)(2,1)S(1)}, u32[]{:S(2)}, u32[]{:S(2)}) collective-permute-start(bf16[256,2048]{1,0:T(8,128)(2,1)S(1)} %copy-done.50), channel_id=1, source_target_pairs={{0,2},{2,0},{1,3},{3,1},{4,6},{6,4},{5,7},{7,5},{8,10},{10,8},{9,1... | collective-permute-start | bytes 3145736 | tf_op jit(solution)/shard_map/ppermute | solution.py:456
  531.6 28.8 %collective-permute-start.116 = (bf16[128,2048]{1,0:T(8,128)(2,1)}, bf16[128,2048]{1,0:T(8,128)(2,1)}, u32[]{:S(2)}, u32[]{:S(2)}) collective-permute-start(bf16[128,2048]{1,0:T(8,128)(2,1)} %get-tuple-element.890), channel_id=1, source_target_pairs={{0,8},{8,16},{16,24},{24,28},{28,20},{20,12},{12,4},{4,0},{1,9},{9... | collective-permute-start | bytes 1572872 | tf_op jit(solution)/shard_map/ppermute | solution.py:461
  532.8 27.6 %collective-permute-start.117 = (bf16[128,2048]{1,0:T(8,128)(2,1)}, bf16[128,2048]{1,0:T(8,128)(2,1)}, u32[]{:S(2)}, u32[]{:S(2)}) collective-permute-start(bf16[128,2048]{1,0:T(8,128)(2,1)} %get-tuple-element.891), channel_id=1, source_target_pairs={{0,4},{8,0},{16,8},{24,16},{28,24},{20,28},{12,20},{4,12},{1,5},{9... | collective-permute-start | bytes 1572872 | tf_op jit(solution)/shard_map/ppermute | solution.py:461
  567.1 23.8 %all-to-all-start = ((bf16[16,64,128]{2,1,0:T(8,128)(2,1)}), bf16[16,64,128]{2,1,0:T(8,128)(2,1)S(1)}, u32[]{:S(2)}, u32[]{:S(2)}) async-start(bf16[16,64,128]{2,1,0:T(8,128)(2,1)} %bitcast.38), calls=%async_computation.3 | async-start | bytes 524288 | tf_op jit(solution)/shard_map/all_to_all | solution.py:1642
  590.9 37.8 %all-to-all-start.1 = ((bf16[16,64,384]{2,1,0:T(8,128)(2,1)}), bf16[16,64,384]{2,1,0:T(8,128)(2,1)}, u32[]{:S(2)}, u32[]{:S(2)}) async-start(bf16[16,64,384]{2,1,0:T(8,128)(2,1)} %bitcast.153), calls=%async_computation.4 | async-start | bytes 1572864 | tf_op jit(solution)/shard_map/all_to_all | solution.py:1642
  (207 other events, 1902.2 us)
Sparse Core Ops, SparseCore 0:
  36.9 65.2 all-gather.3
  103.8 56.5 all-gather.5
  161.9 56.7 all-gather.7
  351.2 54.2 reduce-scatter.3
  408.4 54.2 reduce-scatter.5
  493.2 55.6 reduce-scatter.7
